TPU v7x, 32 devices: a whole 2x2x4 slice. The times are simulated.
32 devices in a mesh: wide: 8 (over z, x), narrow: 4 (over y, core).
Axes of the slice: x: 2, y: 2, z: 4, core: 2. Of those that a mesh axis runs over, the one named last changes fastest.
Arguments:
- tokens: bfloat16 [18432, 768], P(('wide', 'narrow')), may hold values from -6 to 6
- segment_ids: int32 [32, 576], P(('wide', 'narrow')), may hold values from 0 to 7, as said below
- patch_valid: int32 [32, 576], P(('wide', 'narrow')), may hold values from 0 to 1, as said below
- routes: int32 [18432, 2], P(('wide', 'narrow')), may hold values from 0 to 7, all different within a row
- priority: int32 [32, 576], P(('wide', 'narrow')), may hold values from 0 to 575, each once within a row
- gain_attn: bfloat16 [768], P(('wide', 'narrow')), may hold values from 0.099609375 to 1.8984375
- shift_attn: bfloat16 [768], P(('wide', 'narrow')), may hold values from -3 to 3
- w_qkv: bfloat16 [768, 2304], P(('wide', 'narrow')), may hold values from -0.3125 to 0.3125
- query_bias: bfloat16 [768], P(('wide', 'narrow')), may hold values from -3 to 3
- value_bias: bfloat16 [768], P(('wide', 'narrow')), may hold values from -3 to 3
- w_proj: bfloat16 [768, 768], P(('wide', 'narrow')), may hold values from -1.75 to 1.75
- proj_bias: bfloat16 [768], P(('wide', 'narrow')), may hold values from -3 to 3
- gain_moe: bfloat16 [768], P(('wide', 'narrow')), may hold values from 0.099609375 to 1.8984375
- shift_moe: bfloat16 [768], P(('wide', 'narrow')), may hold values from -1.5 to 1.5
- w_router: bfloat16 [768, 8], P(('wide', 'narrow')), may hold values from -0.5 to 0.5
- w_in: bfloat16 [8, 768, 3072], P('wide', None, 'narrow'), may hold values from -0.21875 to 0.21875
- in_bias: bfloat16 [8, 3072], P('wide', 'narrow'), may hold values from -3 to 3
- w_out: bfloat16 [8, 3072, 768], P('wide', 'narrow'), may hold values from -88 to 88
- out_bias: bfloat16 [8, 768], P('wide'), may hold values from -488 to 488
- cotangent: bfloat16 [18432, 768], P(('wide', 'narrow')), may hold values from -6 to 6
Outputs:
- block_out: bfloat16 [18432, 768], P(('wide', 'narrow'))
- grad_tokens: bfloat16 [18432, 768], P(('wide', 'narrow'))
- grad_gain_attn: float32 [768], P(('wide', 'narrow'))
- grad_shift_attn: float32 [768], P(('wide', 'narrow'))
- grad_w_qkv: float32 [768, 2304], P(('wide', 'narrow'))
- grad_query_bias: float32 [768], P(('wide', 'narrow'))
- grad_value_bias: float32 [768], P(('wide', 'narrow'))
- grad_w_proj: float32 [768, 768], P(('wide', 'narrow'))
- grad_proj_bias: float32 [768], P(('wide', 'narrow'))
- grad_gain_moe: float32 [768], P(('wide', 'narrow'))
- grad_shift_moe: float32 [768], P(('wide', 'narrow'))
- grad_w_router: float32 [768, 8], P(('wide', 'narrow'))
- grad_w_in: float32 [8, 768, 3072], P('wide', None, 'narrow')
- grad_in_bias: float32 [8, 3072], P('wide', 'narrow')
- grad_w_out: float32 [8, 3072, 768], P('wide', 'narrow')
- grad_out_bias: float32 [8, 768], P('wide')
Inputs may be any that keep to these rules, and one draw needn't show every extreme that they name: `segment_ids`: along each row of 576 patches the image numbers never fall; row 0 is one image. `patch_valid`: each row is 1 except for a tail of 0 to 71 padded patches. `routes`: the two experts of a patch differ. `priority`: each row holds every rank of 0 to 575 once.
All inputs are finite; a program needn't handle non-finite values.
Results may differ from a plain program's by a relative error of at most 0.02.
The roundings to bfloat16 on the way count: a program that leaves them out, or rounds other values in their place, can miss the bound.
Values may be sent and summed in bfloat16 or wider, within the bound.
A program may use at most 256 MiB of HBM per device.

v0:
```python
import jax
import jax.numpy as jnp
from jax import lax
from jax.sharding import PartitionSpec as P

HEAD = 64


EPSILON = 1e-06
MASKED = -1000000000.0
HIGHEST = lax.Precision.HIGHEST


def layer_norm(values, gain_vec, shift_vec):
    center = jnp.mean(values, axis=-1, keepdims=True)
    offset = values - center
    spread = jnp.mean(offset * offset, axis=-1, keepdims=True)
    return offset * lax.rsqrt(spread + EPSILON) * gain_vec + shift_vec


def gelu_tanh(values):
    return jax.nn.gelu(values, approximate=True)


def contract(first_op, second_op, first_dim, second_dim):
    return lax.dot_general(
        first_op,
        second_op,
        (((first_dim,), (second_dim,)), ((), ())),
        preferred_element_type=jnp.float32,
    )


def split_heads(row_data):
    return row_data.reshape(row_data.shape[0], -1, HEAD).transpose(1, 0, 2)


def merge_heads(stacked):
    return stacked.transpose(1, 0, 2).reshape(stacked.shape[1], -1)


def pair_tables(route_row, priority_row, valid_row, experts, capacity):
    row_count = route_row.shape[0]
    labels = jnp.arange(experts, dtype=jnp.int32)
    rank_ids = jnp.arange(row_count, dtype=jnp.int32)
    ranking = (priority_row[None, :] == rank_ids[:, None]).astype(jnp.float32)
    slot_ids = jnp.arange(experts * capacity, dtype=jnp.int32)
    slot_expert = slot_ids // capacity
    slot_place = (slot_ids % capacity).astype(jnp.float32)
    filled = jnp.zeros((experts,), jnp.float32)
    columns = []
    for pair_index in range(2):
        target = route_row[:, pair_index]
        onehot = ((target[:, None] == labels[None, :]) & (valid_row[:, None] == 1)).astype(
            jnp.float32
        )
        ranked = jnp.dot(ranking, onehot, precision=HIGHEST)
        earlier = jnp.cumsum(ranked, axis=0) - ranked
        queue_pos = jnp.dot(ranking.T, earlier, precision=HIGHEST) + filled[None, :]
        position = jnp.sum(queue_pos * onehot, axis=1)
        matches = (
            (target[None, :] == slot_expert[:, None])
            & (position[None, :] == slot_place[:, None])
            & (valid_row[None, :] == 1)
        )
        columns.append(matches.astype(jnp.float32))
        filled = filled + jnp.sum(onehot, axis=0)
    return jnp.concatenate(columns, axis=1)


def per_device(
    tokens,
    segment_ids,
    patch_valid,
    routes,
    priority,
    gain_attn,
    shift_attn,
    w_qkv,
    query_bias,
    value_bias,
    w_proj,
    proj_bias,
    gain_moe,
    shift_moe,
    w_router,
    w_in,
    in_bias,
    w_out,
    out_bias,
    cotangent,
):
    gathered = (
        lax.all_gather(gain_attn, ("wide", "narrow"), axis=0, tiled=True),
        lax.all_gather(shift_attn, ("wide", "narrow"), axis=0, tiled=True),
        lax.all_gather(w_qkv, ("wide", "narrow"), axis=0, tiled=True),
        lax.all_gather(query_bias, ("wide", "narrow"), axis=0, tiled=True),
        lax.all_gather(value_bias, ("wide", "narrow"), axis=0, tiled=True),
        lax.all_gather(w_proj, ("wide", "narrow"), axis=0, tiled=True),
        lax.all_gather(proj_bias, ("wide", "narrow"), axis=0, tiled=True),
        lax.all_gather(gain_moe, ("wide", "narrow"), axis=0, tiled=True),
        lax.all_gather(shift_moe, ("wide", "narrow"), axis=0, tiled=True),
        lax.all_gather(w_router, ("wide", "narrow"), axis=0, tiled=True),
    )
    (
        full_gain_attn,
        full_shift_attn,
        qkv_weight,
        full_query_bias,
        full_value_bias,
        proj_weight,
        full_proj_bias,
        full_gain_moe,
        full_shift_moe,
        router_weight,
    ) = gathered
    row_count, model_width = tokens.shape
    experts = router_weight.shape[1]
    capacity = (210 * row_count + 100 * experts - 1) // (100 * experts)
    score_scale = HEAD ** (-0.5)
    segments = segment_ids[0]
    is_valid = patch_valid[0]
    places = jnp.arange(row_count, dtype=jnp.int32)
    allowed = (segments[:, None] == segments[None, :]) & (
        (is_valid[None, :] == 1) | (places[:, None] == places[None, :])
    )
    inputs = tokens.astype(jnp.float32)
    normed_attn, attn_norm_back = jax.vjp(
        layer_norm, inputs, full_gain_attn.astype(jnp.float32), full_shift_attn.astype(jnp.float32)
    )
    attn_low = normed_attn.astype(jnp.bfloat16)
    qkv_rows = jnp.dot(attn_low, qkv_weight, preferred_element_type=jnp.float32)
    queries = (qkv_rows[:, :model_width] + full_query_bias.astype(jnp.float32)).astype(jnp.bfloat16)
    keys_low = qkv_rows[:, model_width : 2 * model_width].astype(jnp.bfloat16)
    values_low = (qkv_rows[:, 2 * model_width :] + full_value_bias.astype(jnp.float32)).astype(
        jnp.bfloat16
    )
    head_queries = split_heads(queries)
    head_keys = split_heads(keys_low)
    head_values = split_heads(values_low)

    def head_scores(query_head, key_head):
        scores = contract(query_head, key_head, 1, 1) * score_scale
        return jnp.where(allowed, scores, MASKED)

    def attend(pieces):
        query_head, key_head, value_head = pieces
        scores = head_scores(query_head, key_head)
        row_peak = jnp.max(scores, axis=1, keepdims=True)
        raised = jnp.exp(scores - row_peak)
        row_total = jnp.sum(raised, axis=1, keepdims=True)
        attn_probs = raised / row_total
        head_mix = jnp.dot(
            attn_probs.astype(jnp.bfloat16), value_head, preferred_element_type=jnp.float32
        )
        return (head_mix.astype(jnp.bfloat16), row_peak[:, 0] + jnp.log(row_total[:, 0]))

    head_mixed, log_total = lax.map(attend, (head_queries, head_keys, head_values))
    attended = merge_heads(head_mixed)
    branch = jnp.dot(
        attended, proj_weight, preferred_element_type=jnp.float32
    ) + full_proj_bias.astype(jnp.float32)
    middle = inputs + branch
    normed_moe, moe_norm_back = jax.vjp(
        layer_norm, middle, full_gain_moe.astype(jnp.float32), full_shift_moe.astype(jnp.float32)
    )
    moe_low = normed_moe.astype(jnp.bfloat16)
    logits = jnp.dot(moe_low, router_weight, preferred_element_type=jnp.float32)
    labels = jnp.arange(experts, dtype=jnp.int32)
    route_hot = (jnp.transpose(routes)[:, :, None] == labels[None, None, :]).astype(jnp.float32)

    def gate_of(logit_rows):
        router_probs = jax.nn.softmax(logit_rows, axis=-1)
        return jnp.sum(router_probs[None] * route_hot, axis=-1)

    gate_rows, gate_back = jax.vjp(gate_of, logits)
    pair_table = pair_tables(routes, priority[0], is_valid, experts, capacity)
    pairs_low = pair_table.astype(jnp.bfloat16)
    dispatch_low = (pair_table[:, :row_count] + pair_table[:, row_count:]).astype(jnp.bfloat16)
    expert_rows = (
        jnp.dot(dispatch_low, moe_low, preferred_element_type=jnp.float32)
        .astype(jnp.bfloat16)
        .reshape(experts, capacity, model_width)
    )
    received = lax.all_to_all(expert_rows, "wide", split_axis=0, concat_axis=0, tiled=True)
    rows_flat = lax.all_gather(received, "narrow", axis=0, tiled=True).reshape(-1, model_width)
    first_weight = w_in[0]
    first_bias = in_bias[0]
    second_weight = w_out[0]
    pre_act = jnp.dot(
        rows_flat, first_weight, preferred_element_type=jnp.float32
    ) + first_bias.astype(jnp.float32)
    hidden, gelu_back = jax.vjp(gelu_tanh, pre_act)
    hidden_low = hidden.astype(jnp.bfloat16)
    product = jnp.dot(hidden_low, second_weight, preferred_element_type=jnp.float32).reshape(
        -1, capacity, model_width
    )
    expert_sum = lax.psum_scatter(
        product.astype(jnp.bfloat16), "narrow", scatter_dimension=0, tiled=True
    ).astype(jnp.float32)
    expert_out = (expert_sum + out_bias[0].astype(jnp.float32)).astype(jnp.bfloat16)
    returned = lax.all_to_all(expert_out, "wide", split_axis=0, concat_axis=0, tiled=True).reshape(
        -1, model_width
    )
    picked = contract(pairs_low, returned, 0, 0).reshape(2, row_count, model_width)
    mixture = gate_rows[0][:, None] * picked[0] + gate_rows[1][:, None] * picked[1]
    block_out = (middle + mixture).astype(jnp.bfloat16)
    upstream = cotangent.astype(jnp.float32)
    gate_grads = jnp.sum(upstream[None] * picked, axis=2)
    weighted = (
        (gate_rows[:, :, None] * upstream[None])
        .astype(jnp.bfloat16)
        .reshape(2 * row_count, model_width)
    )
    out_grads = (
        jnp.dot(pairs_low, weighted, preferred_element_type=jnp.float32)
        .astype(jnp.bfloat16)
        .reshape(experts, capacity, model_width)
    )
    back_rows = lax.all_to_all(out_grads, "wide", split_axis=0, concat_axis=0, tiled=True)
    grads_flat = lax.all_gather(back_rows, "narrow", axis=0, tiled=True).reshape(-1, model_width)
    hidden_grad = contract(grads_flat, second_weight, 1, 1)
    pre_grad = gelu_back(hidden_grad)[0].astype(jnp.bfloat16)
    grad_first = contract(rows_flat, pre_grad, 0, 0)
    grad_first_bias = jnp.sum(pre_grad, axis=0, dtype=jnp.float32)
    grad_second = contract(hidden_low, grads_flat, 0, 0)
    grad_second_bias = jnp.sum(grads_flat, axis=0, dtype=jnp.float32)
    rows_grad = contract(pre_grad, first_weight, 1, 1).reshape(-1, capacity, model_width)
    input_rows = lax.psum_scatter(
        rows_grad.astype(jnp.bfloat16), "narrow", scatter_dimension=0, tiled=True
    )
    grad_w_in = grad_first[None]
    grad_in_bias = grad_first_bias[None]
    grad_w_out = grad_second[None]
    grad_out_bias = grad_second_bias[None]
    token_rows = lax.all_to_all(
        input_rows, "wide", split_axis=0, concat_axis=0, tiled=True
    ).reshape(-1, model_width)
    moe_grad = contract(dispatch_low, token_rows, 0, 0)
    logit_grad = gate_back(gate_grads)[0].astype(jnp.bfloat16)
    moe_grad = moe_grad + contract(logit_grad, router_weight, 1, 1)
    grad_router = contract(moe_low, logit_grad, 0, 0)
    middle_part, grad_gain_moe, grad_shift_moe = moe_norm_back(moe_grad)
    middle_grad = upstream + middle_part
    branch_grad = middle_grad.astype(jnp.bfloat16)
    grad_proj_bias = jnp.sum(branch_grad, axis=0, dtype=jnp.float32)
    grad_proj = contract(attended, branch_grad, 0, 0)
    attended_grad = contract(branch_grad, proj_weight, 1, 1).astype(jnp.bfloat16)

    def attend_back(pieces):
        query_head, key_head, value_head, grad_head, log_head = pieces
        scores = head_scores(query_head, key_head)
        attn_probs = jnp.exp(scores - log_head[:, None])
        value_grad = contract(attn_probs.astype(jnp.bfloat16), grad_head, 0, 0).astype(jnp.bfloat16)
        prob_grad = contract(grad_head, value_head, 1, 1)
        score_grad = (
            attn_probs * (prob_grad - jnp.sum(prob_grad * attn_probs, axis=1, keepdims=True))
        ).astype(jnp.bfloat16)
        query_grad = (
            jnp.dot(score_grad, key_head, preferred_element_type=jnp.float32) * score_scale
        ).astype(jnp.bfloat16)
        key_grad = (contract(score_grad, query_head, 0, 0) * score_scale).astype(jnp.bfloat16)
        return (query_grad, key_grad, value_grad)

    head_q_grad, head_k_grad, head_v_grad = lax.map(
        attend_back, (head_queries, head_keys, head_values, split_heads(attended_grad), log_total)
    )
    qkv_grad = jnp.concatenate(
        [merge_heads(head_q_grad), merge_heads(head_k_grad), merge_heads(head_v_grad)], axis=1
    )
    grad_query_bias = jnp.sum(qkv_grad[:, :model_width], axis=0, dtype=jnp.float32)
    grad_value_bias = jnp.sum(qkv_grad[:, 2 * model_width :], axis=0, dtype=jnp.float32)
    grad_qkv = contract(attn_low, qkv_grad, 0, 0)
    attn_grad = contract(qkv_grad, qkv_weight, 1, 1)
    input_part, grad_gain_attn, grad_shift_attn = attn_norm_back(attn_grad)
    tokens_grad = (middle_grad + input_part).astype(jnp.bfloat16)
    shares = (
        lax.psum_scatter(grad_gain_attn, ("wide", "narrow"), scatter_dimension=0, tiled=True),
        lax.psum_scatter(grad_shift_attn, ("wide", "narrow"), scatter_dimension=0, tiled=True),
        lax.psum_scatter(grad_qkv, ("wide", "narrow"), scatter_dimension=0, tiled=True),
        lax.psum_scatter(grad_query_bias, ("wide", "narrow"), scatter_dimension=0, tiled=True),
        lax.psum_scatter(grad_value_bias, ("wide", "narrow"), scatter_dimension=0, tiled=True),
        lax.psum_scatter(grad_proj, ("wide", "narrow"), scatter_dimension=0, tiled=True),
        lax.psum_scatter(grad_proj_bias, ("wide", "narrow"), scatter_dimension=0, tiled=True),
        lax.psum_scatter(grad_gain_moe, ("wide", "narrow"), scatter_dimension=0, tiled=True),
        lax.psum_scatter(grad_shift_moe, ("wide", "narrow"), scatter_dimension=0, tiled=True),
        lax.psum_scatter(grad_router, ("wide", "narrow"), scatter_dimension=0, tiled=True),
    )
    return (
        block_out,
        tokens_grad,
        shares[0],
        shares[1],
        shares[2],
        shares[3],
        shares[4],
        shares[5],
        shares[6],
        shares[7],
        shares[8],
        shares[9],
        grad_w_in,
        grad_in_bias,
        grad_w_out,
        grad_out_bias,
    )


def solution(mesh):
    placed = (
        P(("wide", "narrow"), None),
        P(("wide", "narrow"), None),
        P(("wide", "narrow"), None),
        P(("wide", "narrow"), None),
        P(("wide", "narrow"), None),
        P(("wide", "narrow")),
        P(("wide", "narrow")),
        P(("wide", "narrow"), None),
        P(("wide", "narrow")),
        P(("wide", "narrow")),
        P(("wide", "narrow"), None),
        P(("wide", "narrow")),
        P(("wide", "narrow")),
        P(("wide", "narrow")),
        P(("wide", "narrow"), None),
        P("wide", None, "narrow"),
        P("wide", "narrow"),
        P("wide", "narrow", None),
        P("wide", None),
        P(("wide", "narrow"), None),
    )
    return jax.shard_map(
        per_device,
        mesh=mesh,
        in_specs=placed,
        out_specs=(
            P(("wide", "narrow"), None),
            P(("wide", "narrow"), None),
            P(("wide", "narrow")),
            P(("wide", "narrow")),
            P(("wide", "narrow"), None),
            P(("wide", "narrow")),
            P(("wide", "narrow")),
            P(("wide", "narrow"), None),
            P(("wide", "narrow")),
            P(("wide", "narrow")),
            P(("wide", "narrow")),
            P(("wide", "narrow"), None),
            P("wide", None, "narrow"),
            P("wide", "narrow"),
            P("wide", "narrow", None),
            P("wide", None),
        ),
        check_vma=False,
    )
```

profile of v0, /device:TPU:0, one launch (start us, length us, event | category | flops | bytes accessed | tf_op | source)
XLA Modules:
  0.0 923.8 jit_solution(12786552535657912784)
XLA Ops:
  14.7 42.4 %all-reduce.18 = (bf16[768]{0:T(1024)(128)(2,1)S(1)}, bf16[768]{0:T(1024)(128)(2,1)S(1)}, bf16[768]{0:T(1024)(128)(2,1)S(1)}, bf16[768]{0:T(1024)(128)(2,1)S(1)}...) all-reduce(bf16[768]{0:T(1024)(128)(2,1)S(1)} %dynamic-update-slice, ...), channel_id=1, replica_groups=mesh['wide'=8,'narrow'=4] {'wide','narrow'}, use_global_device_ids=true, to_apply=%add.3 | all-reduce | flops 5376 | bytes 21504
  66.4 7.6 all-gather.6.cloned.1.call-done
  89.8 45.9 %while.28 = (s32[]{:T(128)}, bf16[12,576,64]{1,2,0:T(8,128)(2,1)}, f32[12,576]{1,0:T(8,128)S(1)}, bf16[12,576,64]{2,1,0:T(8,128)(2,1)}, bf16[12,576,64]{2,1,0:T(...) while((s32[]{:T(128)}, bf16[12,576,64]{1,2,0:T(8,128)(2,1)}, ...), condition=%wide.region_5.6_spmd.clone, body=%wide.region_2.5_spmd.clone.sunk | while | flops 88952256 | bytes 4544617 | solution.py:158
  142.2 48.6 %all_to_all.20 = bf16[8,152,768]{2,1,0:T(8,128)(2,1)} all-to-all(bf16[8,152,768]{2,1,0:T(8,128)(2,1)S(1)} %bitcast.209), channel_id=1, replica_groups=mesh['wide'=8,'narrow'=4] {'wide'}, dimensions={0} | all-to-all | bytes 3735552 | tf_op jit(solution)/shard_map/all_to_all | solution.py:185
  191.5 50.0 %all-gather.10.cloned.1.call-done = bf16[32,152,768]{2,1,0:T(8,128)(2,1)} async-done(((bf16[8,152,768]{2,1,0:T(8,128)(2,1)}), bf16[32,152,768]{2,1,0:T(8,128)(2,1)}) %all-gather.10.cloned.1.call-update) | async-done | bytes 7471120 | tf_op jit(solution)/shard_map/all_gather | solution.py:186
  241.6 13.9 %multiply_convert_fusion.1 = (bf16[4864,768]{1,0:T(8,128)(2,1)S(1)}, f32[4864,768]{1,0:T(8,128)}) fusion(f32[768]{0:T(1024)S(1)} %convert_reduce_fusion.8, bf16[4864,768]{1,0:T(8,128)(2,1)} %bitcast.222, bf16[1,768,768]{2,1,0:T(8,128)(2,1)S(1)} %copy-done), kind=kOutput, calls=%fused_computation.71 | convolution fusion | flops 5775163392 | bytes 31067136 | tf_op jit(solution)/shard_map/dot_general | solution.py:190
  258.4 8.2 convolution_convert_fusion.3
  267.3 65.8 %reduce-scatter.6.cloned.1.call-done = bf16[8,152,768]{2,1,0:T(8,128)(2,1)} async-done(((bf16[32,152,768]{2,1,0:T(8,128)(2,1)}), bf16[8,152,768]{2,1,0:T(8,128)(2,1)}) %reduce-scatter.6.cloned.1.call-update) | async-done | bytes 1867792 | tf_op jit(solution)/shard_map/reduce_scatter | solution.py:198
  336.2 5.6 all-to-all-start.1
  341.9 66.2 %all-gather = bf16[32,24,8]{1,2,0:T(8,128)(2,1)S(1)} all-gather(bf16[1,24,8]{1,2,0:T(8,128)(2,1)S(1)} %bitcast.221), channel_id=1, replica_groups=mesh['wide'=8,'narrow'=4] {'wide','narrow'}, dimensions={0}, use_global_device_ids=true | all-gather | bytes 12672 | tf_op jit(solution)/shard_map/all_gather | solution.py:103
  415.9 7.6 fusion.56
  428.7 49.9 %all_to_all.21 = bf16[8,152,768]{2,1,0:T(8,128)(2,1)} all-to-all(bf16[8,152,768]{2,1,0:T(8,128)(2,1)S(1)} %bitcast.208), channel_id=1, replica_groups=mesh['wide'=8,'narrow'=4] {'wide'}, dimensions={0} | all-to-all | bytes 3735552 | tf_op jit(solution)/shard_map/all_to_all | solution.py:220
  479.0 50.3 %all-gather.12.cloned.1.call-done = bf16[32,152,768]{2,1,0:T(8,128)(2,1)} async-done(((bf16[8,152,768]{2,1,0:T(8,128)(2,1)}), bf16[32,152,768]{2,1,0:T(8,128)(2,1)}) %all-gather.12.cloned.1.call-update) | async-done | bytes 7471120 | tf_op jit(solution)/shard_map/all_gather | solution.py:221
  529.3 19.5 %convert_reduce_fusion.1 = (f32[768]{0:T(1024)S(1)}, bf16[4864,768]{1,0:T(8,128)(2,1)S(1)}) fusion(f32[4864,768]{1,0:T(8,128)} %get-tuple-element.298, f32[768]{0:T(1024)S(1)} %convert_reduce_fusion.8, bf16[4864,768]{1,0:T(8,128)(2,1)} %bitcast.200, bf16[1,768,768]{2,1,0:T(8,128)(2,1)} %param.41), kind=kOutput, calls=%fused_computation.70 | convolution fusion | flops 5823724544 | bytes 31070208 | tf_op jit(solution)/shard_map/dot_general | solution.py:26
  551.8 8.2 convolution_convert_fusion.2
  560.0 66.5 %reduce-scatter.8.cloned.1.call-done = bf16[8,152,768]{2,1,0:T(8,128)(2,1)} async-done(((bf16[32,152,768]{2,1,0:T(8,128)(2,1)}), bf16[8,152,768]{2,1,0:T(8,128)(2,1)}) %reduce-scatter.8.cloned.1.call-update) | async-done | bytes 1867792 | tf_op jit(solution)/shard_map/reduce_scatter | solution.py:229
  632.7 42.8 %all-to-all-done.3 = bf16[8,152,768]{2,1,0:T(8,128)(2,1)} async-done(((bf16[8,152,768]{2,1,0:T(8,128)(2,1)}), bf16[8,152,768]{2,1,0:T(8,128)(2,1)}, u32[]{:S(2)}, u32[]{:S(2)}) %all-to-all-start.3) | async-done | bytes 1867808 | tf_op jit(solution)/shard_map/all_to_all | solution.py:236
  693.2 97.9 %while.29 = (s32[]{:T(128)}, bf16[12,576,64]{1,2,0:T(8,128)(2,1)S(1)}, bf16[12,576,64]{1,2,0:T(8,128)(2,1)}, bf16[12,576,64]{1,2,0:T(8,128)(2,1)}, bf16[12,576,6...) while((s32[]{:T(128)}, ...), condition=%wide.region_27.28_spmd.clone, body=%wide.region_25.27_spmd.clone.sunk | while | flops 216833472 | bytes 11201657 | solution.py:265
  791.2 8.1 fusion.79
  806.3 12.2 %convolution_bitcast_fusion = f32[1,768,768]{2,1,0:T(8,128)} fusion(bf16[4864,768]{1,0:T(8,128)(2,1)} %copy-done.35, bf16[4864,768]{1,0:T(8,128)(2,1)} %bitcast.201), kind=kOutput, calls=%fused_computation.124 | convolution fusion | flops 5737807872 | bytes 17301504 | tf_op jit(solution)/shard_map/dot_general | solution.py:26
  818.6 7.5 convolution_bitcast_fusion.1
  827.8 5.6 fusion.130
  834.6 39.5 %all-reduce.17 = (f32[768]{0:T(1024)S(1)}, f32[768]{0:T(1024)S(1)}, f32[768]{0:T(1024)S(1)}, f32[768]{0:T(1024)S(1)}, f32[768]{0:T(1024)S(1)}, /*index=5*/f32[76...) all-reduce(f32[768]{0:T(1024)S(1)} %get-tuple-element.218, ...), channel_id=4, replica_groups=mesh['wide'=8,'narrow'=4] {'wide','narrow'}, use_global_device_ids=true, to_apply=%region_31.32.clone | all-reduce | flops 11520 | bytes 92160
  882.2 34.5 %reduce-scatter.10.cloned.1.call-done = f32[24,2304]{1,0:T(8,128)} async-done(((f32[768,2304]{1,0:T(8,128)}), f32[24,2304]{1,0:T(8,128)}) %reduce-scatter.10.cloned.1.call-update) | async-done | bytes 221200 | tf_op jit(solution)/shard_map/reduce_scatter | solution.py:280
  (378 shorter events, 247.6 us)
Async XLA Ops:
  7.2 234.4 %copy-start = (bf16[1,768,768]{2,1,0:T(8,128)(2,1)S(1)}, bf16[1,768,768]{2,1,0:T(8,128)(2,1)}, u32[]{:S(2)}) copy-start(bf16[1,768,768]{2,1,0:T(8,128)(2,1)} %param.39) | copy-start | bytes 3538948
  7.2 53.0 %copy-start.32 = (s32[1,576]{1,0:T(1,128)S(1)}, s32[1,576]{1,0:T(1,128)}, u32[]{:S(2)}) copy-start(s32[1,576]{1,0:T(1,128)} %param.26) | copy-start | bytes 6916
  7.2 53.1 %copy-start.30 = (s32[1,576]{1,0:T(1,128)S(1)}, s32[1,576]{1,0:T(1,128)}, u32[]{:S(2)}) copy-start(s32[1,576]{1,0:T(1,128)} %param.25) | copy-start | bytes 6916
  7.2 53.1 %copy-start.31 = (s32[1,576]{1,0:T(1,128)S(1)}, s32[1,576]{1,0:T(1,128)}, u32[]{:S(2)}) copy-start(s32[1,576]{1,0:T(1,128)} %param.28) | copy-start | bytes 6916
  7.2 53.1 %copy-start.25 = (s32[576,2]{0,1:T(2,128)S(1)}, s32[576,2]{0,1:T(2,128)}, u32[]{:S(2)}) copy-start(s32[576,2]{0,1:T(2,128)} %param.27) | copy-start | bytes 13828
  7.2 66.7 %all-gather.6.cloned.1.call-start = ((), (), s32[]{:S(2)}) async-start(), calls=%async_computation.8 | async-start | bytes 3649536 | tf_op jit(solution)/shard_map/all_gather | solution.py:96
  8.0 127.8 %all-gather.8.cloned.1.call-start = ((), (), s32[]{:S(2)}) async-start(), calls=%async_computation.9 | async-start | bytes 1216512 | tf_op jit(solution)/shard_map/all_gather | solution.py:99
  8.7 232.8 %all-gather.10.cloned.1.call-start = ((), (), s32[]{:S(2)}) async-start(), calls=%async_computation.10 | async-start | bytes 9338880 | tf_op jit(solution)/shard_map/all_gather | solution.py:186
  58.6 19.8 %copy-start.17 = (f32[576]{0:T(1024)}, f32[576]{0:T(1024)S(1)}, u32[]{:S(2)}) copy-start(f32[576]{0:T(1024)S(1)} %broadcast_multiply_fusion.1) | copy-start | bytes 6916
  60.2 18.2 %copy-start.21 = (f32[576]{0:T(1024)}, f32[576]{0:T(1024)S(1)}, u32[]{:S(2)}) copy-start(f32[576]{0:T(1024)S(1)} %fusion.120) | copy-start | bytes 6916
  190.8 142.3 %reduce-scatter.6.cloned.1.call-start = ((), (), s32[]{:S(2)}) async-start(), calls=%async_computation.11 | async-start | bytes 9338880 | tf_op jit(solution)/shard_map/reduce_scatter | solution.py:198
  336.2 79.7 %all-to-all-start.1 = ((bf16[8,152,768]{2,1,0:T(8,128)(2,1)}), bf16[8,152,768]{2,1,0:T(8,128)(2,1)}, u32[]{:S(2)}, u32[]{:S(2)}) async-start(bf16[8,152,768]{2,1,0:T(8,128)(2,1)} %add_convert_fusion), calls=%async_computation.2 | async-start | bytes 3735552 | tf_op jit(solution)/shard_map/all_to_all | solution.py:202
  341.9 187.5 %all-gather.12.cloned.1.call-start = ((), (), s32[]{:S(2)}) async-start(), calls=%async_computation.12 | async-start | bytes 9338880 | tf_op jit(solution)/shard_map/all_gather | solution.py:221
  478.7 147.9 %reduce-scatter.8.cloned.1.call-start = ((), (), s32[]{:S(2)}) async-start(), calls=%async_computation.13 | async-start | bytes 9338880 | tf_op jit(solution)/shard_map/reduce_scatter | solution.py:229
  626.6 48.9 %all-to-all-start.3 = ((bf16[8,152,768]{2,1,0:T(8,128)(2,1)}), bf16[8,152,768]{2,1,0:T(8,128)(2,1)}, u32[]{:S(2)}, u32[]{:S(2)}) async-start(bf16[8,152,768]{2,1,0:T(8,128)(2,1)} %reduce-scatter.8.cloned.1.call-done), calls=%async_computation.5 | async-start | bytes 3735552 | tf_op jit(solution)/shard_map/all_to_all | solution.py:236
  632.1 250.1 %reduce-scatter.12.cloned.1.call-start = ((), (), s32[]{:S(2)}) async-start(), calls=%async_computation.15 | async-start | bytes 2433024 | tf_op jit(solution)/shard_map/reduce_scatter | solution.py:283
  687.4 229.4 %reduce-scatter.10.cloned.1.call-start = ((), (), s32[]{:S(2)}) async-start(), calls=%async_computation.14 | async-start | bytes 7299072 | tf_op jit(solution)/shard_map/reduce_scatter | solution.py:280
  693.2 98.0 %copy-start.4 = (bf16[576,768]{1,0:T(8,128)(2,1)S(1)}, bf16[576,768]{1,0:T(8,128)(2,1)}, u32[]{:S(2)}) copy-start(bf16[576,768]{1,0:T(8,128)(2,1)} %param.24) | copy-start | bytes 2654212
  693.2 98.0 %copy-start.18 = (f32[576]{0:T(1024)S(1)}, f32[576]{0:T(1024)}, u32[]{:S(2)}) copy-start(f32[576]{0:T(1024)} %copy-done.17) | copy-start | bytes 6916
  693.2 98.0 %copy-start.20 = (f32[768]{0:T(1024)S(1)}, f32[768]{0:T(1024)}, u32[]{:S(2)}) copy-start(f32[768]{0:T(1024)} %copy-done.19) | copy-start | bytes 9220
  693.2 98.0 %copy-start.22 = (f32[576]{0:T(1024)S(1)}, f32[576]{0:T(1024)}, u32[]{:S(2)}) copy-start(f32[576]{0:T(1024)} %copy-done.21) | copy-start | bytes 6916
  693.2 98.0 %copy-start.27 = (f32[768]{0:T(1024)S(1)}, f32[768]{0:T(1024)}, u32[]{:S(2)}) copy-start(f32[768]{0:T(1024)} %copy-done.26) | copy-start | bytes 9220
  801.2 17.3 %slice-start.2 = ((s8[7471104]{0:T(1024)(128)(4,1)}), s8[4194304]{0:T(1024)(128)(4,1)S(1)}, s32[]{:S(2)}) async-start(s8[7471104]{0:T(1024)(128)(4,1)} %bitcast.228), calls=%async_computation.18 | async-start | bytes 8388608
  833.4 45.5 %copy-start.2 = (f32[576,768]{1,0:T(8,128)S(1)}, f32[576,768]{1,0:T(8,128)}, u32[]{:S(2)}) copy-start(f32[576,768]{1,0:T(8,128)} %copy-done.1) | copy-start | bytes 5308420
  (27 other events, 171.4 us)
Sparse Core Ops, SparseCore 0:
  11.0 62.9 all-gather.5
  76.9 52.8 all-gather.7
  191.0 50.5 all-gather.9
  266.8 66.3 reduce-scatter.5
  478.8 50.4 all-gather.11
  560.2 66.3 reduce-scatter.7
  687.5 97.1 reduce-scatter.11
  799.4 117.3 reduce-scatter.9
where the time goes:
time: 936 us; the launch traced here: 924 us
  waiting for transfers between devices  319 us (34%)
  matrix products  252 us (27%)
  blocking collectives  247 us (26%)
  other arithmetic  38.9 us (4%)
  local copies, waits for them, and re-layouts  38.8 us (4%)
  between operations  15 us (2%)
  starting transfers between devices  12.6 us (1%)
    dot_general x72, matrix products, contract(): lax.dot_general(first_op, second_op, (((first_dim,), (second_dim,)), ((),...  177 us
    unnamed x2, blocking collectives  82 us
    reduce_scatter x1, waiting for transfers between devices, per_device(): lax.psum_scatter(rows_grad.astype(jnp.bfloat16), 'narrow', scatter_dimens...  66.5 us
    all_gather x1, blocking collectives, per_device(): lax.all_gather(w_router, ('wide', 'narrow'), axis=0, tiled=True)  66.2 us
    reduce_scatter x1, waiting for transfers between devices, per_device(): lax.psum_scatter(product.astype(jnp.bfloat16), 'narrow', scatter_dimensio...  65.8 us
    all_gather x1, waiting for transfers between devices, per_device(): lax.all_gather(back_rows, 'narrow', axis=0, tiled=True)  50.3 us
    all_gather x1, waiting for transfers between devices, per_device(): lax.all_gather(received, 'narrow', axis=0, tiled=True)  50 us
    all_to_all x1, blocking collectives, per_device(): lax.all_to_all(out_grads, 'wide', split_axis=0, concat_axis=0, tiled=True)  49.9 us
  transfers between devices with their start and end apart: 10, of which 7 were waited for; matrix products, arithmetic and copies ran while one was open for 26% of the time, Pallas kernels for 0%

commit v1 on v0

v1 whole, which is shorter than its diff:
```python
import functools

import jax
import jax.numpy as jnp
from jax import lax
from jax.experimental import pallas as pl
from jax.experimental.pallas import tpu as pltpu
from jax.sharding import PartitionSpec as P

HEAD = 64
PAIR = 2 * HEAD
EPSILON = 1e-06
MASKED = -1000000000.0
MESH = pl.DeviceIdType.MESH
LOW = jnp.bfloat16
F32 = jnp.float32
VMEM_LIMIT = 58 * 1024 * 1024


def dot(a, b):
    return jnp.dot(a, b, preferred_element_type=F32)


def dot_nt(a, b):
    return lax.dot_general(a, b, (((1,), (1,)), ((), ())), preferred_element_type=F32)


def dot_tn(a, b):
    return lax.dot_general(a, b, (((0,), (0,)), ((), ())), preferred_element_type=F32)


def grid_of(wide, narrow):
    along_x = 1 << ((wide.bit_length() - 1) // 2)
    return wide // along_x, along_x, narrow // 2, 2


def place_of(dims):
    depth, across, rows, cores = dims
    wide, narrow = lax.axis_index("wide"), lax.axis_index("narrow")
    return wide // across, wide % across, narrow // cores, narrow % cores


def device_at(dims, z, x, y, c):
    depth, across, rows, cores = dims
    return (z * across + x, y * cores + c)


def greet(peers):
    barrier = pltpu.get_barrier_semaphore()
    for peer in peers:
        pl.semaphore_signal(barrier, inc=1, device_id=peer, device_id_type=MESH)
    pl.semaphore_wait(barrier, len(peers))


def neighbours(dims):
    depth, across, rows, cores = dims
    z, x, y, c = place_of(dims)
    peers = [device_at(dims, (z + d) % depth, x, y, c) for d in range(1, depth)]
    peers += [device_at(dims, z, (x + d) % across, y, c) for d in range(1, across)]
    peers += [device_at(dims, z, x, (y + d) % rows, c) for d in range(1, rows)]
    peers += [device_at(dims, z, x, y, 1 - c)]
    return peers


def gather_kernel(dims, cut, shard, out, s1, r1, sx, rx, sy, ry, sa, ra, sb, rb, sc, rc, local):
    depth, across, rows, cores = dims
    z, x, y, c = place_of(dims)
    width = shard.shape[1]

    def block(dz, dx, dy, core):
        wide = ((z - dz) % depth) * across + (x - dx) % across
        return out.at[(wide * rows + (y - dy) % rows) * cores + core]

    def send(src, dst, ssem, rsem, to):
        copy = pltpu.make_async_remote_copy(
            src_ref=src, dst_ref=dst, send_sem=ssem, recv_sem=rsem, device_id=to, device_id_type=MESH
        )
        copy.start()
        return copy

    greet(neighbours(dims))
    own = block(0, 0, 0, c)
    keep = pltpu.make_async_copy(shard, own, local)
    keep.start()
    first, by_x, by_y, half_a, half_b, by_core = {}, {}, {}, {}, {}, {}
    for dz in range(1, depth):
        first[dz] = send(
            shard, own, s1.at[dz - 1], r1.at[dz - 1], device_at(dims, (z + dz) % depth, x, y, c)
        )

    def to_core(dz, dx, dy):
        at = (dz * across + dx) * rows + dy
        src = shard if (dz, dx, dy) == (0, 0, 0) else block(dz, dx, dy, c)
        by_core[at] = send(
            src, block(dz, dx, dy, c), sc.at[at], rc.at[at], device_at(dims, z, x, y, 1 - c)
        )

    def spread(dz):
        if dz:
            first[dz].wait_recv()
        src = block(dz, 0, 0, c) if dz else shard
        for dx in range(1, across):
            at = dz * (across - 1) + dx - 1
            by_x[dz, dx] = send(
                src, block(dz, 0, 0, c), sx.at[at], rx.at[at],
                device_at(dims, z, (x + dx) % across, y, c),
            )
        for dy in range(1, rows):
            at = dz * (rows - 1) + dy - 1
            by_y[dz, dy] = send(
                src, block(dz, 0, 0, c), sy.at[at], ry.at[at],
                device_at(dims, z, x, (y + dy) % rows, c),
            )
        to_core(dz, 0, 0)

    def corner(dz):
        for dx in range(1, across):
            by_x[dz, dx].wait_recv()
            part = block(dz, dx, 0, c).at[:, pl.ds(0, cut)]
            for dy in range(1, rows):
                at = (dz * (across - 1) + dx - 1) * (rows - 1) + dy - 1
                half_a[dz, dx, dy] = send(
                    part, part, sa.at[at], ra.at[at], device_at(dims, z, x, (y + dy) % rows, c)
                )
            to_core(dz, dx, 0)
        for dy in range(1, rows):
            by_y[dz, dy].wait_recv()
            part = block(dz, 0, dy, c).at[:, pl.ds(cut, width - cut)]
            for dx in range(1, across):
                at = (dz * (across - 1) + dx - 1) * (rows - 1) + dy - 1
                half_b[dz, dx, dy] = send(
                    part, part, sb.at[at], rb.at[at], device_at(dims, z, (x + dx) % across, y, c)
                )
            to_core(dz, 0, dy)

    def finish(dz):
        for dx in range(1, across):
            for dy in range(1, rows):
                half_a[dz, dx, dy].wait_recv()
                half_b[dz, dx, dy].wait_recv()
                to_core(dz, dx, dy)

    for step in range(depth + 2):
        if step < depth:
            spread(step)
        if 0 <= step - 1 < depth:
            corner(step - 1)
        if 0 <= step - 2 < depth:
            finish(step - 2)
    for copy in by_core.values():
        copy.wait_recv()
    for group in (first, by_x, by_y, half_a, half_b, by_core):
        for copy in group.values():
            copy.wait_send()
    keep.wait()


def gather_params(dims, shard):
    depth, across, rows, cores = dims
    count = depth * across * rows * cores
    height, width = shard.shape
    cut = (width // 256) * 128
    sizes = (
        depth - 1,
        depth * (across - 1),
        depth * (rows - 1),
        depth * (across - 1) * (rows - 1),
        depth * (across - 1) * (rows - 1),
        depth * across * rows,
    )
    sems = []
    for size in sizes:
        sems += [pltpu.SemaphoreType.DMA((size,))] * 2
    out = pl.pallas_call(
        functools.partial(gather_kernel, dims, cut),
        out_shape=jax.ShapeDtypeStruct((count, height, width), shard.dtype),
        in_specs=[pl.BlockSpec(memory_space=pl.ANY)],
        out_specs=pl.BlockSpec(memory_space=pl.ANY),
        scratch_shapes=sems + [pltpu.SemaphoreType.DMA],
        compiler_params=pltpu.CompilerParams(collective_id=0, has_side_effects=True),
        name="gather_params",
    )(shard)
    return out.reshape(count * height, width)


def scatter_kernel(
    dims, cut, grads, out, mine, r1, r2a, r2b, r3x, r3y, r4, out_a, out_b, out_z,
    s1, q1, s2a, q2a, s2b, q2b, s3x, q3x, s3y, q3y, s4, q4, local,
):
    depth, across, rows, cores = dims
    z, x, y, c = place_of(dims)
    width = grads.shape[-1]
    rest = width - cut

    def send(src, dst, ssem, rsem, to):
        copy = pltpu.make_async_remote_copy(
            src_ref=src, dst_ref=dst, send_sem=ssem, recv_sem=rsem, device_id=to, device_id_type=MESH
        )
        copy.start()
        return copy

    greet(neighbours(dims))
    order = [*range(1, depth), 0]
    first, keeps = {}, {}
    for dz in order:
        planes = pl.ds(((z + dz) % depth) * across, across)
        first[dz] = send(
            grads.at[planes, :, 1 - c], r1.at[dz], s1.at[dz], q1.at[dz],
            device_at(dims, z, x, y, 1 - c),
        )
        keeps[dz] = pltpu.make_async_copy(grads.at[planes, :, c], mine.at[dz], local.at[dz])
        keeps[dz].start()
    corner_a, corner_b, side_x, side_y, last = {}, {}, {}, {}, {}

    def total(*terms):
        acc = terms[0].astype(F32)
        for term in terms[1:]:
            acc = acc + term.astype(F32)
        return acc

    def begin(dz):
        keeps[dz].wait()
        first[dz].wait_recv()
        for a in range(across):
            for b in range(rows):
                mine[dz, a, b] = total(mine[dz, a, b], r1[dz, a, b]).astype(LOW)
        for dx in range(1, across):
            for dy in range(1, rows):
                at = (dz * (across - 1) + dx - 1) * (rows - 1) + dy - 1
                block = mine.at[dz, (x + dx) % across, (y + dy) % rows]
                corner_a[dz, dx, dy] = send(
                    block.at[:, pl.ds(0, cut)], r2a.at[at], s2a.at[at], q2a.at[at],
                    device_at(dims, z, x, (y + dy) % rows, c),
                )
                corner_b[dz, dx, dy] = send(
                    block.at[:, pl.ds(cut, rest)], r2b.at[at], s2b.at[at], q2b.at[at],
                    device_at(dims, z, (x + dx) % across, y, c),
                )

    def middle(dz):
        for dx in range(1, across):
            at = dz * (across - 1) + dx - 1
            block = mine.at[dz, (x + dx) % across, y]
            arrived = []
            for dy in range(1, rows):
                corner_a[dz, dx, dy].wait_recv()
                arrived.append(r2a[at * (rows - 1) + dy - 1])
            out_a[at, :, pl.ds(0, cut)] = total(block[:, pl.ds(0, cut)], *arrived).astype(LOW)
            out_a[at, :, pl.ds(cut, rest)] = block[:, pl.ds(cut, rest)]
            side_x[dz, dx] = send(
                out_a.at[at], r3x.at[at], s3x.at[at], q3x.at[at],
                device_at(dims, z, (x + dx) % across, y, c),
            )
        for dy in range(1, rows):
            at = dz * (rows - 1) + dy - 1
            block = mine.at[dz, x, (y + dy) % rows]
            arrived = []
            for dx in range(1, across):
                corner_b[dz, dx, dy].wait_recv()
                arrived.append(r2b[(dz * (across - 1) + dx - 1) * (rows - 1) + dy - 1])
            out_b[at, :, pl.ds(0, cut)] = block[:, pl.ds(0, cut)]
            out_b[at, :, pl.ds(cut, rest)] = total(block[:, pl.ds(cut, rest)], *arrived).astype(LOW)
            side_y[dz, dy] = send(
                out_b.at[at], r3y.at[at], s3y.at[at], q3y.at[at],
                device_at(dims, z, x, (y + dy) % rows, c),
            )

    def end(dz):
        arrived = []
        for dx in range(1, across):
            side_x[dz, dx].wait_recv()
            arrived.append(r3x[dz * (across - 1) + dx - 1])
        for dy in range(1, rows):
            side_y[dz, dy].wait_recv()
            arrived.append(r3y[dz * (rows - 1) + dy - 1])
        summed = total(mine[dz, x, y], *arrived)
        if dz:
            out_z[dz - 1] = summed.astype(LOW)
            last[dz] = send(
                out_z.at[dz - 1], r4.at[dz - 1], s4.at[dz - 1], q4.at[dz - 1],
                device_at(dims, (z + dz) % depth, x, y, c),
            )
        else:
            out[...] = summed

    for step in range(depth + 2):
        if step < depth:
            begin(order[step])
        if 0 <= step - 1 < depth:
            middle(order[step - 1])
        if 0 <= step - 2 < depth:
            end(order[step - 2])
    for dz in range(1, depth):
        last[dz].wait_recv()
        out[...] += r4[dz - 1].astype(F32)
    for group in (first, corner_a, corner_b, side_x, side_y, last):
        for copy in group.values():
            copy.wait_send()


def scatter_grads(dims, grads):
    depth, across, rows, cores = dims
    wide = depth * across
    height, width = grads.shape[0] // (wide * rows * cores), grads.shape[1]
    cut = (width // 256) * 128
    grads = grads.reshape(wide, rows, cores, height, width)
    n_x, n_y = depth * (across - 1), depth * (rows - 1)
    n_c = n_x * (rows - 1)
    sems = []
    for size in (depth, n_c, n_c, n_x, n_y, depth - 1):
        sems += [pltpu.SemaphoreType.DMA((size,))] * 2
    return pl.pallas_call(
        functools.partial(scatter_kernel, dims, cut),
        out_shape=jax.ShapeDtypeStruct((height, width), F32),
        in_specs=[pl.BlockSpec(memory_space=pl.ANY)],
        out_specs=pl.BlockSpec(memory_space=pltpu.VMEM),
        scratch_shapes=[
            pltpu.VMEM((depth, across, rows, height, width), LOW),
            pltpu.VMEM((depth, across, rows, height, width), LOW),
            pltpu.VMEM((n_c, height, cut), LOW),
            pltpu.VMEM((n_c, height, width - cut), LOW),
            pltpu.VMEM((n_x, height, width), LOW),
            pltpu.VMEM((n_y, height, width), LOW),
            pltpu.VMEM((depth - 1, height, width), LOW),
            pltpu.VMEM((n_x, height, width), LOW),
            pltpu.VMEM((n_y, height, width), LOW),
            pltpu.VMEM((depth - 1, height, width), LOW),
            *sems,
            pltpu.SemaphoreType.DMA((depth,)),
        ],
        compiler_params=pltpu.CompilerParams(
            collective_id=1, has_side_effects=True, vmem_limit_bytes=VMEM_LIMIT
        ),
        name="scatter_grads",
    )(grads)


def norm_parts(values):
    center = jnp.mean(values, axis=-1, keepdims=True)
    offset = values - center
    spread = jnp.mean(offset * offset, axis=-1, keepdims=True)
    scale = lax.rsqrt(spread + EPSILON)
    return offset * scale, scale


def fwd_kernel(
    experts, tokens, wq, wk, wv, wp, small, seg_col, seg_row, valid_row, routes,
    normed, q_out, k_out, v_out, attended, lse_rows, middle, moe_low, probs_out, gates_out, vecs,
    total, bias, lse,
):
    pair = pl.program_id(0)
    count, model = tokens.shape
    lanes = lax.broadcasted_iota(jnp.int32, (count, PAIR), 1)

    @pl.when(pair == 0)
    def _():
        turned = jnp.transpose(small[...].astype(F32))
        vecs[...] = turned[experts : experts + 8]
        xhat, _ = norm_parts(tokens[...].astype(F32))
        normed[...] = (xhat * vecs[0:1] + vecs[1:2]).astype(LOW)
        keys_at = lax.broadcasted_iota(jnp.int32, (count, count), 1)
        rows_at = lax.broadcasted_iota(jnp.int32, (count, count), 0)
        allowed = (seg_col[...] == seg_row[...]) & ((valid_row[...] == 1) | (keys_at == rows_at))
        bias[...] = jnp.where(allowed, 0.0, MASKED)
        total[...] = jnp.zeros_like(total)
        lse[...] = jnp.zeros_like(lse)

    here = pl.ds(pl.multiple_of(pair * PAIR, PAIR), PAIR)
    source = normed[...]
    queries = (dot(source, wq[...]) + vecs[2:3, here]).astype(LOW) * LOW(HEAD**-0.5)
    keys = dot(source, wk[...]).astype(LOW)
    values = (dot(source, wv[...]) + vecs[3:4, here]).astype(LOW)
    q_out[...] = queries
    k_out[...] = keys
    v_out[...] = values
    mixed = None
    for half in range(2):
        side = (lanes < HEAD) if half == 0 else (lanes >= HEAD)
        own_keys = jnp.where(side, keys, LOW(0))
        own_values = jnp.where(side, values, LOW(0))
        scores = dot_nt(queries, own_keys) + bias[...]
        peak = jnp.max(scores, axis=1, keepdims=True)
        raised = jnp.exp(scores - peak)
        row_total = jnp.sum(raised, axis=1, keepdims=True)
        attn = (raised * (1.0 / row_total)).astype(LOW)
        part = dot(attn, own_values)
        mixed = part if mixed is None else mixed + part
        lse[...] = jnp.where(lanes == 2 * pair + half, peak + jnp.log(row_total), lse[...])
    mixed = mixed.astype(LOW)
    attended[...] = mixed
    total[...] += dot(mixed, wp[...])

    @pl.when(pair == pl.num_programs(0) - 1)
    def _():
        lse_rows[...] = jnp.transpose(lse[...])
        mid = tokens[...].astype(F32) + (total[...] + vecs[4:5])
        middle[...] = mid
        xhat, _ = norm_parts(mid)
        low = (xhat * vecs[5:6] + vecs[6:7]).astype(LOW)
        moe_low[...] = low
        logits = jnp.where(lanes < experts, dot(low, small[...]), -jnp.inf)
        raised = jnp.exp(logits - jnp.max(logits, axis=1, keepdims=True))
        probs = raised / jnp.sum(raised, axis=1, keepdims=True)
        probs_out[...] = probs
        gate_a = jnp.sum(jnp.where(lanes == routes[:, 0:1], probs, 0.0), axis=1, keepdims=True)
        gate_b = jnp.sum(jnp.where(lanes == routes[:, 1:2], probs, 0.0), axis=1, keepdims=True)
        gates_out[...] = jnp.where(lanes == 0, gate_a, gate_b)


def attention_forward(experts, tokens, params, segment_ids, patch_valid, routes):
    count, model = tokens.shape
    pairs = model // PAIR
    full = lambda shape: pl.BlockSpec(shape, lambda p: (0,) * len(shape))
    column = lambda first: pl.BlockSpec((model, PAIR), lambda p: (0, first + p))
    moving = pl.BlockSpec((count, PAIR), lambda p: (0, p))
    low = lambda *shape: jax.ShapeDtypeStruct(shape, LOW)
    f32 = lambda *shape: jax.ShapeDtypeStruct(shape, F32)
    return pl.pallas_call(
        functools.partial(fwd_kernel, experts),
        grid=(pairs,),
        out_shape=(
            low(count, model), low(count, model), low(count, model), low(count, model),
            low(count, model), f32(PAIR, count), f32(count, model), low(count, model),
            f32(count, PAIR), f32(count, PAIR), f32(8, model),
        ),
        in_specs=[
            full((count, model)),
            column(0),
            column(pairs),
            column(2 * pairs),
            pl.BlockSpec((PAIR, model), lambda p: (p, 3)),
            pl.BlockSpec((model, PAIR), lambda p: (0, 4 * pairs)),
            full((count, 1)),
            full((1, count)),
            full((1, count)),
            full((count, 2)),
        ],
        out_specs=[
            full((count, model)), moving, moving, moving, moving, full((PAIR, count)),
            full((count, model)), full((count, model)), full((count, PAIR)), full((count, PAIR)),
            full((8, model)),
        ],
        scratch_shapes=[
            pltpu.VMEM((count, model), F32),
            pltpu.VMEM((count, count), F32),
            pltpu.VMEM((count, PAIR), F32),
        ],
        compiler_params=pltpu.CompilerParams(
            dimension_semantics=("arbitrary",), vmem_limit_bytes=VMEM_LIMIT
        ),
        cost_estimate=pl.CostEstimate(flops=6 * 10**9, bytes_accessed=15 * 10**6, transcendentals=4 * 10**6),
        name="attention_forward",
    )(tokens, params, params, params, params, params, segment_ids.reshape(count, 1), segment_ids, patch_valid, routes)


def norm_back(grad, gain, xhat, scale):
    scaled = grad * gain
    mean_a = jnp.mean(scaled, axis=-1, keepdims=True)
    mean_b = jnp.mean(scaled * xhat, axis=-1, keepdims=True)
    return scale * (scaled - mean_a - xhat * mean_b)


def bwd_kernel(
    experts, tokens, normed, queries, keys, values, attended, lse_rows, middle, moe_low, probs, vecs,
    wq, wk, wv, wp, small, seg_col, seg_row, valid_col, routes, slots, token_rows, gate_slots, cotangent,
    grads, tokens_grad,
    bias, normed_t, branch, middle_grad, total, sums, moe_total, router,
):
    pair = pl.program_id(0)
    count, model = tokens.shape
    lanes = lax.broadcasted_iota(jnp.int32, (count, PAIR), 1)

    @pl.when(pair == 0)
    def _():
        keys_at = lax.broadcasted_iota(jnp.int32, (count, count), 0)
        rows_at = lax.broadcasted_iota(jnp.int32, (count, count), 1)
        allowed = (seg_col[...] == seg_row[...]) & ((valid_col[...] == 1) | (keys_at == rows_at))
        bias[...] = jnp.where(allowed, 0.0, MASKED)
        normed_t[...] = jnp.transpose(normed[...])
        total[...] = jnp.zeros_like(total)
        sums[...] = jnp.zeros_like(sums)
        total_slots = token_rows.shape[0]
        slot_at = lax.broadcasted_iota(jnp.int32, (count, total_slots), 1)
        hit_a = slot_at == slots[:, 0:1]
        hit_b = slot_at == slots[:, 1:2]
        picked = jnp.where(hit_a | hit_b, 1.0, 0.0).astype(LOW)
        moe_total[...] = dot(picked, token_rows[...])
        grad_a = jnp.sum(jnp.where(hit_a, gate_slots[...], 0.0), axis=1, keepdims=True)
        grad_b = jnp.sum(jnp.where(hit_b, gate_slots[...], 0.0), axis=1, keepdims=True)
        prob_grad = jnp.where(lanes == routes[:, 0:1], grad_a, 0.0) + jnp.where(
            lanes == routes[:, 1:2], grad_b, 0.0
        )
        own = probs[...]
        logit_grad = (own * (prob_grad - jnp.sum(prob_grad * own, axis=1, keepdims=True))).astype(LOW)
        router[...] = dot_tn(moe_low[...], logit_grad)
        moe_grad = moe_total[...] + dot_nt(logit_grad, small[...])
        xhat, scale = norm_parts(middle[...])
        sums[5:6] = jnp.sum(moe_grad * xhat, axis=0, keepdims=True)
        sums[6:7] = jnp.sum(moe_grad, axis=0, keepdims=True)
        mid = cotangent[...].astype(F32) + norm_back(moe_grad, vecs[5:6], xhat, scale)
        middle_grad[...] = mid
        low = mid.astype(LOW)
        branch[...] = low
        sums[4:5] = jnp.sum(low.astype(F32), axis=0, keepdims=True)

    here = pl.ds(pl.multiple_of(pair * PAIR, PAIR), PAIR)
    upward = branch[...]
    grad_mixed = dot_nt(upward, wp[...]).astype(LOW)
    grads[here, 3 * model : 4 * model] = dot_tn(attended[...], upward).astype(grads.dtype)
    q_pair, k_pair, v_pair = queries[...], keys[...], values[...]
    k_turned = jnp.transpose(k_pair)
    sides = lax.broadcasted_iota(jnp.int32, (PAIR, count), 0)
    q_grad_t, k_grad, v_grad = None, None, None
    for half in range(2):
        side = (lanes < HEAD) if half == 0 else (lanes >= HEAD)
        side_t = (sides < HEAD) if half == 0 else (sides >= HEAD)
        own_keys = jnp.where(side, k_pair, LOW(0))
        own_values = jnp.where(side, v_pair, LOW(0))
        own_queries = jnp.where(side, q_pair, LOW(0))
        own_grads = jnp.where(side, grad_mixed, LOW(0))
        own_turned = jnp.where(side_t, k_turned, LOW(0))
        scores = dot_nt(own_keys, q_pair) + bias[...]
        attn = jnp.exp(scores - lse_rows[pl.ds(2 * pair + half, 1), :])
        attn_grad = dot_nt(own_values, grad_mixed)
        mean = jnp.sum(attn * attn_grad, axis=0, keepdims=True)
        score_grad = (attn * (attn_grad - mean)).astype(LOW)
        v_part = dot(attn.astype(LOW), own_grads)
        k_part = dot(score_grad, own_queries)
        q_part = dot(own_turned, score_grad)
        if half == 0:
            q_grad_t, k_grad, v_grad = q_part, k_part, v_part
        else:
            q_grad_t, k_grad, v_grad = q_grad_t + q_part, k_grad + k_part, v_grad + v_part
    q_grad = (jnp.transpose(q_grad_t) * HEAD**-0.5).astype(LOW)
    k_grad = k_grad.astype(LOW)
    v_grad = v_grad.astype(LOW)
    sums[2:3, here] = jnp.sum(q_grad.astype(F32), axis=0, keepdims=True)
    sums[3:4, here] = jnp.sum(v_grad.astype(F32), axis=0, keepdims=True)
    source = normed_t[...]
    for which, part in enumerate((q_grad, k_grad, v_grad)):
        at = pl.ds(pl.multiple_of(which * model + pair * PAIR, PAIR), PAIR)
        grads[:, at] = dot(source, part).astype(grads.dtype)
    total[...] += dot_nt(q_grad, wq[...]) + dot_nt(k_grad, wk[...]) + dot_nt(v_grad, wv[...])

    @pl.when(pair == pl.num_programs(0) - 1)
    def _():
        grad = total[...]
        xhat, scale = norm_parts(tokens[...].astype(F32))
        sums[0:1] = jnp.sum(grad * xhat, axis=0, keepdims=True)
        sums[1:2] = jnp.sum(grad, axis=0, keepdims=True)
        tokens_grad[...] = (middle_grad[...] + norm_back(grad, vecs[0:1], xhat, scale)).astype(LOW)
        stacked = jnp.concatenate([sums[...], jnp.zeros((PAIR - 8, model), F32)], axis=0)
        turned = pltpu.roll(jnp.transpose(stacked), experts, 1)
        wide_lanes = lax.broadcasted_iota(jnp.int32, (model, PAIR), 1)
        grads[:, 4 * model :] = jnp.where(wide_lanes < experts, router[...], turned).astype(grads.dtype)


def attention_backward(
    experts, tokens, saved, params, segment_ids, patch_valid, routes, slots, token_rows, gate_slots, cotangent
):
    normed, queries, keys, values, attended, lse_rows, middle, moe_low, probs, vecs = saved
    count, model = tokens.shape
    pairs = model // PAIR
    total_slots = token_rows.shape[0]
    full = lambda shape: pl.BlockSpec(shape, lambda p: (0,) * len(shape))
    column = lambda first: pl.BlockSpec((model, PAIR), lambda p: (0, first + p))
    moving = pl.BlockSpec((count, PAIR), lambda p: (0, p))
    return pl.pallas_call(
        functools.partial(bwd_kernel, experts),
        grid=(pairs,),
        out_shape=(
            jax.ShapeDtypeStruct((model, 4 * model + PAIR), LOW),
            jax.ShapeDtypeStruct((count, model), LOW),
        ),
        in_specs=[
            full((count, model)),
            full((count, model)),
            moving, moving, moving, moving,
            full((PAIR, count)),
            full((count, model)),
            full((count, model)),
            full((count, PAIR)),
            full((8, model)),
            column(0),
            column(pairs),
            column(2 * pairs),
            pl.BlockSpec((PAIR, model), lambda p: (p, 3)),
            pl.BlockSpec((model, PAIR), lambda p: (0, 4 * pairs)),
            full((count, 1)),
            full((1, count)),
            full((count, 1)),
            full((count, 2)),
            full((count, 2)),
            full((total_slots, model)),
            full((1, total_slots)),
            full((count, model)),
        ],
        out_specs=[full((model, 4 * model + PAIR)), full((count, model))],
        scratch_shapes=[
            pltpu.VMEM((count, count), F32),
            pltpu.VMEM((model, count), LOW),
            pltpu.VMEM((count, model), LOW),
            pltpu.VMEM((count, model), F32),
            pltpu.VMEM((count, model), F32),
            pltpu.VMEM((8, model), F32),
            pltpu.VMEM((count, model), F32),
            pltpu.VMEM((model, PAIR), F32),
        ],
        compiler_params=pltpu.CompilerParams(
            dimension_semantics=("arbitrary",), vmem_limit_bytes=VMEM_LIMIT
        ),
        cost_estimate=pl.CostEstimate(flops=14 * 10**9, bytes_accessed=25 * 10**6, transcendentals=4 * 10**6),
        name="attention_backward",
    )(
        tokens, normed, queries, keys, values, attended, lse_rows, middle, moe_low, probs, vecs,
        params, params, params, params, params,
        segment_ids.reshape(count, 1), segment_ids, patch_valid.reshape(count, 1), routes, slots,
        token_rows, gate_slots, cotangent,
    )


def gelu_and_slope(v):
    root = 0.7978845608028654
    cubic = 0.044715
    square = v * v
    bend = jnp.tanh(root * v * (1.0 + cubic * square))
    slope = 0.5 * (1.0 + bend) + 0.5 * v * (1.0 - bend * bend) * root * (1.0 + 3.0 * cubic * square)
    return 0.5 * v * (1.0 + bend), slope


def expert_kernel(
    rows, ups, gates, w_in, b_in, w_out, b_out,
    y_out, dx_out, gate_grad, hidden_out, pre_out, bias_grad, out_bias_grad, weighted_out,
    y_acc, dx_acc, gate_acc,
):
    part = pl.program_id(0)
    x = rows[...]
    g = ups[...]

    @pl.when(part == 0)
    def _():
        y_acc[...] = jnp.zeros_like(y_acc)
        dx_acc[...] = jnp.zeros_like(dx_acc)
        gate_acc[...] = jnp.zeros_like(gate_acc)
        weighted = (gates[...] * g.astype(F32)).astype(LOW)
        weighted_out[...] = weighted
        out_bias_grad[...] = jnp.sum(weighted.astype(F32), axis=0, keepdims=True)

    pre = dot(x, w_in[0]) + b_in[...].astype(F32)
    back = dot_nt(g, w_out[0])
    value, slope = gelu_and_slope(pre)
    hidden = value.astype(LOW)
    gate_acc[...] += jnp.sum(hidden.astype(F32) * back, axis=1, keepdims=True)
    pre_grad = (slope * (gates[...] * back)).astype(LOW)
    hidden_out[...] = hidden
    pre_out[...] = pre_grad
    bias_grad[...] = jnp.sum(pre_grad.astype(F32), axis=0, keepdims=True)
    y_acc[...] += dot(hidden, w_out[0])
    dx_acc[...] += dot_nt(pre_grad, w_in[0])

    @pl.when(part == pl.num_programs(0) - 1)
    def _():
        bias = b_out[...].astype(F32)
        y_out[...] = (y_acc[...] + bias).astype(LOW)
        dx_out[...] = dx_acc[...].astype(LOW)
        gate_grad[...] = gate_acc[...] + jnp.sum(g.astype(F32) * bias, axis=1, keepdims=True)


def expert_stage(rows, ups, gates, w_in, b_in, w_out, b_out):
    count, model = rows.shape
    parts, _, wide = w_in.shape
    full = lambda shape: pl.BlockSpec(shape, lambda p: (0,) * len(shape))
    low = lambda *shape: jax.ShapeDtypeStruct(shape, LOW)
    f32 = lambda *shape: jax.ShapeDtypeStruct(shape, F32)
    return pl.pallas_call(
        expert_kernel,
        grid=(parts,),
        out_shape=(
            low(count, model), low(count, model), f32(count, 1), low(count, parts * wide),
            low(count, parts * wide), f32(1, parts * wide), f32(1, model), low(count, model),
        ),
        in_specs=[
            full((count, model)), full((count, model)), full((count, 1)),
            pl.BlockSpec((1, model, wide), lambda p: (p, 0, 0)),
            pl.BlockSpec((1, wide), lambda p: (0, p)),
            pl.BlockSpec((1, wide, model), lambda p: (p, 0, 0)),
            full((1, model)),
        ],
        out_specs=[
            full((count, model)), full((count, model)), full((count, 1)),
            pl.BlockSpec((count, wide), lambda p: (0, p)),
            pl.BlockSpec((count, wide), lambda p: (0, p)),
            pl.BlockSpec((1, wide), lambda p: (0, p)),
            full((1, model)),
            full((count, model)),
        ],
        scratch_shapes=[
            pltpu.VMEM((count, model), F32), pltpu.VMEM((count, model), F32), pltpu.VMEM((count, 1), F32),
        ],
        compiler_params=pltpu.CompilerParams(
            dimension_semantics=("arbitrary",), vmem_limit_bytes=VMEM_LIMIT
        ),
        cost_estimate=pl.CostEstimate(flops=23 * 10**9, bytes_accessed=35 * 10**6, transcendentals=4 * 10**6),
        name="expert_stage",
    )(rows, ups, gates, w_in, b_in, w_out, b_out)


def pair_slots(routes, priority, valid, experts, capacity):
    labels = jnp.arange(experts, dtype=jnp.int32)
    hot = ((routes[:, :, None] == labels) & (valid[:, None, None] == 1)).astype(F32)
    ahead = (priority[None, :] < priority[:, None]).astype(LOW)
    both = hot.reshape(routes.shape[0], 2 * experts).astype(LOW)
    earlier = dot(ahead, both).reshape(routes.shape[0], 2, experts)
    filled = jnp.sum(hot[:, 0], axis=0)
    first = jnp.sum(earlier[:, 0] * hot[:, 0], axis=1)
    second = jnp.sum((earlier[:, 1] + filled) * hot[:, 1], axis=1)
    place = jnp.stack([first, second], axis=1).astype(jnp.int32)
    kept = (place < capacity) & (valid[:, None] == 1)
    return jnp.where(kept, routes * capacity + place, -1)


def per_device(
    dims,
    tokens, segment_ids, patch_valid, routes, priority, gain_attn, shift_attn, w_qkv, query_bias, value_bias,
    w_proj, proj_bias, gain_moe, shift_moe, w_router, w_in, in_bias, w_out, out_bias, cotangent,
):
    count, model = tokens.shape
    experts = w_router.shape[1]
    capacity = (210 * count + 100 * experts - 1) // (100 * experts)
    shard_rows = gain_attn.shape[0]
    vectors = jnp.stack(
        [gain_attn, shift_attn, query_bias, value_bias, proj_bias, gain_moe, shift_moe], axis=1
    )
    pack = jnp.concatenate(
        [w_qkv, w_proj, w_router, vectors, jnp.zeros((shard_rows, PAIR - 7 - experts), LOW)], axis=1
    )
    params = gather_params(dims, pack)

    slots = pair_slots(routes, priority[0], patch_valid[0], experts, capacity)
    slot_ids = jnp.arange(experts * capacity, dtype=jnp.int32)[:, None]
    hit_a = slot_ids == slots[:, 0][None, :]
    hit_b = slot_ids == slots[:, 1][None, :]
    dispatch = (hit_a | hit_b).astype(LOW)
    swap = functools.partial(lax.all_to_all, axis_name="wide", split_axis=0, concat_axis=0, tiled=True)
    up_rows = dot(dispatch, cotangent).astype(LOW).reshape(experts, capacity, model)
    ups = swap(up_rows).reshape(-1, model)
    full_in = lax.all_gather(w_in[0], "narrow", axis=0, tiled=False)
    full_out = lax.all_gather(w_out[0], "narrow", axis=0, tiled=False)
    full_in_bias = lax.all_gather(in_bias, "narrow", axis=1, tiled=True)

    (normed, queries, keys, values, attended, lse_rows, middle, moe_low, probs, gates, vecs) = attention_forward(
        experts, tokens, params, segment_ids, patch_valid, routes
    )
    gate_slot = jnp.sum(
        jnp.where(hit_a, gates[:, 0][None, :], 0.0) + jnp.where(hit_b, gates[:, 1][None, :], 0.0), axis=1
    )
    rows = swap(dot(dispatch, moe_low).astype(LOW).reshape(experts, capacity, model)).reshape(-1, model)
    gate_rows = swap(gate_slot.reshape(experts, capacity)).reshape(-1, 1)

    y, dx, gate_grad, hidden, pre_grad, bias_grad, out_bias_grad, weighted = expert_stage(
        rows, ups, gate_rows, full_in, full_in_bias, full_out, out_bias
    )
    token_rows = swap(dx.reshape(-1, capacity, model)).reshape(-1, model)
    gate_slots = swap(gate_grad.reshape(-1, capacity)).reshape(1, -1)
    returned = swap(y.reshape(-1, capacity, model)).reshape(-1, model)

    parts = full_in.shape[0]
    grad_in = dot_tn(pre_grad, rows).reshape(parts, -1, model).astype(LOW)
    grad_out = dot_tn(hidden, weighted).reshape(parts, -1, model).astype(LOW)
    grad_in = lax.psum_scatter(grad_in, "narrow", scatter_dimension=0, tiled=True)[0].astype(F32)
    grad_out = lax.psum_scatter(grad_out, "narrow", scatter_dimension=0, tiled=True)[0].astype(F32)
    grad_in_bias = lax.psum_scatter(bias_grad[0], "narrow", scatter_dimension=0, tiled=True)
    grad_out_bias = lax.psum(out_bias_grad, "narrow")

    grads, tokens_grad = attention_backward(
        experts, tokens,
        (normed, queries, keys, values, attended, lse_rows, middle, moe_low, probs, vecs),
        params, segment_ids, patch_valid, routes, slots, token_rows, gate_slots, cotangent,
    )
    shares = scatter_grads(dims, grads)

    picked_a = lax.dot_general(hit_a.astype(LOW), returned, (((0,), (0,)), ((), ())), preferred_element_type=F32)
    picked_b = lax.dot_general(hit_b.astype(LOW), returned, (((0,), (0,)), ((), ())), preferred_element_type=F32)
    block_out = (middle + gates[:, 0:1] * picked_a + gates[:, 1:2] * picked_b).astype(LOW)

    at = 4 * model + experts
    vector = lambda i: shares[:, at + i]
    return (
        block_out,
        tokens_grad,
        vector(0),
        vector(1),
        shares[:, : 3 * model],
        vector(2),
        vector(3),
        shares[:, 3 * model : 4 * model],
        vector(4),
        vector(5),
        vector(6),
        shares[:, 4 * model : at],
        jnp.transpose(grad_in)[None],
        grad_in_bias[None],
        grad_out[None],
        grad_out_bias,
    )


def solution(mesh):
    dims = grid_of(mesh.shape["wide"], mesh.shape["narrow"])
    every = ("wide", "narrow")
    rows, vector = P(every, None), P(every)
    return jax.shard_map(
        functools.partial(per_device, dims),
        mesh=mesh,
        in_specs=(
            rows, rows, rows, rows, rows, vector, vector, rows, vector, vector, rows, vector, vector, vector,
            rows, P("wide", None, "narrow"), P("wide", "narrow"), P("wide", "narrow", None), P("wide", None), rows,
        ),
        out_specs=(
            rows, rows, vector, vector, rows, vector, vector, rows, vector, vector, vector, rows,
            P("wide", None, "narrow"), P("wide", "narrow"), P("wide", "narrow", None), P("wide", None),
        ),
        check_vma=False,
    )
```

time: 936 us -> 444 us (0.47)
  waiting for transfers between devices: 319 us -> 79.7 us
  matrix products: 252 us -> 35.3 us
  Pallas kernels: 0 us -> 186 us
  blocking collectives: 247 us -> 72.4 us
  other arithmetic: 38.9 us -> 5.96 us
  local copies, waits for them, and re-layouts: 38.8 us -> 21.4 us
    dot_general x107 -> x7, matrix products: 252 us -> 35.3 us  [the longest x2 23.2 us: dot_tn(): lax.dot_general(a, b, (((0,), (0,)), ((), ())), preferred_element_type=F32)]
    pallas_call x0 -> x5, Pallas kernels: none -> 186 us  [the longest x1 48.6 us: gather_params(): pl.pallas_call(functools.partial(gather_kernel, dims, cut), out_shape=jax...]
    reduce_scatter x4 -> x2, waiting for transfers between devices: 167 us -> 0.01 us  [the longest x1 0.01 us: per_device(): lax.psum_scatter(grad_out, 'narrow', scatter_dimension=0, tiled=True)[0]]
    all_gather x4 -> x2, waiting for transfers between devices: 108 us -> 0.01 us  [the longest x1 0.01 us: per_device(): full_in = lax.all_gather(w_in[0], 'narrow', axis=0, tiled=False)]
    unnamed x2 -> x1, blocking collectives: 82 us -> 11.4 us
    all_gather x1, blocking collectives: 66.2 us -> 5.6 us  [per_device(): full_in_bias = lax.all_gather(in_bias, 'narrow', axis=1, tiled=True)]
    all_to_all x2, blocking collectives: 98.6 us -> 55.4 us  [the longest x1 46.3 us: per_device(): token_rows = swap(dx.reshape(-1, capacity, model)).reshape(-1, model)]
    all_to_all x2 -> x4, waiting for transfers between devices: 42.8 us -> 78.3 us  [the longest x1 40 us: per_device(): swap(dot(dispatch, moe_low).astype(LOW).reshape(experts, capacity, model))]
  transfers between devices with their start and end apart: 10 -> 8, of which waited for: 7 -> 3; matrix products, arithmetic and copies ran while one was open for 26% -> 10% of each run, Pallas kernels for 0% -> 33%
where the time goes in v1:
time: 444 us; the launch traced here: 435 us
  Pallas kernels  186 us (42%)
  waiting for transfers between devices  79.7 us (18%)
  blocking collectives  72.4 us (16%)
  matrix products  35.3 us (8%)
  local copies, waits for them, and re-layouts  21.4 us (5%)
  starting transfers between devices  19.4 us (4%)
  between operations  15.1 us (3%)
  other arithmetic  5.96 us (1%)
    pallas_call x1, Pallas kernels, gather_params(): pl.pallas_call(functools.partial(gather_kernel, dims, cut), out_shape=jax...  48.6 us
    all_to_all x1, blocking collectives, per_device(): token_rows = swap(dx.reshape(-1, capacity, model)).reshape(-1, model)  46.3 us
    pallas_call x1, Pallas kernels, expert_stage(): pl.pallas_call(expert_kernel, grid=(parts,), out_shape=(low(count, model)...  41.8 us
    all_to_all x1, waiting for transfers between devices, per_device(): swap(dot(dispatch, moe_low).astype(LOW).reshape(experts, capacity, model))  40 us
    pallas_call x1, Pallas kernels, attention_backward(): pl.pallas_call(functools.partial(bwd_kernel, experts), grid=(pairs,), out...  38.2 us
    all_to_all x1, waiting for transfers between devices, per_device(): ups = swap(up_rows).reshape(-1, model)  36.2 us
    pallas_call x1, Pallas kernels, scatter_grads(): pl.pallas_call(functools.partial(scatter_kernel, dims, cut), out_shape=ja...  33 us
    pallas_call x1, Pallas kernels, attention_forward(): pl.pallas_call(functools.partial(fwd_kernel, experts), grid=(pairs,), out...  24.5 us
  transfers between devices with their start and end apart: 8, of which 3 were waited for; matrix products, arithmetic and copies ran while one was open for 10% of the time, Pallas kernels for 33%

profile of v1, /device:TPU:0, one launch (start us, length us, event | category | flops | bytes accessed | tf_op | source)
XLA Modules:
  0.0 435.3 jit_solution(2863011239979354438)
XLA Ops:
  13.2 48.6 %gather_params.1 = bf16[32,24,3200]{2,1,0:T(8,128)(2,1)} custom-call(bf16[24,3200]{1,0:T(8,128)(2,1)} %concatenate.3.shard), custom_call_target="tpu_custom_call" | custom-call | tf_op jit(solution)/shard_map/gather_params/pallas_call | solution.py:174
  62.8 24.5 %attention_forward.1 = (bf16[576,768]{1,0:T(8,128)(2,1)}, bf16[576,768]{1,0:T(8,128)(2,1)}, bf16[576,768]{1,0:T(8,128)(2,1)}, bf16[576,768]{1,0:T(8,128)(2,1)}, ...) custom-call(bf16[576,768]{1,0:T(8,128)(2,1)} %tokens.3, ...), custom_call_target="tpu_custom_call" | custom-call | flops 6000000000 | bytes 15000000 | tf_op jit(solution)/shard_map/attention_forward/pallas_call | solution.py:418
  90.3 6.9 %all-to-all-start.2 = ((f32[8,1,152]{2,1,0:T(1,128)}), f32[8,1,152]{2,1,0:T(1,128)S(1)}, u32[]{:S(2)}, u32[]{:S(2)}) async-start(f32[8,1,152]{2,1,0:T(1,128)} %all_to_all.26), calls=%async_computation.2 | async-start | bytes 16384 | tf_op jit(solution)/shard_map/all_to_all | solution.py:758
  97.2 4.4 %convolution_convert_fusion.2 = bf16[1216,768]{1,0:T(8,128)(2,1)} fusion(bf16[576,768]{1,0:T(8,128)(2,1)} %get-tuple-element.39.moe_low, s32[576]{0:T(1024)S(1)} %get-tuple-element.148, s32[576]{0:T(1024)S(1)} %get-tuple-element.147), kind=kOutput, calls=%fused_computation.5 | convolution fusion | flops 1078874112 | bytes 2757120 | tf_op jit(solution)/shard_map/dot_general | solution.py:21
  101.6 2.1 all-to-all-done.2
  103.7 4.3 all-to-all-start
  108.0 3.3 convolution_convert_fusion.1
  111.3 40.0 %all-to-all-done = bf16[8,152,768]{2,1,0:T(8,128)(2,1)S(1)} async-done(((bf16[8,152,768]{2,1,0:T(8,128)(2,1)}), bf16[8,152,768]{2,1,0:T(8,128)(2,1)S(1)}, u32[]{:S(2)}, u32[]{:S(2)}) %all-to-all-start) | async-done | bytes 1867808 | tf_op jit(solution)/shard_map/all_to_all | solution.py:757
  151.3 4.3 all-to-all-start.1
  155.7 5.6 %all_gather.10.b_in = bf16[1,3072]{1,0:T(2,128)(2,1)} all-gather(bf16[1,768]{1,0:T(2,128)(2,1)S(1)} %copy-done.11), channel_id=1, replica_groups=mesh['wide'=8,'narrow'=4] {'narrow'}, dimensions={1}, use_global_device_ids=true | all-gather | bytes 7680 | tf_op jit(solution)/shard_map/all_gather | solution.py:749
  162.4 36.2 %all-to-all-done.1 = bf16[8,152,768]{2,1,0:T(8,128)(2,1)} async-done(((bf16[8,152,768]{2,1,0:T(8,128)(2,1)}), bf16[8,152,768]{2,1,0:T(8,128)(2,1)}, u32[]{:S(2)}, u32[]{:S(2)}) %all-to-all-start.1) | async-done | bytes 1867808 | tf_op jit(solution)/shard_map/all_to_all | solution.py:746
  198.6 41.8 %expert_stage.1 = (bf16[1216,768]{1,0:T(8,128)(2,1)}, bf16[1216,768]{1,0:T(8,128)(2,1)}, f32[1216,1]{1,0:T(8,128)}, bf16[1216,3072]{1,0:T(8,128)(2,1)}, bf16[121...) custom-call(bf16[1216,768]{1,0:T(8,128)(2,1)} %bitcast.89, ...), custom_call_target="tpu_custom_call" | custom-call | flops 23000000512 | bytes 35000000 | tf_op jit(solution)/shard_map/expert_stage/pallas_call | solution.py:675
  240.3 11.0 %fusion.6 = bf16[4,768,768]{2,1,0:T(8,128)(2,1)} fusion(bf16[1216,768,1]{1,0,2:T(8,128)(2,1)} %bitcast.90, bf16[152,4,8,768]{3,2,1,0:T(8,128)(2,1)} %bitcast.104), kind=kOutput, calls=%fused_computation.12 | convolution fusion | flops 5740167168 | bytes 14057472 | tf_op jit(solution)/shard_map/dot_general | solution.py:29
  252.9 12.2 %convolution_convert_fusion = bf16[3072,768]{1,0:T(8,128)(2,1)} fusion(bf16[1216,3072]{1,0:T(8,128)(2,1)} %get-tuple-element.55, bf16[1216,768]{1,0:T(8,128)(2,1)S(1)} %copy-done.25), kind=kOutput, calls=%fused_computation.3 | convolution fusion | flops 5740167168 | bytes 14057472 | tf_op jit(solution)/shard_map/dot_general | solution.py:29
  266.5 9.2 %all_to_all.39 = f32[8,1,152]{2,1,0:T(1,128)S(1)} all-to-all(f32[8,1,152]{2,1,0:T(1,128)S(1)} %all_to_all.32), channel_id=1, replica_groups=mesh['wide'=8,'narrow'=4] {'wide'}, dimensions={0} | all-to-all | bytes 9728 | tf_op jit(solution)/shard_map/all_to_all | solution.py:764
  275.6 46.3 %all_to_all.40 = bf16[8,152,768]{2,1,0:T(8,128)(2,1)} all-to-all(bf16[8,152,768]{2,1,0:T(8,128)(2,1)S(1)} %bitcast.91), channel_id=1, replica_groups=mesh['wide'=8,'narrow'=4] {'wide'}, dimensions={0} | all-to-all | bytes 3735552 | tf_op jit(solution)/shard_map/all_to_all | solution.py:763
  321.9 3.7 all-to-all-start.3
  327.8 11.4 %all-reduce.1 = (f32[3072]{0:T(1024)S(1)}, f32[1,768]{1,0:T(1,128)}) all-reduce(f32[3072]{0:T(1024)S(1)} %bitcast.95, f32[1,768]{1,0:T(1,128)S(1)} %copy-done.12), channel_id=3, replica_groups=mesh['wide'=8,'narrow'=4] {'narrow'}, use_global_device_ids=true, to_apply=%region_5.6.clone | all-reduce | flops 3840 | bytes 30720
  340.5 38.2 %attention_backward.1 = (bf16[768,3200]{1,0:T(8,128)(2,1)}, bf16[576,768]{1,0:T(8,128)(2,1)}) custom-call(bf16[576,768]{1,0:T(8,128)(2,1)} %tokens.3, bf16[576,768]{1,0:T(8,128)(2,1)} %get-tuple-element.41.normed, bf16[576,768]{1,0:T(8,128)(2,1)} %get-tuple-element.42.queries, bf16[576,768]{1,0:T(8,128)(2,1)} %get-tuple-element.43.keys, ...), custom_call_target="tpu_custom_call" | custom-call | flops 14000000000 | bytes 25000000 | tf_op jit(solution)/shard_map/attention_backward/pallas_call | solution.py:568
  378.7 33.0 %scatter_grads.1 = f32[24,3200]{1,0:T(8,128)} custom-call(bf16[8,2,2,24,3200]{4,3,2,1,0:T(8,128)(2,1)} %bitcast.84), custom_call_target="tpu_custom_call" | custom-call | tf_op jit(solution)/shard_map/scatter_grads/pallas_call | solution.py:312
  416.3 2.0 slice_reduce_fusion.5
  419.8 2.5 add_convert_fusion
  423.8 2.0 copy.138
  425.7 2.8 convert_element_type.53
  (114 shorter events, 24.0 us)
Async XLA Ops:
  7.2 191.3 %all-gather.3.cloned.1.call-start = ((), (), s32[]{:S(2)}) async-start(), calls=%async_computation.8 | async-start | bytes 5898240 | tf_op jit(solution)/shard_map/all_gather | solution.py:747
  8.0 3.9 copy-start.17
  8.0 4.0 copy-start.18
  8.0 4.1 copy-start.19
  8.0 4.2 copy-start.20
  8.0 4.3 copy-start.21
  8.0 4.4 %copy-start.4 = (bf16[24,2304]{1,0:T(8,128)(2,1)S(1)}, bf16[24,2304]{1,0:T(8,128)(2,1)}, u32[]{:S(2)}) copy-start(bf16[24,2304]{1,0:T(8,128)(2,1)} %param.27) | copy-start | bytes 331780
  8.0 4.4 %copy-start.6 = (bf16[24,768]{1,0:T(8,128)(2,1)S(1)}, bf16[24,768]{1,0:T(8,128)(2,1)}, u32[]{:S(2)}) copy-start(bf16[24,768]{1,0:T(8,128)(2,1)} %param.30) | copy-start | bytes 110596
  8.1 190.5 %all-gather.5.cloned.1.call-start = ((), (), s32[]{:S(2)}) async-start(), calls=%async_computation.9 | async-start | bytes 5898240 | tf_op jit(solution)/shard_map/all_gather | solution.py:748
  11.3 50.6 %copy-start = (s32[576,2]{1,0:T(8,128)}, s32[576,2]{1,0:T(8,128)S(1)}, u32[]{:S(2)}) copy-start(s32[576,2]{1,0:T(8,128)S(1)} %add_select_fusion.slots) | copy-start | bytes 13828
  13.2 48.6 %copy-start.10 = (s32[1,576]{1,0:T(1,128)S(1)}, s32[1,576]{1,0:T(1,128)}, u32[]{:S(2)}) copy-start(s32[1,576]{1,0:T(1,128)} %seg_row.3) | copy-start | bytes 6916
  90.3 13.4 %all-to-all-start.2 = ((f32[8,1,152]{2,1,0:T(1,128)}), f32[8,1,152]{2,1,0:T(1,128)S(1)}, u32[]{:S(2)}, u32[]{:S(2)}) async-start(f32[8,1,152]{2,1,0:T(1,128)} %all_to_all.26), calls=%async_computation.2 | async-start | bytes 16384 | tf_op jit(solution)/shard_map/all_to_all | solution.py:758
  101.6 6.4 %copy-start.23 = (bf16[576,768]{1,0:T(8,128)(2,1)S(1)}, bf16[576,768]{1,0:T(8,128)(2,1)}, u32[]{:S(2)}) copy-start(bf16[576,768]{1,0:T(8,128)(2,1)} %cotangent.1) | copy-start | bytes 2654212
  103.7 47.6 %all-to-all-start = ((bf16[8,152,768]{2,1,0:T(8,128)(2,1)}), bf16[8,152,768]{2,1,0:T(8,128)(2,1)S(1)}, u32[]{:S(2)}, u32[]{:S(2)}) async-start(bf16[8,152,768]{2,1,0:T(8,128)(2,1)} %bitcast.93), calls=%async_computation | async-start | bytes 3735552 | tf_op jit(solution)/shard_map/all_to_all | solution.py:757
  111.3 44.4 %copy-start.11 = (bf16[1,768]{1,0:T(2,128)(2,1)S(1)}, bf16[1,768]{1,0:T(2,128)(2,1)}, u32[]{:S(2)}) copy-start(bf16[1,768]{1,0:T(2,128)(2,1)} %param.36) | copy-start | bytes 4612
  151.3 47.3 %copy-start.1 = (bf16[8,152,768]{2,1,0:T(8,128)(2,1)}, bf16[8,152,768]{2,1,0:T(8,128)(2,1)S(1)}, u32[]{:S(2)}) copy-start(bf16[8,152,768]{2,1,0:T(8,128)(2,1)S(1)} %all-to-all-done) | copy-start | bytes 5603332
  151.3 47.3 %all-to-all-start.1 = ((bf16[8,152,768]{2,1,0:T(8,128)(2,1)}), bf16[8,152,768]{2,1,0:T(8,128)(2,1)}, u32[]{:S(2)}, u32[]{:S(2)}) async-start(bf16[8,152,768]{2,1,0:T(8,128)(2,1)} %bitcast.92), calls=%async_computation.1 | async-start | bytes 3735552 | tf_op jit(solution)/shard_map/all_to_all | solution.py:746
  155.6 266.7 %reduce-scatter.3.cloned.1.call-start = ((), (), s32[]{:S(2)}) async-start(), calls=%async_computation.10 | async-start | bytes 5898240 | tf_op jit(solution)/shard_map/reduce_scatter | solution.py:770
  251.4 174.3 %reduce-scatter.5.cloned.1.call-start = ((), (), s32[]{:S(2)}) async-start(), calls=%async_computation.11 | async-start | bytes 5898240 | tf_op jit(solution)/shard_map/reduce_scatter | solution.py:771
  265.1 10.6 %copy-start.2 = (bf16[1216,768]{1,0:T(8,128)(2,1)S(1)}, bf16[1216,768]{1,0:T(8,128)(2,1)}, u32[]{:S(2)}) copy-start(bf16[1216,768]{1,0:T(8,128)(2,1)} %get-tuple-element.49) | copy-start | bytes 5603332
  321.9 4.7 %copy-start.24 = (u32[32]{0:T(128)S(1)}, u32[32]{0:T(128)}, u32[]{:S(2)}) copy-start(u32[32]{0:T(128)} %constant.30) | copy-start | bytes 388
  321.9 5.9 %copy-start.9 = (f32[1,3072]{1,0:T(1,128)S(1)}, f32[1,3072]{1,0:T(1,128)}, u32[]{:S(2)}) copy-start(f32[1,3072]{1,0:T(1,128)} %get-tuple-element.54) | copy-start | bytes 36868
  321.9 5.9 %copy-start.12 = (f32[1,768]{1,0:T(1,128)S(1)}, f32[1,768]{1,0:T(1,128)}, u32[]{:S(2)}) copy-start(f32[1,768]{1,0:T(1,128)} %get-tuple-element.57) | copy-start | bytes 9220
  321.9 96.4 %all-to-all-start.3 = ((bf16[8,152,768]{2,1,0:T(8,128)(2,1)}), bf16[8,152,768]{2,1,0:T(8,128)(2,1)S(1)}, u32[]{:S(2)}, u32[]{:S(2)}) async-start(bf16[8,152,768]{2,1,0:T(8,128)(2,1)} %bitcast.19), calls=%async_computation.3 | async-start | bytes 3735552 | tf_op jit(solution)/shard_map/all_to_all | solution.py:765
  (10 other events, 24.2 us)
Sparse Core Ops, SparseCore 0:
  9.6 57.2 all-gather.2
  68.5 36.1 all-gather.4
  251.5 45.9 reduce-scatter.2
  300.1 48.1 reduce-scatter.4

commit v2 on v1

--- a/solution.py
+++ b/solution.py
@@ -60,127 +60,6 @@
     peers += [device_at(dims, z, x, (y + d) % rows, c) for d in range(1, rows)]
     peers += [device_at(dims, z, x, y, 1 - c)]
     return peers
-
-
-def gather_kernel(dims, cut, shard, out, s1, r1, sx, rx, sy, ry, sa, ra, sb, rb, sc, rc, local):
-    depth, across, rows, cores = dims
-    z, x, y, c = place_of(dims)
-    width = shard.shape[1]
-
-    def block(dz, dx, dy, core):
-        wide = ((z - dz) % depth) * across + (x - dx) % across
-        return out.at[(wide * rows + (y - dy) % rows) * cores + core]
-
-    def send(src, dst, ssem, rsem, to):
-        copy = pltpu.make_async_remote_copy(
-            src_ref=src, dst_ref=dst, send_sem=ssem, recv_sem=rsem, device_id=to, device_id_type=MESH
-        )
-        copy.start()
-        return copy
-
-    greet(neighbours(dims))
-    own = block(0, 0, 0, c)
-    keep = pltpu.make_async_copy(shard, own, local)
-    keep.start()
-    first, by_x, by_y, half_a, half_b, by_core = {}, {}, {}, {}, {}, {}
-    for dz in range(1, depth):
-        first[dz] = send(
-            shard, own, s1.at[dz - 1], r1.at[dz - 1], device_at(dims, (z + dz) % depth, x, y, c)
-        )
-
-    def to_core(dz, dx, dy):
-        at = (dz * across + dx) * rows + dy
-        src = shard if (dz, dx, dy) == (0, 0, 0) else block(dz, dx, dy, c)
-        by_core[at] = send(
-            src, block(dz, dx, dy, c), sc.at[at], rc.at[at], device_at(dims, z, x, y, 1 - c)
-        )
-
-    def spread(dz):
-        if dz:
-            first[dz].wait_recv()
-        src = block(dz, 0, 0, c) if dz else shard
-        for dx in range(1, across):
-            at = dz * (across - 1) + dx - 1
-            by_x[dz, dx] = send(
-                src, block(dz, 0, 0, c), sx.at[at], rx.at[at],
-                device_at(dims, z, (x + dx) % across, y, c),
-            )
-        for dy in range(1, rows):
-            at = dz * (rows - 1) + dy - 1
-            by_y[dz, dy] = send(
-                src, block(dz, 0, 0, c), sy.at[at], ry.at[at],
-                device_at(dims, z, x, (y + dy) % rows, c),
-            )
-        to_core(dz, 0, 0)
-
-    def corner(dz):
-        for dx in range(1, across):
-            by_x[dz, dx].wait_recv()
-            part = block(dz, dx, 0, c).at[:, pl.ds(0, cut)]
-            for dy in range(1, rows):
-                at = (dz * (across - 1) + dx - 1) * (rows - 1) + dy - 1
-                half_a[dz, dx, dy] = send(
-                    part, part, sa.at[at], ra.at[at], device_at(dims, z, x, (y + dy) % rows, c)
-                )
-            to_core(dz, dx, 0)
-        for dy in range(1, rows):
-            by_y[dz, dy].wait_recv()
-            part = block(dz, 0, dy, c).at[:, pl.ds(cut, width - cut)]
-            for dx in range(1, across):
-                at = (dz * (across - 1) + dx - 1) * (rows - 1) + dy - 1
-                half_b[dz, dx, dy] = send(
-                    part, part, sb.at[at], rb.at[at], device_at(dims, z, (x + dx) % across, y, c)
-                )
-            to_core(dz, 0, dy)
-
-    def finish(dz):
-        for dx in range(1, across):
-            for dy in range(1, rows):
-                half_a[dz, dx, dy].wait_recv()
-                half_b[dz, dx, dy].wait_recv()
-                to_core(dz, dx, dy)
-
-    for step in range(depth + 2):
-        if step < depth:
-            spread(step)
-        if 0 <= step - 1 < depth:
-            corner(step - 1)
-        if 0 <= step - 2 < depth:
-            finish(step - 2)
-    for copy in by_core.values():
-        copy.wait_recv()
-    for group in (first, by_x, by_y, half_a, half_b, by_core):
-        for copy in group.values():
-            copy.wait_send()
-    keep.wait()
-
-
-def gather_params(dims, shard):
-    depth, across, rows, cores = dims
-    count = depth * across * rows * cores
-    height, width = shard.shape
-    cut = (width // 256) * 128
-    sizes = (
-        depth - 1,
-        depth * (across - 1),
-        depth * (rows - 1),
-        depth * (across - 1) * (rows - 1),
-        depth * (across - 1) * (rows - 1),
-        depth * across * rows,
-    )
-    sems = []
-    for size in sizes:
-        sems += [pltpu.SemaphoreType.DMA((size,))] * 2
-    out = pl.pallas_call(
-        functools.partial(gather_kernel, dims, cut),
-        out_shape=jax.ShapeDtypeStruct((count, height, width), shard.dtype),
-        in_specs=[pl.BlockSpec(memory_space=pl.ANY)],
-        out_specs=pl.BlockSpec(memory_space=pl.ANY),
-        scratch_shapes=sems + [pltpu.SemaphoreType.DMA],
-        compiler_params=pltpu.CompilerParams(collective_id=0, has_side_effects=True),
-        name="gather_params",
-    )(shard)
-    return out.reshape(count * height, width)
 
 
 def scatter_kernel(
@@ -343,114 +222,320 @@
     return offset * scale, scale
 
 
-def fwd_kernel(
-    experts, tokens, wq, wk, wv, wp, small, seg_col, seg_row, valid_row, routes,
-    normed, q_out, k_out, v_out, attended, lse_rows, middle, moe_low, probs_out, gates_out, vecs,
-    total, bias, lse,
+def column_of(row):
+    return jnp.transpose(jnp.broadcast_to(row, (PAIR, row.shape[1])))[:, 0:1]
+
+
+def front_kernel(
+    dims, experts, capacity, gathered, shard, tokens, seg_row, valid_row, routes, priority, cotangent, w_out, b_in, *rest
 ):
-    pair = pl.program_id(0)
+    depth, across, rows, cores = dims
+    wide, narrow = depth * across, rows * cores
+    (
+        params, normed, q_out, k_out, v_out, attended, lse_rows, middle, moe_low, probs_out, gates_out, vecs,
+        slots_out, slot_rows, ups, full_b_in,
+    ) = rest[:16]
+    side_out = rest[16 : 15 + rows]
+    (
+        total, bias, lse, up_send,
+        s1, r1, sx, rx, sy, ry, sa, ra, sb, rb, sc, rc, s_up, r_up, s_w, r_w, s_b, r_b, local,
+    ) = rest[15 + rows :]
+    z, x, y, c = place_of(dims)
+    me, n = z * across + x, y * cores + c
     count, model = tokens.shape
+    stride = ups.shape[1]
     lanes = lax.broadcasted_iota(jnp.int32, (count, PAIR), 1)
 
-    @pl.when(pair == 0)
-    def _():
-        turned = jnp.transpose(small[...].astype(F32))
-        vecs[...] = turned[experts : experts + 8]
-        xhat, _ = norm_parts(tokens[...].astype(F32))
-        normed[...] = (xhat * vecs[0:1] + vecs[1:2]).astype(LOW)
-        keys_at = lax.broadcasted_iota(jnp.int32, (count, count), 1)
-        rows_at = lax.broadcasted_iota(jnp.int32, (count, count), 0)
-        allowed = (seg_col[...] == seg_row[...]) & ((valid_row[...] == 1) | (keys_at == rows_at))
-        bias[...] = jnp.where(allowed, 0.0, MASKED)
-        total[...] = jnp.zeros_like(total)
-        lse[...] = jnp.zeros_like(lse)
-
-    here = pl.ds(pl.multiple_of(pair * PAIR, PAIR), PAIR)
-    source = normed[...]
-    queries = (dot(source, wq[...]) + vecs[2:3, here]).astype(LOW) * LOW(HEAD**-0.5)
-    keys = dot(source, wk[...]).astype(LOW)
-    values = (dot(source, wv[...]) + vecs[3:4, here]).astype(LOW)
-    q_out[...] = queries
-    k_out[...] = keys
-    v_out[...] = values
-    mixed = None
-    for half in range(2):
-        side = (lanes < HEAD) if half == 0 else (lanes >= HEAD)
-        own_keys = jnp.where(side, keys, LOW(0))
-        own_values = jnp.where(side, values, LOW(0))
-        scores = dot_nt(queries, own_keys) + bias[...]
-        peak = jnp.max(scores, axis=1, keepdims=True)
-        raised = jnp.exp(scores - peak)
-        row_total = jnp.sum(raised, axis=1, keepdims=True)
-        attn = (raised * (1.0 / row_total)).astype(LOW)
-        part = dot(attn, own_values)
-        mixed = part if mixed is None else mixed + part
-        lse[...] = jnp.where(lanes == 2 * pair + half, peak + jnp.log(row_total), lse[...])
-    mixed = mixed.astype(LOW)
-    attended[...] = mixed
-    total[...] += dot(mixed, wp[...])
-
-    @pl.when(pair == pl.num_programs(0) - 1)
-    def _():
-        lse_rows[...] = jnp.transpose(lse[...])
-        mid = tokens[...].astype(F32) + (total[...] + vecs[4:5])
-        middle[...] = mid
-        xhat, _ = norm_parts(mid)
-        low = (xhat * vecs[5:6] + vecs[6:7]).astype(LOW)
-        moe_low[...] = low
-        logits = jnp.where(lanes < experts, dot(low, small[...]), -jnp.inf)
-        raised = jnp.exp(logits - jnp.max(logits, axis=1, keepdims=True))
-        probs = raised / jnp.sum(raised, axis=1, keepdims=True)
-        probs_out[...] = probs
-        gate_a = jnp.sum(jnp.where(lanes == routes[:, 0:1], probs, 0.0), axis=1, keepdims=True)
-        gate_b = jnp.sum(jnp.where(lanes == routes[:, 1:2], probs, 0.0), axis=1, keepdims=True)
-        gates_out[...] = jnp.where(lanes == 0, gate_a, gate_b)
-
-
-def attention_forward(experts, tokens, params, segment_ids, patch_valid, routes):
+    def remote(src, dst, ssem, rsem, to):
+        return pltpu.make_async_remote_copy(
+            src_ref=src, dst_ref=dst, send_sem=ssem, recv_sem=rsem, device_id=to, device_id_type=MESH
+        )
+
+    def send(src, dst, ssem, rsem, to):
+        copy = remote(src, dst, ssem, rsem, to)
+        copy.start()
+        return copy
+
+    peers = [((me + d) % wide, n) for d in range(1, wide)]
+    peers += [(me, (n + d) % narrow) for d in range(1, narrow)]
+    greet(peers)
+
+    first, by_x, by_y, half_a, half_b, by_core = {}, {}, {}, {}, {}, {}
+    keeps = []
+    if not gathered:
+        width = shard.shape[1]
+        cut = (width // 256) * 128
+
+        def block(dz, dx, dy, core):
+            at = ((z - dz) % depth) * across + (x - dx) % across
+            return params.at[(at * rows + (y - dy) % rows) * cores + core]
+
+        own = block(0, 0, 0, c)
+        keeps.append(pltpu.make_async_copy(shard, own, local.at[0]))
+        keeps[-1].start()
+        for dz in range(1, depth):
+            first[dz] = send(
+                shard, own, s1.at[dz - 1], r1.at[dz - 1], device_at(dims, (z + dz) % depth, x, y, c)
+            )
+
+    def to_core(dz, dx, dy):
+        at = (dz * across + dx) * rows + dy
+        src = shard if (dz, dx, dy) == (0, 0, 0) else block(dz, dx, dy, c)
+        by_core[at] = send(
+            src, block(dz, dx, dy, c), sc.at[at], rc.at[at], device_at(dims, z, x, y, 1 - c)
+        )
+
+    def spread(dz):
+        if dz:
+            first[dz].wait_recv()
+        src = block(dz, 0, 0, c) if dz else shard
+        for dx in range(1, across):
+            at = dz * (across - 1) + dx - 1
+            by_x[dz, dx] = send(
+                src, block(dz, 0, 0, c), sx.at[at], rx.at[at],
+                device_at(dims, z, (x + dx) % across, y, c),
+            )
+        for dy in range(1, rows):
+            at = dz * (rows - 1) + dy - 1
+            by_y[dz, dy] = send(
+                src, block(dz, 0, 0, c), sy.at[at], ry.at[at],
+                device_at(dims, z, x, (y + dy) % rows, c),
+            )
+        to_core(dz, 0, 0)
+
+    def corner(dz):
+        for dx in range(1, across):
+            by_x[dz, dx].wait_recv()
+            part = block(dz, dx, 0, c).at[:, pl.ds(0, cut)]
+            for dy in range(1, rows):
+                at = (dz * (across - 1) + dx - 1) * (rows - 1) + dy - 1
+                half_a[dz, dx, dy] = send(
+                    part, part, sa.at[at], ra.at[at], device_at(dims, z, x, (y + dy) % rows, c)
+                )
+            to_core(dz, dx, 0)
+        for dy in range(1, rows):
+            by_y[dz, dy].wait_recv()
+            part = block(dz, 0, dy, c).at[:, pl.ds(cut, width - cut)]
+            for dx in range(1, across):
+                at = (dz * (across - 1) + dx - 1) * (rows - 1) + dy - 1
+                half_b[dz, dx, dy] = send(
+                    part, part, sb.at[at], rb.at[at], device_at(dims, z, (x + dx) % across, y, c)
+                )
+            to_core(dz, 0, dy)
+
+    def finish(dz):
+        for dx in range(1, across):
+            for dy in range(1, rows):
+                half_a[dz, dx, dy].wait_recv()
+                half_b[dz, dx, dy].wait_recv()
+                to_core(dz, dx, dy)
+
+    if not gathered:
+        spread(0)
+    b_copies = []
+    for d in range(1, narrow):
+        b_copies.append(send(b_in, full_b_in.at[n], s_b.at[d], r_b.at[d], (me, (n + d) % narrow)))
+    keeps.append(pltpu.make_async_copy(b_in, full_b_in.at[n], local.at[1]))
+    keeps[-1].start()
+
+    half = PAIR // 2
+    valid = valid_row[...].astype(F32)
+    valid_col = column_of(valid)
+    rank_row = priority[...].astype(F32)
+    ahead = jnp.where(rank_row < column_of(rank_row), 1.0, 0.0).astype(LOW)
+    first_at, second_at = routes[:, 0:1], routes[:, 1:2]
+    hit_first, hit_second = lanes == first_at, lanes == second_at + half
+    hot = jnp.where(hit_first | hit_second, valid_col, 0.0)
+    earlier = dot(ahead, hot.astype(LOW))
+    filled = pltpu.roll(jnp.sum(hot, axis=0, keepdims=True), half, 1)
+    filled = jnp.broadcast_to(jnp.where(lanes[0:1] >= half, filled, 0.0), (8, PAIR))[0:1]
+    earlier = earlier + filled
+    place_a = jnp.sum(jnp.where(hit_first, earlier, 0.0), axis=1, keepdims=True).astype(jnp.int32)
+    place_b = jnp.sum(jnp.where(hit_second, earlier, 0.0), axis=1, keepdims=True).astype(jnp.int32)
+    kept_a = (place_a < capacity) & (valid_col > 0.5)
+    kept_b = (place_b < capacity) & (valid_col > 0.5)
+    slot_a = jnp.where(kept_a, first_at * stride + place_a, -1)
+    slot_b = jnp.where(kept_b, second_at * stride + place_b, -1)
+    slots = jnp.where(lanes == 0, slot_a, slot_b)
+    slots_out[...] = slots
+    slot_rows[...] = jnp.transpose(slots.astype(F32))[0:8].astype(jnp.int32)
+
+    segments = seg_row[...].astype(F32)
+    keys_at = lax.broadcasted_iota(jnp.int32, (count, count), 1)
+    rows_at = lax.broadcasted_iota(jnp.int32, (count, count), 0)
+    allowed = (column_of(segments) == segments) & ((valid > 0.5) | (keys_at == rows_at))
+    bias[...] = jnp.where(allowed, 0.0, MASKED)
+    xhat, _ = norm_parts(tokens[...].astype(F32))
+    total[...] = xhat
+    lse[...] = jnp.zeros_like(lse)
+
+    row_at = lax.broadcasted_iota(jnp.int32, (stride, count), 0)
+
+    def up_copy(d, to):
+        return remote(up_send.at[to], ups.at[me], s_up.at[d], r_up.at[d], (to, n))
+
+    def rows_for(expert):
+        start = expert * stride
+        hit = (slot_rows[0:1] - start == row_at) | (slot_rows[1:2] - start == row_at)
+        return dot(jnp.where(hit, 1.0, 0.0).astype(LOW), cotangent[...]).astype(LOW)
+
+    def dispatch(k, carry):
+        d = (k + wide // 2 - 1) % (wide - 1) + 1
+        to = (me + d) % wide
+        up_send[to] = rows_for(to)
+        up_copy(d, to).start()
+        return carry
+
+    if not gathered:
+        for step in range(1, depth):
+            spread(step)
+            corner(step - 1)
+            if step >= 2:
+                finish(step - 2)
+        lax.fori_loop(0, (wide - 1) // 2, dispatch, 0)
+        corner(depth - 1)
+        finish(depth - 2)
+        lax.fori_loop((wide - 1) // 2, wide - 1, dispatch, 0)
+        finish(depth - 1)
+    else:
+        lax.fori_loop(0, wide - 1, dispatch, 0)
+        keeps.append(pltpu.make_async_copy(shard, params, local.at[0]))
+        keeps[-1].start()
+    up_send[me] = rows_for(me)
+    keep_up = pltpu.make_async_copy(up_send.at[me], ups.at[me], local.at[2])
+    keep_up.start()
+    for copy in by_core.values():
+        copy.wait_recv()
+    for copy in keeps:
+        copy.wait()
+    w_copies = []
+    for dy in range(1, rows):
+        w_copies.append(
+            send(
+                w_out, side_out[dy - 1], s_w.at[dy - 1], r_w.at[dy - 1],
+                device_at(dims, z, x, (y + dy) % rows, c),
+            )
+        )
+
+
+    def columns(at):
+        return params[:, at] if gathered else params[:, :, at].reshape(model, PAIR)
+
+    small = columns(pl.ds(4 * model, PAIR))
+    vecs[...] = jnp.transpose(small.astype(F32))[experts : experts + 8]
+    normed[...] = (total[...] * vecs[0:1] + vecs[1:2]).astype(LOW)
+
+    def attend(pair, carry):
+        at = lambda which: pl.ds(pl.multiple_of(which * model + pair * PAIR, PAIR), PAIR)
+        here = at(0)
+        source = normed[...]
+        queries = (dot(source, columns(at(0))) + vecs[2:3, here]).astype(LOW) * LOW(HEAD**-0.5)
+        keys = dot(source, columns(at(1))).astype(LOW)
+        values = (dot(source, columns(at(2))) + vecs[3:4, here]).astype(LOW)
+        q_out[:, here] = queries
+        k_out[:, here] = keys
+        v_out[:, here] = values
+        mixed = None
+        for part in range(2):
+            side = (lanes < HEAD) if part == 0 else (lanes >= HEAD)
+            own_keys = jnp.where(side, keys, LOW(0))
+            own_values = jnp.where(side, values, LOW(0))
+            scores = dot_nt(queries, own_keys) + bias[...]
+            peak = jnp.max(scores, axis=1, keepdims=True)
+            raised = jnp.exp(scores - peak)
+            row_total = jnp.sum(raised, axis=1, keepdims=True)
+            attn = (raised * (1.0 / row_total)).astype(LOW)
+            piece = dot(attn, own_values)
+            mixed = piece if mixed is None else mixed + piece
+            lse[...] = jnp.where(lanes == 2 * pair + part, peak + jnp.log(row_total), lse[...])
+        mixed = mixed.astype(LOW)
+        attended[:, here] = mixed
+        return carry
+
+    lax.fori_loop(0, model // PAIR, attend, 0)
+
+    def project(pair, carry):
+        here = pl.ds(pl.multiple_of(pair * PAIR, PAIR), PAIR)
+        there = pl.ds(pl.multiple_of(3 * model + pair * PAIR, PAIR), PAIR)
+        total[:, here] = dot(attended[...], columns(there))
+        return carry
+
+    lax.fori_loop(0, model // PAIR, project, 0)
+    lse_rows[...] = jnp.transpose(lse[...])
+    mid = tokens[...].astype(F32) + (total[...] + vecs[4:5])
+    middle[...] = mid
+    xhat, _ = norm_parts(mid)
+    low = (xhat * vecs[5:6] + vecs[6:7]).astype(LOW)
+    moe_low[...] = low
+    logits = jnp.where(lanes < experts, dot(low, columns(pl.ds(4 * model, PAIR))), -jnp.inf)
+    raised = jnp.exp(logits - jnp.max(logits, axis=1, keepdims=True))
+    probs = raised / jnp.sum(raised, axis=1, keepdims=True)
+    probs_out[...] = probs
+    gate_a = jnp.sum(jnp.where(lanes == first_at, probs, 0.0), axis=1, keepdims=True)
+    gate_b = jnp.sum(jnp.where(lanes == second_at, probs, 0.0), axis=1, keepdims=True)
+    gates_out[...] = jnp.where(lanes == 0, gate_a, gate_b)
+
+    def settle(k, carry):
+        d = k + 1
+        up_copy(d, (me + d) % wide).wait_send()
+        up_copy(d, (me - d + wide) % wide).wait_recv()
+        return carry
+
+    lax.fori_loop(0, wide - 1, settle, 0)
+    keep_up.wait()
+    for copy in w_copies + b_copies:
+        copy.wait()
+    for group in (first, by_x, by_y, half_a, half_b, by_core):
+        for copy in group.values():
+            copy.wait_send()
+
+
+def front_stage(
+    dims, experts, capacity, stride, gathered, shard, tokens, segment_ids, patch_valid, routes, priority,
+    cotangent, w_out, in_bias,
+):
+    depth, across, rows, cores = dims
+    wide, narrow = depth * across, rows * cores
     count, model = tokens.shape
-    pairs = model // PAIR
-    full = lambda shape: pl.BlockSpec(shape, lambda p: (0,) * len(shape))
-    column = lambda first: pl.BlockSpec((model, PAIR), lambda p: (0, first + p))
-    moving = pl.BlockSpec((count, PAIR), lambda p: (0, p))
+    any_, vmem = pl.BlockSpec(memory_space=pl.ANY), pl.BlockSpec(memory_space=pltpu.VMEM)
     low = lambda *shape: jax.ShapeDtypeStruct(shape, LOW)
     f32 = lambda *shape: jax.ShapeDtypeStruct(shape, F32)
-    return pl.pallas_call(
-        functools.partial(fwd_kernel, experts),
-        grid=(pairs,),
+    i32 = lambda *shape: jax.ShapeDtypeStruct(shape, jnp.int32)
+    height, width = shard.shape
+    full = (height, width) if gathered else (wide * narrow, height, width)
+    corners = depth * (across - 1) * (rows - 1)
+    sems = []
+    for size in (
+        depth - 1, depth * (across - 1), depth * (rows - 1), corners, corners, depth * across * rows,
+        wide, rows - 1, narrow,
+    ):
+        sems += [pltpu.SemaphoreType.DMA((size,))] * 2
+    outs = pl.pallas_call(
+        functools.partial(front_kernel, dims, experts, capacity, gathered),
         out_shape=(
-            low(count, model), low(count, model), low(count, model), low(count, model),
-            low(count, model), f32(PAIR, count), f32(count, model), low(count, model),
-            f32(count, PAIR), f32(count, PAIR), f32(8, model),
+            low(*full), low(count, model), low(count, model), low(count, model), low(count, model),
+            low(count, model), f32(PAIR, count), f32(count, model), low(count, model), f32(count, PAIR),
+            f32(count, PAIR), f32(8, model), i32(count, PAIR), i32(8, count), low(wide, stride, model),
+            f32(narrow, 1, in_bias.shape[1]), *[low(*w_out.shape)] * (rows - 1),
         ),
-        in_specs=[
-            full((count, model)),
-            column(0),
-            column(pairs),
-            column(2 * pairs),
-            pl.BlockSpec((PAIR, model), lambda p: (p, 3)),
-            pl.BlockSpec((model, PAIR), lambda p: (0, 4 * pairs)),
-            full((count, 1)),
-            full((1, count)),
-            full((1, count)),
-            full((count, 2)),
-        ],
-        out_specs=[
-            full((count, model)), moving, moving, moving, moving, full((PAIR, count)),
-            full((count, model)), full((count, model)), full((count, PAIR)), full((count, PAIR)),
-            full((8, model)),
-        ],
+        in_specs=[any_] + [vmem] * 6 + [any_] * 2,
+        out_specs=[vmem] * 14 + [any_] * (1 + rows),
         scratch_shapes=[
             pltpu.VMEM((count, model), F32),
             pltpu.VMEM((count, count), F32),
             pltpu.VMEM((count, PAIR), F32),
+            pltpu.VMEM((wide, stride, model), LOW),
+            *sems,
+            pltpu.SemaphoreType.DMA((3,)),
         ],
         compiler_params=pltpu.CompilerParams(
-            dimension_semantics=("arbitrary",), vmem_limit_bytes=VMEM_LIMIT
+            collective_id=0, has_side_effects=True, vmem_limit_bytes=VMEM_LIMIT
         ),
-        cost_estimate=pl.CostEstimate(flops=6 * 10**9, bytes_accessed=15 * 10**6, transcendentals=4 * 10**6),
-        name="attention_forward",
-    )(tokens, params, params, params, params, params, segment_ids.reshape(count, 1), segment_ids, patch_valid, routes)
+        cost_estimate=pl.CostEstimate(flops=7 * 10**9, bytes_accessed=20 * 10**6, transcendentals=4 * 10**6),
+        name="front_stage",
+    )(shard, tokens, segment_ids, patch_valid, routes, priority, cotangent, w_out, in_bias)
+    params = outs[0] if gathered else outs[0].reshape(wide * narrow * height, width)
+    return params, outs[1:12], outs[12:16], outs[16:]
 
 
 def norm_back(grad, gain, xhat, scale):
@@ -590,7 +675,7 @@
             full((1, count)),
             full((count, 1)),
             full((count, 2)),
-            full((count, 2)),
+            full((count, PAIR)),
             full((total_slots, model)),
             full((1, total_slots)),
             full((count, model)),
@@ -628,95 +713,282 @@
     return 0.5 * v * (1.0 + bend), slope
 
 
-def expert_kernel(
-    rows, ups, gates, w_in, b_in, w_out, b_out,
-    y_out, dx_out, gate_grad, hidden_out, pre_out, bias_grad, out_bias_grad, weighted_out,
-    y_acc, dx_acc, gate_acc,
+def moe_kernel(
+    dims, moe_low, slot_rows, slot_cols, gates, ups, b_in, b_out, w_in, w_out, *rest
 ):
-    part = pl.program_id(0)
-    x = rows[...]
-    g = ups[...]
-
-    @pl.when(part == 0)
-    def _():
-        y_acc[...] = jnp.zeros_like(y_acc)
-        dx_acc[...] = jnp.zeros_like(dx_acc)
-        gate_acc[...] = jnp.zeros_like(gate_acc)
-        weighted = (gates[...] * g.astype(F32)).astype(LOW)
-        weighted_out[...] = weighted
-        out_bias_grad[...] = jnp.sum(weighted.astype(F32), axis=0, keepdims=True)
-
-    pre = dot(x, w_in[0]) + b_in[...].astype(F32)
-    back = dot_nt(g, w_out[0])
-    value, slope = gelu_and_slope(pre)
-    hidden = value.astype(LOW)
-    gate_acc[...] += jnp.sum(hidden.astype(F32) * back, axis=1, keepdims=True)
-    pre_grad = (slope * (gates[...] * back)).astype(LOW)
-    hidden_out[...] = hidden
-    pre_out[...] = pre_grad
-    bias_grad[...] = jnp.sum(pre_grad.astype(F32), axis=0, keepdims=True)
-    y_acc[...] += dot(hidden, w_out[0])
-    dx_acc[...] += dot_nt(pre_grad, w_in[0])
-
-    @pl.when(part == pl.num_programs(0) - 1)
-    def _():
-        bias = b_out[...].astype(F32)
-        y_out[...] = (y_acc[...] + bias).astype(LOW)
-        dx_out[...] = dx_acc[...].astype(LOW)
-        gate_grad[...] = gate_acc[...] + jnp.sum(g.astype(F32) * bias, axis=1, keepdims=True)
-
-
-def expert_stage(rows, ups, gates, w_in, b_in, w_out, b_out):
-    count, model = rows.shape
-    parts, _, wide = w_in.shape
-    full = lambda shape: pl.BlockSpec(shape, lambda p: (0,) * len(shape))
+    depth, across, rows, cores = dims
+    wide = depth * across
+    narrow = rows * cores
+    side_out = rest[: rows - 1]
+    rest = rest[rows - 1 :]
+    token_rows, gate_slots, y_out, own_grad = rest[:4]
+    side_grad = rest[4 : 3 + rows]
+    own_extra = rest[3 + rows]
+    side_extra = rest[4 + rows : 3 + 2 * rows]
+    (
+        full_in, full_out, x_send, x_here, g_send, g_here, dx_send, h_send, hidden, pre_grad, weighted,
+        x_turned, w_turned, grad_send, grad_here, extra, extra_here,
+        local, s_y, r_y, s_in, r_in, s_out, r_out, s_x, r_x, s_g, r_g, s_dx, r_dx, s_h, r_h, s_w, r_w, s_e, r_e,
+    ) = rest[3 + 2 * rows :]
+    z, x, y, c = place_of(dims)
+    me, n = z * across + x, y * cores + c
+    count, model = moe_low.shape
+    capacity = x_send.shape[1]
+    gate_width = g_send.shape[2]
+    ff = full_in.shape[2]
+    other = device_at(dims, z, x, y, 1 - c)
+
+    def remote(src, dst, ssem, rsem, to):
+        return pltpu.make_async_remote_copy(
+            src_ref=src, dst_ref=dst, send_sem=ssem, recv_sem=rsem, device_id=to, device_id_type=MESH
+        )
+
+    along_y = [device_at(dims, z, x, (y + i) % rows, c) for i in range(1, rows)]
+    greet([((me + d) % wide, n) for d in range(1, wide)] + [other] + along_y)
+
+    ups_at = [((y - i) % rows) * cores + c for i in range(rows)]
+    from_y, in_passes, out_loads, out_passes = [], [], [], []
+    for i, h in enumerate(ups_at):
+        if i:
+            from_y.append(remote(w_in.at[0], full_in.at[n], s_y.at[i - 1], r_y.at[i - 1], along_y[i - 1]))
+        src_out = w_out.at[0] if i == 0 else side_out[i - 1].at[0]
+        out_loads.append(pltpu.make_async_copy(src_out, full_out.at[h], local.at[i]))
+        out_passes.append(remote(src_out, full_out.at[h], s_out.at[i], r_out.at[i], other))
+        src_in = w_in.at[0] if i == 0 else full_in.at[h]
+        in_passes.append(remote(src_in, full_in.at[h], s_in.at[i], r_in.at[i], other))
+    in_load = pltpu.make_async_copy(w_in.at[0], full_in.at[n], local.at[rows])
+    for copy in from_y + out_loads + out_passes:
+        copy.start()
+
+    slot_a, slot_b = slot_cols[:, 0:1], slot_cols[:, 1:2]
+    gate_a, gate_b = gates[:, 0:1], gates[:, 1:2]
+    row_at = lax.broadcasted_iota(jnp.int32, (capacity, count), 0)
+    lane_at = lax.broadcasted_iota(jnp.int32, (count, gate_width), 1)
+    source = moe_low[...]
+
+    def rows_for(expert):
+        first = expert * capacity
+        hit = (slot_rows[0:1] - first == row_at) | (slot_rows[1:2] - first == row_at)
+        picked = dot(jnp.where(hit, 1.0, 0.0).astype(LOW), source).astype(LOW)
+        inside = lane_at < capacity
+        hit_a = (slot_a - first == lane_at) & inside
+        hit_b = (slot_b - first == lane_at) & inside
+        gate = jnp.where(hit_a, gate_a, 0.0) + jnp.where(hit_b, gate_b, 0.0)
+        return picked, jnp.sum(gate, axis=0, keepdims=True)
+
+    def x_copy(d, to):
+        return remote(x_send.at[to], x_here.at[me], s_x.at[d], r_x.at[d], (to, n))
+
+    def g_copy(d, to):
+        return remote(g_send.at[to], g_here.at[me], s_g.at[d], r_g.at[d], (to, n))
+
+    def dx_copy(d, to):
+        return remote(dx_send.at[to], token_rows.at[me], s_dx.at[d], r_dx.at[d], (to, n))
+
+    def h_copy(d, to):
+        return remote(h_send.at[to], gate_slots.at[me], s_h.at[d], r_h.at[d], (to, n))
+
+    def dispatch(k, carry):
+        d = (k + wide // 2 - 1) % (wide - 1) + 1
+        to = (me + d) % wide
+        picked, gate = rows_for(to)
+        x_send[to] = picked
+        g_send[to] = gate
+        x_copy(d, to).start()
+        g_copy(d, to).start()
+        return carry
+
+    lax.fori_loop(0, wide - 1, dispatch, 0)
+    in_load.start()
+    in_passes[0].start()
+    picked, gate = rows_for(me)
+    x_here[me] = picked
+    g_here[me] = gate
+    extra[...] = jnp.zeros_like(extra)
+    out_bias = b_out[...].astype(F32)
+    for copy in out_loads:
+        copy.wait()
+    for copy in out_passes:
+        copy.wait_recv()
+
+    def backs(k, carry):
+        two = pl.ds(2 * k, 2)
+        up = ups[two].reshape(2 * capacity, model)
+        for h in range(narrow):
+            back = dot_nt(up, full_out[h]).astype(LOW)
+            pre_grad[two, :, h * ff : (h + 1) * ff] = back.reshape(2, capacity, ff)
+        return carry
+
+    lax.fori_loop(0, wide // 2, backs, 0)
+    for i in range(1, rows):
+        from_y[i - 1].wait_recv()
+        in_passes[i].start()
+    in_load.wait()
+    for copy in in_passes:
+        copy.wait_recv()
+
+    def expert(src):
+        own = x_here[src]
+        up = ups[src]
+        gate = jnp.transpose(jnp.broadcast_to(g_here[src], (PAIR, gate_width)))[:capacity, 0:1]
+        weigh = (gate * up.astype(F32)).astype(LOW)
+        weighted[src] = weigh
+        back_total = jnp.sum(up.astype(F32) * out_bias, axis=1, keepdims=True)
+        dx = None
+        for h in range(narrow):
+            pre = dot(own, full_in[h]) + b_in[h]
+            back = pre_grad[src, :, h * ff : (h + 1) * ff].astype(F32)
+            value, slope = gelu_and_slope(pre)
+            low = value.astype(LOW)
+            hidden[src, :, h * ff : (h + 1) * ff] = low
+            back_total += jnp.sum(low.astype(F32) * back, axis=1, keepdims=True)
+            grad = (slope * (gate * back)).astype(LOW)
+            pre_grad[src, :, h * ff : (h + 1) * ff] = grad
+            extra[h, 0:1, :ff] += jnp.sum(grad.astype(F32), axis=0, keepdims=True)
+            part = dot_nt(grad, full_in[h])
+            dx = part if dx is None else dx + part
+        dx_send[src] = dx.astype(LOW)
+        spread = jnp.broadcast_to(back_total, (capacity, PAIR))
+        spread = jnp.concatenate([spread, jnp.zeros((gate_width - capacity, PAIR), F32)], axis=0)
+        h_send[src] = jnp.transpose(spread)[0:1]
+
+    expert(me)
+    keep_rows = pltpu.make_async_copy(dx_send.at[me], token_rows.at[me], local.at[rows + 1])
+    keep_gate = pltpu.make_async_copy(h_send.at[me], gate_slots.at[me], local.at[rows + 2])
+    keep_rows.start()
+    keep_gate.start()
+
+    def serve(k, carry):
+        d = jnp.where(k % 2 == 0, k // 2 + 1, wide - (k + 1) // 2)
+        src = (me - d + wide) % wide
+        x_copy(d, src).wait_recv()
+        g_copy(d, src).wait_recv()
+        expert(src)
+        dx_copy(d, src).start()
+        h_copy(d, src).start()
+        return carry
+
+    lax.fori_loop(0, wide - 1, serve, 0)
+
+    def outputs(src, carry):
+        total = None
+        for h in range(narrow):
+            part = dot(hidden[src, :, h * ff : (h + 1) * ff], full_out[h])
+            total = part if total is None else total + part
+        x_send[src] = (total + out_bias).astype(LOW)
+        return carry
+
+    def sent(k, carry):
+        to = (me + k + 1) % wide
+        x_copy(k + 1, to).wait_send()
+        g_copy(k + 1, to).wait_send()
+        return carry
+
+    lax.fori_loop(0, wide - 1, sent, 0)
+    lax.fori_loop(0, wide, outputs, 0)
+    keep_y = pltpu.make_async_copy(x_send, y_out, local.at[rows + 3])
+    keep_y.start()
+
+    all_rows = wide * capacity
+    x_turned[...] = jnp.transpose(x_here[...].reshape(all_rows, model))
+    w_turned[...] = jnp.transpose(weighted[...].reshape(all_rows, model))
+    bias_grad = jnp.sum(weighted[...].reshape(all_rows, model).astype(F32), axis=0, keepdims=True)
+    for h in range(narrow):
+        extra[h, 1:2] = bias_grad
+
+    def grad_of(h):
+        lanes = pl.ds(pl.multiple_of(h * ff, PAIR), ff)
+        grad_in = dot(x_turned[...], pre_grad[:, :, lanes].reshape(all_rows, ff))
+        grad_out = dot(w_turned[...], hidden[:, :, lanes].reshape(all_rows, ff))
+        return grad_in, grad_out
+
+    swaps = []
+    for i in range(rows):
+        at = (y + i) % rows
+        h = at * cores + 1 - c
+        grad_in, grad_out = grad_of(h)
+        grad_send[i, 0] = grad_in.astype(LOW)
+        grad_send[i, 1] = grad_out.astype(LOW)
+        swaps.append(remote(grad_send.at[i], grad_here.at[i], s_w.at[i], r_w.at[i], other))
+        swaps.append(remote(extra.at[h], extra_here.at[i], s_e.at[i], r_e.at[i], other))
+        swaps[-2].start()
+        swaps[-1].start()
+    keep_grads = []
+    for i in range(rows):
+        at = (y + i) % rows
+        grad_in, grad_out = grad_of(at * cores + c)
+        swaps[2 * i].wait_recv()
+        swaps[2 * i + 1].wait_recv()
+        target = own_grad if i == 0 else side_grad[i - 1]
+        target_extra = own_extra if i == 0 else side_extra[i - 1]
+        grad_here[i, 0] = (grad_in + grad_here[i, 0].astype(F32)).astype(LOW)
+        grad_here[i, 1] = (grad_out + grad_here[i, 1].astype(F32)).astype(LOW)
+        keep_grads.append(pltpu.make_async_copy(grad_here.at[i], target, local.at[rows + 4 + i]))
+        keep_grads[-1].start()
+        target_extra[...] = extra[at * cores + c] + extra_here[i]
+
+    def finish(k, carry):
+        d = k + 1
+        back = (me - d + wide) % wide
+        dx_copy(d, back).wait_recv()
+        h_copy(d, back).wait_recv()
+        dx_copy(d, back).wait_send()
+        h_copy(d, back).wait_send()
+        return carry
+
+    lax.fori_loop(0, wide - 1, finish, 0)
+    for copy in from_y + in_passes + out_passes + swaps:
+        copy.wait_send()
+    for copy in [keep_rows, keep_gate, keep_y] + keep_grads:
+        copy.wait()
+
+
+def moe_stage(dims, capacity, moe_low, slot_rows, slots, gates, ups, b_in, b_out, w_in, w_out, side_out):
+    depth, across, rows, cores = dims
+    wide, narrow = depth * across, rows * cores
+    count, model = moe_low.shape
+    ff = w_in.shape[2]
+    gate_width = -(-capacity // PAIR) * PAIR
+    any_, vmem = pl.BlockSpec(memory_space=pl.ANY), pl.BlockSpec(memory_space=pltpu.VMEM)
     low = lambda *shape: jax.ShapeDtypeStruct(shape, LOW)
     f32 = lambda *shape: jax.ShapeDtypeStruct(shape, F32)
-    return pl.pallas_call(
-        expert_kernel,
-        grid=(parts,),
+    sem = lambda size: [pltpu.SemaphoreType.DMA((size,))] * 2
+    outs = pl.pallas_call(
+        functools.partial(moe_kernel, dims),
         out_shape=(
-            low(count, model), low(count, model), f32(count, 1), low(count, parts * wide),
-            low(count, parts * wide), f32(1, parts * wide), f32(1, model), low(count, model),
+            low(wide, capacity, model), f32(wide, 1, gate_width), low(wide, capacity, model),
+            *[low(2, model, ff)] * rows, *[f32(8, model)] * rows,
         ),
-        in_specs=[
-            full((count, model)), full((count, model)), full((count, 1)),
-            pl.BlockSpec((1, model, wide), lambda p: (p, 0, 0)),
-            pl.BlockSpec((1, wide), lambda p: (0, p)),
-            pl.BlockSpec((1, wide, model), lambda p: (p, 0, 0)),
-            full((1, model)),
-        ],
-        out_specs=[
-            full((count, model)), full((count, model)), full((count, 1)),
-            pl.BlockSpec((count, wide), lambda p: (0, p)),
-            pl.BlockSpec((count, wide), lambda p: (0, p)),
-            pl.BlockSpec((1, wide), lambda p: (0, p)),
-            full((1, model)),
-            full((count, model)),
-        ],
+        in_specs=[vmem] * 7 + [any_] * (1 + rows),
+        out_specs=[any_] * (3 + rows) + [vmem] * rows,
         scratch_shapes=[
-            pltpu.VMEM((count, model), F32), pltpu.VMEM((count, model), F32), pltpu.VMEM((count, 1), F32),
+            pltpu.VMEM((narrow, model, ff), LOW),
+            pltpu.VMEM((narrow, ff, model), LOW),
+            pltpu.VMEM((wide, capacity, model), LOW),
+            pltpu.VMEM((wide, capacity, model), LOW),
+            pltpu.VMEM((wide, 1, gate_width), F32),
+            pltpu.VMEM((wide, 1, gate_width), F32),
+            pltpu.VMEM((wide, capacity, model), LOW),
+            pltpu.VMEM((wide, 1, gate_width), F32),
+            pltpu.VMEM((wide, capacity, narrow * ff), LOW),
+            pltpu.VMEM((wide, capacity, narrow * ff), LOW),
+            pltpu.VMEM((wide, capacity, model), LOW),
+            pltpu.VMEM((model, wide * capacity), LOW),
+            pltpu.VMEM((model, wide * capacity), LOW),
+            pltpu.VMEM((rows, 2, model, ff), LOW),
+            pltpu.VMEM((rows, 2, model, ff), LOW),
+            pltpu.VMEM((narrow, 8, model), F32),
+            pltpu.VMEM((rows, 8, model), F32),
+            pltpu.SemaphoreType.DMA((2 * rows + 4,)),
+            *sem(rows), *sem(rows), *sem(rows), *sem(wide), *sem(wide), *sem(wide), *sem(wide), *sem(rows), *sem(rows),
         ],
         compiler_params=pltpu.CompilerParams(
-            dimension_semantics=("arbitrary",), vmem_limit_bytes=VMEM_LIMIT
+            collective_id=2, has_side_effects=True, vmem_limit_bytes=60 * 1024 * 1024
         ),
-        cost_estimate=pl.CostEstimate(flops=23 * 10**9, bytes_accessed=35 * 10**6, transcendentals=4 * 10**6),
-        name="expert_stage",
-    )(rows, ups, gates, w_in, b_in, w_out, b_out)
-
-
-def pair_slots(routes, priority, valid, experts, capacity):
-    labels = jnp.arange(experts, dtype=jnp.int32)
-    hot = ((routes[:, :, None] == labels) & (valid[:, None, None] == 1)).astype(F32)
-    ahead = (priority[None, :] < priority[:, None]).astype(LOW)
-    both = hot.reshape(routes.shape[0], 2 * experts).astype(LOW)
-    earlier = dot(ahead, both).reshape(routes.shape[0], 2, experts)
-    filled = jnp.sum(hot[:, 0], axis=0)
-    first = jnp.sum(earlier[:, 0] * hot[:, 0], axis=1)
-    second = jnp.sum((earlier[:, 1] + filled) * hot[:, 1], axis=1)
-    place = jnp.stack([first, second], axis=1).astype(jnp.int32)
-    kept = (place < capacity) & (valid[:, None] == 1)
-    return jnp.where(kept, routes * capacity + place, -1)
+        cost_estimate=pl.CostEstimate(flops=36 * 10**9, bytes_accessed=25 * 10**6, transcendentals=4 * 10**6),
+        name="moe_stage",
+    )(moe_low, slot_rows, slots, gates, ups, b_in, b_out, w_in, w_out, *side_out)
+    return outs[:3], outs[3 : 3 + rows], outs[3 + rows :]
 
 
 def per_device(
@@ -734,53 +1006,43 @@
     pack = jnp.concatenate(
         [w_qkv, w_proj, w_router, vectors, jnp.zeros((shard_rows, PAIR - 7 - experts), LOW)], axis=1
     )
-    params = gather_params(dims, pack)
-
-    slots = pair_slots(routes, priority[0], patch_valid[0], experts, capacity)
-    slot_ids = jnp.arange(experts * capacity, dtype=jnp.int32)[:, None]
-    hit_a = slot_ids == slots[:, 0][None, :]
-    hit_b = slot_ids == slots[:, 1][None, :]
-    dispatch = (hit_a | hit_b).astype(LOW)
+    depth, across, rows, cores = dims
+    stride = -(-capacity // 16) * 16
+    gathered = shard_rows % 8 != 0
+    if gathered:
+        pack = lax.all_gather(pack, ("wide", "narrow"), axis=0, tiled=True)
+    params, saved, (slots, slot_rows, ups, full_b_in), side_out = front_stage(
+        dims, experts, capacity, stride, gathered, pack, tokens, segment_ids, patch_valid, routes, priority,
+        cotangent, w_out, in_bias.astype(F32),
+    )
+    normed, queries, keys, values, attended, lse_rows, middle, moe_low, probs, gates, vecs = saved
+    (token_rows, gate_slots, y), weight_grads, extras = moe_stage(
+        dims, stride, moe_low, slot_rows, slots, gates, ups, full_b_in, out_bias, w_in, w_out, side_out
+    )
     swap = functools.partial(lax.all_to_all, axis_name="wide", split_axis=0, concat_axis=0, tiled=True)
-    up_rows = dot(dispatch, cotangent).astype(LOW).reshape(experts, capacity, model)
-    ups = swap(up_rows).reshape(-1, model)
-    full_in = lax.all_gather(w_in[0], "narrow", axis=0, tiled=False)
-    full_out = lax.all_gather(w_out[0], "narrow", axis=0, tiled=False)
-    full_in_bias = lax.all_gather(in_bias, "narrow", axis=1, tiled=True)
-
-    (normed, queries, keys, values, attended, lse_rows, middle, moe_low, probs, gates, vecs) = attention_forward(
-        experts, tokens, params, segment_ids, patch_valid, routes
-    )
-    gate_slot = jnp.sum(
-        jnp.where(hit_a, gates[:, 0][None, :], 0.0) + jnp.where(hit_b, gates[:, 1][None, :], 0.0), axis=1
-    )
-    rows = swap(dot(dispatch, moe_low).astype(LOW).reshape(experts, capacity, model)).reshape(-1, model)
-    gate_rows = swap(gate_slot.reshape(experts, capacity)).reshape(-1, 1)
-
-    y, dx, gate_grad, hidden, pre_grad, bias_grad, out_bias_grad, weighted = expert_stage(
-        rows, ups, gate_rows, full_in, full_in_bias, full_out, out_bias
-    )
-    token_rows = swap(dx.reshape(-1, capacity, model)).reshape(-1, model)
-    gate_slots = swap(gate_grad.reshape(-1, capacity)).reshape(1, -1)
-    returned = swap(y.reshape(-1, capacity, model)).reshape(-1, model)
-
-    parts = full_in.shape[0]
-    grad_in = dot_tn(pre_grad, rows).reshape(parts, -1, model).astype(LOW)
-    grad_out = dot_tn(hidden, weighted).reshape(parts, -1, model).astype(LOW)
-    grad_in = lax.psum_scatter(grad_in, "narrow", scatter_dimension=0, tiled=True)[0].astype(F32)
-    grad_out = lax.psum_scatter(grad_out, "narrow", scatter_dimension=0, tiled=True)[0].astype(F32)
-    grad_in_bias = lax.psum_scatter(bias_grad[0], "narrow", scatter_dimension=0, tiled=True)
-    grad_out_bias = lax.psum(out_bias_grad, "narrow")
+    steps = [
+        [(y * cores + c, (y + d) % rows * cores + c) for y in range(rows) for c in range(cores)]
+        for d in range(1, rows)
+    ]
+    slot_ids = jnp.arange(experts * stride, dtype=jnp.int32)
+    hit_a = slots[:, 0:1] == slot_ids
+    hit_b = slots[:, 1:2] == slot_ids
+    returned = swap(y).reshape(-1, model)
+    pair_grad = weight_grads[0].astype(F32)
+    bias_rows = extras[0]
+    for step, grad, extra in zip(steps, weight_grads[1:], extras[1:]):
+        pair_grad = pair_grad + lax.ppermute(grad, "narrow", step).astype(F32)
+        bias_rows = bias_rows + lax.ppermute(extra, "narrow", step)
 
     grads, tokens_grad = attention_backward(
         experts, tokens,
         (normed, queries, keys, values, attended, lse_rows, middle, moe_low, probs, vecs),
-        params, segment_ids, patch_valid, routes, slots, token_rows, gate_slots, cotangent,
+        params, segment_ids, patch_valid, routes, slots, token_rows.reshape(-1, model),
+        gate_slots[:, 0, :stride].reshape(1, -1), cotangent,
     )
     shares = scatter_grads(dims, grads)
 
-    picked_a = lax.dot_general(hit_a.astype(LOW), returned, (((0,), (0,)), ((), ())), preferred_element_type=F32)
-    picked_b = lax.dot_general(hit_b.astype(LOW), returned, (((0,), (0,)), ((), ())), preferred_element_type=F32)
+    picked_a, picked_b = dot(hit_a.astype(LOW), returned), dot(hit_b.astype(LOW), returned)
     block_out = (middle + gates[:, 0:1] * picked_a + gates[:, 1:2] * picked_b).astype(LOW)
 
     at = 4 * model + experts
@@ -798,10 +1060,10 @@
         vector(5),
         vector(6),
         shares[:, 4 * model : at],
-        jnp.transpose(grad_in)[None],
-        grad_in_bias[None],
-        grad_out[None],
-        grad_out_bias,
+        pair_grad[0][None],
+        bias_rows[0:1, : w_in.shape[2]],
+        jnp.transpose(pair_grad[1])[None],
+        bias_rows[1:2],
     )
 
 

time: 444 us -> 295 us (0.66); the launches traced: 435 us -> 291 us
  waiting for transfers between devices: 79.7 us -> 0.01 us
  blocking collectives: 72.4 us -> 0 us
  Pallas kernels: 186 us -> 246 us
  matrix products: 35.3 us -> 7.13 us
  between operations: 15.1 us -> 1 us
  starting transfers between devices: 19.4 us -> 10.9 us
    all_to_all x4 -> x1, waiting for transfers between devices: 78.3 us -> 0.01 us  [per_device(): returned = swap(y).reshape(-1, model)]
    pallas_call x3 -> x2, Pallas kernels: 115 us -> 172 us  [the longest x1 94.7 us: moe_stage(): pl.pallas_call(functools.partial(moe_kernel, dims), out_shape=(low(wide,...]
    all_to_all x2 -> x0, blocking collectives: 55.4 us -> none  [the longest x1 46.3 us: per_device(): token_rows = swap(dx.reshape(-1, capacity, model)).reshape(-1, model)]
    dot_general x4 -> x0, matrix products: 27.2 us -> none  [the longest x2 23.2 us: dot_tn(): lax.dot_general(a, b, (((0,), (0,)), ((), ())), preferred_element_type=F32)]
    unnamed x1 -> x0, blocking collectives: 11.4 us -> none
    all_to_all x4 -> x1, starting transfers between devices: 19.2 us -> 8.82 us  [per_device(): returned = swap(y).reshape(-1, model)]
    all_gather x1 -> x0, blocking collectives: 5.6 us -> none  [per_device(): full_in_bias = lax.all_gather(in_bias, 'narrow', axis=1, tiled=True)]
    another operation x7, local copies, waits for them, and re-layouts: 0.69 us -> 5.23 us  [per_device(): jnp.stack([gain_attn, shift_attn, query_bias, value_bias, proj_bias, gain...]
  transfers between devices with their start and end apart: 8 -> 3, of which waited for: 3 -> 0; matrix products, arithmetic and copies ran while one was open for 10% -> 5% of each run, Pallas kernels for 33% -> 25%
where the time goes in v2:
time: 295 us; the launch traced here: 291 us
  Pallas kernels  246 us (83%)
  local copies, waits for them, and re-layouts  23.1 us (8%)
  starting transfers between devices  10.9 us (4%)
  matrix products  7.13 us (2%)
  other arithmetic  3.39 us (1%)
    pallas_call x1, Pallas kernels, moe_stage(): pl.pallas_call(functools.partial(moe_kernel, dims), out_shape=(low(wide,...  94.7 us
    pallas_call x1, Pallas kernels, front_stage(): pl.pallas_call(functools.partial(front_kernel, dims, experts, capacity, g...  77.4 us
    pallas_call x1, Pallas kernels, attention_backward(): pl.pallas_call(functools.partial(bwd_kernel, experts), grid=(pairs,), out...  38 us
    pallas_call x1, Pallas kernels, scatter_grads(): pl.pallas_call(functools.partial(scatter_kernel, dims, cut), out_shape=ja...  35.8 us
    all_to_all x1, starting transfers between devices, per_device(): returned = swap(y).reshape(-1, model)  8.82 us
    dot_general x2, matrix products, dot(): return jnp.dot(a, b, preferred_element_type=F32)  7.13 us
  transfers between devices with their start and end apart: 3, of which 0 were waited for; matrix products, arithmetic and copies ran while one was open for 5% of the time, Pallas kernels for 25%

profile of v2, /device:TPU:0, one launch (start us, length us, event | category | flops | bytes accessed | tf_op | source)
XLA Modules:
  0.0 291.5 jit_solution(5478835647893825559)
XLA Ops:
  0.6 0.8 copy.48
  1.4 0.7 copy.49
  2.2 0.7 copy.50
  5.9 0.7 copy.55
  6.6 1.6 copy.56.routes
  8.2 1.3 convert_element_type.14.b_in
  9.5 1.7 concatenate.3.shard
  11.1 77.4 %front_stage.1 = (bf16[32,24,3200]{2,1,0:T(8,128)(2,1)}, bf16[576,768]{1,0:T(8,128)(2,1)}, bf16[576,768]{1,0:T(8,128)(2,1)}, bf16[576,768]{1,0:T(8,128)(2,1)}, b...) custom-call(bf16[24,3200]{1,0:T(8,128)(2,1)} %concatenate.3.shard, ...), custom_call_target="tpu_custom_call" | custom-call | flops 7000000000 | bytes 20000000 | tf_op jit(solution)/shard_map/front_stage/pallas_call | solution.py:513
  88.5 94.7 %moe_stage.1 = (bf16[8,160,768]{2,1,0:T(8,128)(2,1)}, f32[8,1,256]{2,1,0:T(1,128)}, bf16[8,160,768]{2,1,0:T(8,128)(2,1)}, bf16[2,768,768]{2,1,0:T(8,128)(2,1)}, ...) custom-call(bf16[576,768]{1,0:T(8,128)(2,1)} %get-tuple-element.45.moe_low, ...), custom_call_target="tpu_custom_call" | custom-call | flops 35999997952 | bytes 25000000 | tf_op jit(solution)/shard_map/moe_stage/pallas_call | solution.py:956
  183.3 8.8 %all-to-all-start = ((bf16[8,160,768]{2,1,0:T(8,128)(2,1)}), bf16[8,160,768]{2,1,0:T(8,128)(2,1)}, u32[]{:S(2)}, u32[]{:S(2)}) async-start(bf16[8,160,768]{2,1,0:T(8,128)(2,1)} %get-tuple-element.50), calls=%async_computation | async-start | bytes 3932160 | tf_op jit(solution)/shard_map/all_to_all | solution.py:1030
  192.1 1.1 collective-permute-start
  193.2 1.0 collective-permute-start.1
  194.2 0.9 copy.57.seg_col
  195.1 0.9 copy.58.valid_col
  196.7 38.0 %attention_backward.1 = (bf16[768,3200]{1,0:T(8,128)(2,1)}, bf16[576,768]{1,0:T(8,128)(2,1)}) custom-call(bf16[576,768]{1,0:T(8,128)(2,1)} %tokens.3, bf16[576,768]{1,0:T(8,128)(2,1)} %get-tuple-element.51.normed, bf16[576,768]{1,0:T(8,128)(2,1)} %get-tuple-element.52.queries, bf16[576,768]{1,0:T(8,128)(2,1)} %get-tuple-element.53.keys, ...), custom_call_target="tpu_custom_call" | custom-call | flops 14000000000 | bytes 25000000 | tf_op jit(solution)/shard_map/attention_backward/pallas_call | solution.py:653
  234.7 35.8 %scatter_grads.1 = f32[24,3200]{1,0:T(8,128)} custom-call(bf16[8,2,2,24,3200]{4,3,2,1,0:T(8,128)(2,1)} %bitcast.21), custom_call_target="tpu_custom_call" | custom-call | tf_op jit(solution)/shard_map/scatter_grads/pallas_call | solution.py:191
  271.2 2.0 slice_reduce_fusion.4
  273.2 1.6 slice.64
  274.9 1.5 slice.67
  278.4 2.1 convert_add_fusion
  280.5 1.7 slice_bitcast_fusion
  282.2 1.9 copy.61
  284.2 3.1 %fusion = f32[576,768]{1,0:T(8,128)S(1)} fusion(bf16[1280,768]{1,0:T(8,128)(2,1)} %bitcast.7, s32[576]{0:T(1024)S(1)} %get-tuple-element.110), kind=kOutput, calls=%fused_computation.3 | convolution fusion | flops 1133199360 | bytes 3737856 | tf_op jit(solution)/shard_map/dot_general | solution.py:21
  287.3 4.0 %add_convert_fusion = bf16[576,768]{1,0:T(8,128)(2,1)} fusion(f32[576,768]{1,0:T(8,128)S(1)} %copy-done.8, f32[576,768]{1,0:T(8,128)S(1)} %fusion, bf16[1280,768]{1,0:T(8,128)(2,1)} %bitcast.7, s32[576]{0:T(1024)S(1)} %get-tuple-element.109, f32[576]{0:T(1024)S(1)} %get-tuple-element.108, f32[576]{0:T(1024)S(1)} %get-tuple-element.107), kind=kOutput, calls=%fused_computation.6 | convolution fusion | flops 1135411200 | bytes 6396672 | tf_op jit(solution)/shard_map/dot_general | solution.py:21
  (34 shorter events, 6.4 us)
Async XLA Ops:
  183.3 9.9 %copy-start.7 = (f32[8,768]{1,0:T(8,128)S(1)}, f32[8,768]{1,0:T(8,128)}, u32[]{:S(2)}) copy-start(f32[8,768]{1,0:T(8,128)} %get-tuple-element.67) | copy-start | bytes 73732
  183.3 11.0 %copy-start.6 = (s32[1,576]{1,0:T(1,128)S(1)}, s32[1,576]{1,0:T(1,128)}, u32[]{:S(2)}) copy-start(s32[1,576]{1,0:T(1,128)} %seg_row.3) | copy-start | bytes 6916
  183.3 11.8 %copy-start.5 = (s32[1,576]{1,0:T(1,128)S(1)}, s32[1,576]{1,0:T(1,128)}, u32[]{:S(2)}) copy-start(s32[1,576]{1,0:T(1,128)} %valid_row.1) | copy-start | bytes 6916
  183.3 12.7 %copy-start.4 = (f32[8,1,256]{2,1,0:T(1,128)S(1)}, f32[8,1,256]{2,1,0:T(1,128)}, u32[]{:S(2)}) copy-start(f32[8,1,256]{2,1,0:T(1,128)} %get-tuple-element.61) | copy-start | bytes 24580
  183.3 100.9 %all-to-all-start = ((bf16[8,160,768]{2,1,0:T(8,128)(2,1)}), bf16[8,160,768]{2,1,0:T(8,128)(2,1)}, u32[]{:S(2)}, u32[]{:S(2)}) async-start(bf16[8,160,768]{2,1,0:T(8,128)(2,1)} %get-tuple-element.50), calls=%async_computation | async-start | bytes 3932160 | tf_op jit(solution)/shard_map/all_to_all | solution.py:1030
  192.1 86.2 %collective-permute-start = (bf16[2,768,768]{2,1,0:T(8,128)(2,1)}, bf16[2,768,768]{2,1,0:T(8,128)(2,1)}, u32[]{:S(2)}, u32[]{:S(2)}) collective-permute-start(bf16[2,768,768]{2,1,0:T(8,128)(2,1)} %get-tuple-element.65), channel_id=1, source_target_pairs={{0,2},{1,3},{2,0},{3,1},{4,6},{5,7},{6,4},{7,5},{8,10},{9,11},{10,... | collective-permute-start | bytes 7077896 | tf_op jit(solution)/shard_map/ppermute | solution.py:1034
  193.2 84.6 %collective-permute-start.1 = (f32[8,768]{1,0:T(8,128)S(1)}, f32[8,768]{1,0:T(8,128)S(1)}, u32[]{:S(2)}, u32[]{:S(2)}) collective-permute-start(f32[8,768]{1,0:T(8,128)S(1)} %copy-done.7), channel_id=1, source_target_pairs={{0,2},{1,3},{2,0},{3,1},{4,6},{5,7},{6,4},{7,5},{8,10},{9,11},{10,... | collective-permute-start | bytes 73736 | tf_op jit(solution)/shard_map/ppermute | solution.py:1035
  234.7 35.8 %copy-start.2 = (s32[576,128]{1,0:T(8,128)S(1)}, s32[576,128]{1,0:T(8,128)}, u32[]{:S(2)}) copy-start(s32[576,128]{1,0:T(8,128)} %get-tuple-element.44.slot_cols.slots) | copy-start | bytes 884740
  234.7 36.2 %copy-start.1 = (f32[576,128]{1,0:T(8,128)S(1)}, f32[576,128]{1,0:T(8,128)}, u32[]{:S(2)}) copy-start(f32[576,128]{1,0:T(8,128)} %get-tuple-element.43.gates) | copy-start | bytes 884740
  234.7 43.0 %copy-start.3 = (f32[8,768]{1,0:T(8,128)S(1)}, f32[8,768]{1,0:T(8,128)}, u32[]{:S(2)}) copy-start(f32[8,768]{1,0:T(8,128)} %get-tuple-element.66) | copy-start | bytes 73732
  234.7 43.6 %copy-start = (bf16[2,768,768]{2,1,0:T(8,128)(2,1)S(1)}, bf16[2,768,768]{2,1,0:T(8,128)(2,1)}, u32[]{:S(2)}) copy-start(bf16[2,768,768]{2,1,0:T(8,128)(2,1)} %get-tuple-element.64) | copy-start | bytes 7077892
  284.2 3.1 %copy-start.8 = (f32[576,768]{1,0:T(8,128)S(1)}, f32[576,768]{1,0:T(8,128)}, u32[]{:S(2)}) copy-start(f32[576,768]{1,0:T(8,128)} %get-tuple-element.42.middle) | copy-start | bytes 5308420

commit v3 on v2

v3 whole, which is shorter than its diff:
```python
import functools

import jax
import jax.numpy as jnp
from jax import lax
from jax.experimental import pallas as pl
from jax.experimental.pallas import tpu as pltpu
from jax.sharding import PartitionSpec as P

HEAD = 64
PAIR = 2 * HEAD
EPSILON = 1e-06
MASKED = -1000000000.0
MESH = pl.DeviceIdType.MESH
LOW = jnp.bfloat16
F32 = jnp.float32
PIECES = 8
VMEM_LIMIT = 58 * 1024 * 1024


def dot(a, b):
    return jnp.dot(a, b, preferred_element_type=F32)


def dot_nt(a, b):
    return lax.dot_general(a, b, (((1,), (1,)), ((), ())), preferred_element_type=F32)


def dot_tn(a, b):
    return lax.dot_general(a, b, (((0,), (0,)), ((), ())), preferred_element_type=F32)


def grid_of(wide, narrow):
    along_x = 1 << ((wide.bit_length() - 1) // 2)
    return wide // along_x, along_x, narrow // 2, 2


def place_of(dims):
    depth, across, rows, cores = dims
    wide, narrow = lax.axis_index("wide"), lax.axis_index("narrow")
    return wide // across, wide % across, narrow // cores, narrow % cores


def device_at(dims, z, x, y, c):
    depth, across, rows, cores = dims
    return (z * across + x, y * cores + c)


def greet(peers):
    barrier = pltpu.get_barrier_semaphore()
    for peer in peers:
        pl.semaphore_signal(barrier, inc=1, device_id=peer, device_id_type=MESH)
    pl.semaphore_wait(barrier, len(peers))


def neighbours(dims):
    depth, across, rows, cores = dims
    z, x, y, c = place_of(dims)
    peers = [device_at(dims, (z + d) % depth, x, y, c) for d in range(1, depth)]
    peers += [device_at(dims, z, (x + d) % across, y, c) for d in range(1, across)]
    peers += [device_at(dims, z, x, (y + d) % rows, c) for d in range(1, rows)]
    peers += [device_at(dims, z, x, y, 1 - c)]
    return peers


def norm_parts(values):
    center = jnp.mean(values, axis=-1, keepdims=True)
    offset = values - center
    spread = jnp.mean(offset * offset, axis=-1, keepdims=True)
    scale = lax.rsqrt(spread + EPSILON)
    return offset * scale, scale


def column_of(row):
    return jnp.transpose(jnp.broadcast_to(row, (PAIR, row.shape[1])))[:, 0:1]


def front_kernel(
    dims, experts, capacity, gathered, heads, *rest
):
    depth, across, rows, cores = dims
    wide, narrow = depth * across, rows * cores
    pack_refs, rest = rest[:heads], rest[heads:]
    tokens, seg_row, valid_row, routes, priority, cotangent, w_out, b_in = rest[:8]
    rest = rest[8:]
    (
        params, normed_t, q_out, k_out, v_out, attended_t, lse_rows, middle, moe_low, moe_low_t, probs_out, gates_out, vecs,
        bias_t, slots_out, slot_rows, full_b_in, ups,
    ) = rest[:18]
    side_out = rest[18 : 17 + rows]
    (
        normed, attended, total, bias, lse, up_send, b_send, shard, turn, blank,
        s1, r1, sx, rx, sy, ry, sa, ra, sb, rb, sc, rc, s_up, r_up, s_w, r_w, s_b, r_b, local, blanks,
    ) = rest[17 + rows :]
    z, x, y, c = place_of(dims)
    me, n = z * across + x, y * cores + c
    count, model = tokens.shape
    stride = ups.shape[1]
    lanes = lax.broadcasted_iota(jnp.int32, (count, PAIR), 1)

    def remote(src, dst, ssem, rsem, to):
        return pltpu.make_async_remote_copy(
            src_ref=src, dst_ref=dst, send_sem=ssem, recv_sem=rsem, device_id=to, device_id_type=MESH
        )

    def send(src, dst, ssem, rsem, to):
        copy = remote(src, dst, ssem, rsem, to)
        copy.start()
        return copy

    if not gathered:
        w_qkv, w_proj, router_t, vectors = pack_refs
        packs = [
            pltpu.make_async_copy(w_qkv, shard.at[:, pl.ds(0, 3 * model)], local.at[3]),
            pltpu.make_async_copy(w_proj, shard.at[:, pl.ds(3 * model, model)], local.at[4]),
        ]
        for copy in packs:
            copy.start()
        height = shard.shape[0]
        turn[...] = jnp.zeros_like(turn)
        turn[0:experts, 0:height] = router_t[...].astype(F32)
        turn[experts : experts + 7, 0:height] = vectors[...].astype(F32)
        shard[:, 4 * model : 4 * model + PAIR] = jnp.transpose(turn[...])[0:height].astype(LOW)
    b_send[...] = b_in[...].astype(F32)
    peers = [((me + d) % wide, n) for d in range(1, wide)]
    peers += [(me, (n + d) % narrow) for d in range(1, narrow)]
    greet(peers)
    if not gathered:
        for copy in packs:
            copy.wait()

    first, by_x, by_y, half_a, half_b, by_core = {}, {}, {}, {}, {}, {}
    keeps = []
    if not gathered:
        width = shard.shape[1]
        cut = (width // 256) * 128

        def block(dz, dx, dy, core):
            at = ((z - dz) % depth) * across + (x - dx) % across
            return params.at[(at * rows + (y - dy) % rows) * cores + core]

        own = block(0, 0, 0, c)
        keeps.append(pltpu.make_async_copy(shard, own, local.at[0]))
        keeps[-1].start()
        for dz in range(1, depth):
            first[dz] = send(
                shard, own, s1.at[dz - 1], r1.at[dz - 1], device_at(dims, (z + dz) % depth, x, y, c)
            )

    def to_core(dz, dx, dy):
        at = (dz * across + dx) * rows + dy
        src = shard if (dz, dx, dy) == (0, 0, 0) else block(dz, dx, dy, c)
        by_core[at] = send(
            src, block(dz, dx, dy, c), sc.at[at], rc.at[at], device_at(dims, z, x, y, 1 - c)
        )

    def spread(dz):
        if dz:
            first[dz].wait_recv()
        src = block(dz, 0, 0, c) if dz else shard
        for dx in range(1, across):
            at = dz * (across - 1) + dx - 1
            by_x[dz, dx] = send(
                src, block(dz, 0, 0, c), sx.at[at], rx.at[at],
                device_at(dims, z, (x + dx) % across, y, c),
            )
        for dy in range(1, rows):
            at = dz * (rows - 1) + dy - 1
            by_y[dz, dy] = send(
                src, block(dz, 0, 0, c), sy.at[at], ry.at[at],
                device_at(dims, z, x, (y + dy) % rows, c),
            )
        to_core(dz, 0, 0)

    def corner(dz):
        for dx in range(1, across):
            by_x[dz, dx].wait_recv()
            part = block(dz, dx, 0, c).at[:, pl.ds(0, cut)]
            for dy in range(1, rows):
                at = (dz * (across - 1) + dx - 1) * (rows - 1) + dy - 1
                half_a[dz, dx, dy] = send(
                    part, part, sa.at[at], ra.at[at], device_at(dims, z, x, (y + dy) % rows, c)
                )
            to_core(dz, dx, 0)
        for dy in range(1, rows):
            by_y[dz, dy].wait_recv()
            part = block(dz, 0, dy, c).at[:, pl.ds(cut, width - cut)]
            for dx in range(1, across):
                at = (dz * (across - 1) + dx - 1) * (rows - 1) + dy - 1
                half_b[dz, dx, dy] = send(
                    part, part, sb.at[at], rb.at[at], device_at(dims, z, (x + dx) % across, y, c)
                )
            to_core(dz, 0, dy)

    def finish(dz):
        for dx in range(1, across):
            for dy in range(1, rows):
                half_a[dz, dx, dy].wait_recv()
                half_b[dz, dx, dy].wait_recv()
                to_core(dz, dx, dy)

    if not gathered:
        spread(0)
    b_copies = []
    for d in range(1, narrow):
        b_copies.append(send(b_send, full_b_in.at[n], s_b.at[d], r_b.at[d], (me, (n + d) % narrow)))
    keeps.append(pltpu.make_async_copy(b_send, full_b_in.at[n], local.at[1]))
    keeps[-1].start()
    w_copies = []

    piece = w_out.shape[1] // PIECES

    def weight_piece(i):
        for dy in range(1, rows):
            at = (dy - 1) * PIECES + i
            part = pl.ds(i * piece, piece)
            to = device_at(dims, z, x, (y + dy) % rows, c)
            w_copies.append(send(w_out.at[:, part], side_out[dy - 1].at[:, part], s_w.at[at], r_w.at[at], to))

    used = -(-capacity // 8) * 8
    fills = []
    if used < stride:
        blank[...] = jnp.zeros_like(blank)
        for w in range(wide):
            fills.append(pltpu.make_async_copy(blank, ups.at[w, pl.ds(used, stride - used)], blanks.at[w]))
            fills[-1].start()

    half = PAIR // 2
    valid = valid_row[...].astype(F32)
    valid_col = column_of(valid)
    rank_row = priority[...].astype(F32)
    ahead = jnp.where(rank_row < column_of(rank_row), 1.0, 0.0).astype(LOW)
    first_at = column_of(routes[0:1].astype(F32)).astype(jnp.int32)
    second_at = column_of(routes[1:2].astype(F32)).astype(jnp.int32)
    hit_first, hit_second = lanes == first_at, lanes == second_at + half
    hot = jnp.where(hit_first | hit_second, valid_col, 0.0)
    earlier = dot(ahead, hot.astype(LOW))
    filled = pltpu.roll(jnp.sum(hot, axis=0, keepdims=True), half, 1)
    filled = jnp.broadcast_to(jnp.where(lanes[0:1] >= half, filled, 0.0), (8, PAIR))[0:1]
    earlier = earlier + filled
    place_a = jnp.sum(jnp.where(hit_first, earlier, 0.0), axis=1, keepdims=True).astype(jnp.int32)
    place_b = jnp.sum(jnp.where(hit_second, earlier, 0.0), axis=1, keepdims=True).astype(jnp.int32)
    kept_a = (place_a < capacity) & (valid_col > 0.5)
    kept_b = (place_b < capacity) & (valid_col > 0.5)
    slot_a = jnp.where(kept_a, first_at * stride + place_a, -1)
    slot_b = jnp.where(kept_b, second_at * stride + place_b, -1)
    slots = jnp.where(lanes == 0, slot_a, slot_b)
    slots_out[...] = jnp.where(lanes < 2, slots, jnp.where(lanes == 2, first_at, second_at))
    slot_rows[...] = jnp.transpose(slots.astype(F32))[0:8].astype(jnp.int32)

    segments = seg_row[...].astype(F32)
    keys_at = lax.broadcasted_iota(jnp.int32, (count, count), 1)
    rows_at = lax.broadcasted_iota(jnp.int32, (count, count), 0)
    allowed = (column_of(segments) == segments) & ((valid > 0.5) | (keys_at == rows_at))
    bias[...] = jnp.where(allowed, 0.0, MASKED)
    xhat, _ = norm_parts(tokens[...].astype(F32))
    total[...] = xhat
    lse[...] = jnp.zeros_like(lse)

    row_at = lax.broadcasted_iota(jnp.int32, (stride, count), 0)

    def up_copy(d, to):
        body = pl.ds(0, used)
        return remote(up_send.at[to, body], ups.at[me, body], s_up.at[d], r_up.at[d], (to, n))

    def rows_for(expert):
        start = expert * stride
        hit = (slot_rows[0:1] - start == row_at) | (slot_rows[1:2] - start == row_at)
        return dot(jnp.where(hit, 1.0, 0.0).astype(LOW), cotangent[...]).astype(LOW)

    def dispatch(k, carry):
        d = (k + wide // 2 - 1) % (wide - 1) + 1
        to = (me + d) % wide
        up_send[to] = rows_for(to)
        up_copy(d, to).start()
        return carry

    if not gathered:
        for step in range(1, depth):
            spread(step)
            corner(step - 1)
            if step >= 2:
                finish(step - 2)
        lax.fori_loop(0, (wide - 1) // 2, dispatch, 0)
        corner(depth - 1)
        finish(depth - 2)
        lax.fori_loop((wide - 1) // 2, wide - 1, dispatch, 0)
        finish(depth - 1)
    else:
        lax.fori_loop(0, wide - 1, dispatch, 0)
        keeps.append(pltpu.make_async_copy(pack_refs[0], params, local.at[0]))
        keeps[-1].start()
    for i in range(PIECES):
        weight_piece(i)
    bias_t[...] = jnp.where(
        (column_of(segments) == segments) & ((valid_col > 0.5) | (keys_at == rows_at)), 0.0, MASKED
    )
    up_send[me] = rows_for(me)
    body = pl.ds(0, used)
    keep_up = pltpu.make_async_copy(up_send.at[me, body], ups.at[me, body], local.at[2])
    keep_up.start()
    for copy in by_core.values():
        copy.wait_recv()
    for copy in keeps:
        copy.wait()


    def columns(at):
        return params[:, at] if gathered else params[:, :, at].reshape(model, PAIR)

    small = columns(pl.ds(4 * model, PAIR))
    vecs[...] = jnp.transpose(small.astype(F32))[experts : experts + 8]
    normed[...] = (total[...] * vecs[0:1] + vecs[1:2]).astype(LOW)

    def attend(pair, carry):
        at = lambda which: pl.ds(pl.multiple_of(which * model + pair * PAIR, PAIR), PAIR)
        here = at(0)
        source = normed[...]
        queries = (dot(source, columns(at(0))) + vecs[2:3, here]).astype(LOW) * LOW(HEAD**-0.5)
        keys = dot(source, columns(at(1))).astype(LOW)
        values = (dot(source, columns(at(2))) + vecs[3:4, here]).astype(LOW)
        q_out[:, here] = queries
        k_out[:, here] = keys
        v_out[:, here] = values
        mixed = None
        for part in range(2):
            side = (lanes < HEAD) if part == 0 else (lanes >= HEAD)
            own_keys = jnp.where(side, keys, LOW(0))
            own_values = jnp.where(side, values, LOW(0))
            scores = dot_nt(queries, own_keys) + bias[...]
            peak = jnp.max(scores, axis=1, keepdims=True)
            raised = jnp.exp(scores - peak)
            row_total = jnp.sum(raised, axis=1, keepdims=True)
            attn = (raised * (1.0 / row_total)).astype(LOW)
            piece = dot(attn, own_values)
            mixed = piece if mixed is None else mixed + piece
            lse[...] = jnp.where(lanes == 2 * pair + part, peak + jnp.log(row_total), lse[...])
        mixed = mixed.astype(LOW)
        attended[:, here] = mixed
        return carry

    lax.fori_loop(0, model // PAIR, attend, 0)

    def project(pair, carry):
        here = pl.ds(pl.multiple_of(pair * PAIR, PAIR), PAIR)
        there = pl.ds(pl.multiple_of(3 * model + pair * PAIR, PAIR), PAIR)
        total[:, here] = dot(attended[...], columns(there))
        return carry

    lax.fori_loop(0, model // PAIR, project, 0)
    lse_rows[...] = jnp.transpose(lse[...])
    normed_t[...] = jnp.transpose(normed[...])
    attended_t[...] = jnp.transpose(attended[...])
    mid = tokens[...].astype(F32) + (total[...] + vecs[4:5])
    middle[...] = mid
    xhat, _ = norm_parts(mid)
    low = (xhat * vecs[5:6] + vecs[6:7]).astype(LOW)
    moe_low[...] = low
    moe_low_t[...] = jnp.transpose(low)
    logits = jnp.where(lanes < experts, dot(low, columns(pl.ds(4 * model, PAIR))), -jnp.inf)
    raised = jnp.exp(logits - jnp.max(logits, axis=1, keepdims=True))
    probs = raised / jnp.sum(raised, axis=1, keepdims=True)
    probs_out[...] = probs
    gate_a = jnp.sum(jnp.where(lanes == first_at, probs, 0.0), axis=1, keepdims=True)
    gate_b = jnp.sum(jnp.where(lanes == second_at, probs, 0.0), axis=1, keepdims=True)
    gates_out[...] = jnp.where(lanes == 0, gate_a, gate_b)

    def settle(k, carry):
        d = k + 1
        up_copy(d, (me + d) % wide).wait_send()
        up_copy(d, (me - d + wide) % wide).wait_recv()
        return carry

    lax.fori_loop(0, wide - 1, settle, 0)
    keep_up.wait()
    for copy in w_copies + b_copies + fills:
        copy.wait()
    for group in (first, by_x, by_y, half_a, half_b, by_core):
        for copy in group.values():
            copy.wait_send()


def front_stage(
    dims, experts, capacity, stride, gathered, pack, tokens, segment_ids, patch_valid, routes, priority,
    cotangent, w_out, in_bias,
):
    depth, across, rows, cores = dims
    wide, narrow = depth * across, rows * cores
    count, model = tokens.shape
    used = -(-capacity // 8) * 8
    any_, vmem = pl.BlockSpec(memory_space=pl.ANY), pl.BlockSpec(memory_space=pltpu.VMEM)
    low = lambda *shape: jax.ShapeDtypeStruct(shape, LOW)
    f32 = lambda *shape: jax.ShapeDtypeStruct(shape, F32)
    i32 = lambda *shape: jax.ShapeDtypeStruct(shape, jnp.int32)
    width = 4 * model + PAIR
    height = model if gathered else pack[0].shape[0]
    full = (height, width) if gathered else (wide * narrow, height, width)
    packed = 1 if gathered else height
    corners = depth * (across - 1) * (rows - 1)
    sems = []
    for size in (
        depth - 1, depth * (across - 1), depth * (rows - 1), corners, corners, depth * across * rows,
        wide, (rows - 1) * PIECES, narrow,
    ):
        sems += [pltpu.SemaphoreType.DMA((size,))] * 2
    outs = pl.pallas_call(
        functools.partial(front_kernel, dims, experts, capacity, gathered, len(pack)),
        out_shape=(
            low(*full), low(model, count), low(count, model), low(count, model), low(count, model),
            low(model, count), f32(PAIR, count), f32(count, model), low(count, model), low(model, count),
            f32(count, PAIR), f32(count, PAIR), f32(8, model), f32(count, count), i32(count, PAIR), i32(8, count),
            f32(narrow, 1, in_bias.shape[1]), low(wide, stride, model), *[low(*w_out.shape)] * (rows - 1),
        ),
        in_specs=([any_] if gathered else [any_, any_, vmem, vmem]) + [vmem] * 6 + [any_, vmem],
        out_specs=[vmem] * 17 + [any_] * rows,
        scratch_shapes=[
            pltpu.VMEM((count, model), LOW),
            pltpu.VMEM((count, model), LOW),
            pltpu.VMEM((count, model), F32),
            pltpu.VMEM((count, count), F32),
            pltpu.VMEM((count, PAIR), F32),
            pltpu.VMEM((wide, stride, model), LOW),
            pltpu.VMEM((1, in_bias.shape[1]), F32),
            pltpu.VMEM((packed, width), LOW),
            pltpu.VMEM((PAIR, PAIR), F32),
            pltpu.VMEM((max(stride - used, 8), model), LOW),
            *sems,
            pltpu.SemaphoreType.DMA((5,)),
            pltpu.SemaphoreType.DMA((wide,)),
        ],
        compiler_params=pltpu.CompilerParams(
            collective_id=0, has_side_effects=True, vmem_limit_bytes=VMEM_LIMIT
        ),
        cost_estimate=pl.CostEstimate(flops=7 * 10**9, bytes_accessed=20 * 10**6, transcendentals=4 * 10**6),
        name="front_stage",
    )(*pack, tokens, segment_ids, patch_valid, jnp.transpose(routes), priority, cotangent, w_out, in_bias)
    params = outs[0] if gathered else outs[0].reshape(wide * narrow * height, width)
    return params, outs[1:14], outs[14:18], outs[18:]


def norm_back(grad, gain, xhat, scale):
    scaled = grad * gain
    mean_a = jnp.mean(scaled, axis=-1, keepdims=True)
    mean_b = jnp.mean(scaled * xhat, axis=-1, keepdims=True)
    return scale * (scaled - mean_a - xhat * mean_b)


def back_kernel(dims, used, experts, gathered, *rest):
    depth, across, rows, cores = dims
    wide, narrow = depth * across, rows * cores
    (
        tokens, normed_t, queries, keys, values, attended_t, lse_rows, middle, _, moe_low_t, probs, gates, vecs, bias,
        weights, slots, token_rows, gate_slots, cotangent, y_rows,
    ) = rest[:20]
    side_grad = rest[20 : 19 + rows]
    rest = rest[19 + rows :]
    if gathered:
        block_out, tokens_grad, grad_here, group = rest[:4]
        rest = rest[4:]
    else:
        block_out, tokens_grad, grad_here, out_qkv, out_proj, out_router, *out_vecs = rest[:13]
        group, n1, n2, n3, n4 = rest[13:18]
        rest = rest[18:]
    branch, middle_grad, total, sums, router, parts, y_here = rest[:7]
    s_y, q_y, s_g, q_g, local = rest[7:12]
    z, x, y, c = place_of(dims)
    me, n = z * across + x, y * cores + c
    count, model = tokens.shape
    stride = y_here.shape[1]
    pairs = model // PAIR
    per = 3 * PAIR
    n_proj = model // per
    small_at = n_proj + pairs
    lanes = lax.broadcasted_iota(jnp.int32, (count, PAIR), 1)

    def remote(src, dst, ssem, rsem, to):
        return pltpu.make_async_remote_copy(
            src_ref=src, dst_ref=dst, send_sem=ssem, recv_sem=rsem, device_id=to, device_id_type=MESH
        )

    peers = [((me + d) % wide, n) for d in range(1, wide)]
    peers += [device_at(dims, z, x, (y + d) % rows, c) for d in range(1, rows)]
    peers += [device_at(dims, z, x, y, 1 - c)]
    body = pl.ds(0, used)
    if used < stride:
        y_here[:, used:stride] = jnp.zeros((wide, stride - used, model), LOW)
    greet(peers)

    def y_copy(d, to):
        return remote(y_rows.at[to, body], y_here.at[me, body], s_y.at[d], q_y.at[d], (to, n))

    def give(k, carry):
        d = (k + wide // 2 - 1) % (wide - 1) + 1
        y_copy(d, (me + d) % wide).start()
        return carry

    lax.fori_loop(0, wide - 1 - pairs, give, 0)
    keep_y = pltpu.make_async_copy(y_rows.at[me, body], y_here.at[me, body], local.at[0])
    keep_y.start()
    piece = grad_here.shape[2] // PIECES

    def g_copies(i):
        copies = []
        for dy in range(1, rows):
            at = (dy - 1) * PIECES + i
            part = pl.ds(i * piece, piece)
            to = device_at(dims, z, x, (y + dy) % rows, c)
            copies.append(remote(side_grad[dy - 1].at[:, part], grad_here.at[dy - 1, :, part], s_g.at[at], q_g.at[at], to))
        return copies

    def give_grad(i):
        for copy in g_copies(i):
            copy.start()

    for i in range(PIECES - pairs):
        give_grad(i)

    if not gathered:
        s1, q1, s2, q2, s3, q3, s4, q4 = rest[12:20]
        height = group.shape[-2]

    def put(g, third, value):
        at = pl.ds(third * PAIR, PAIR)
        value = value.astype(LOW)
        if gathered:
            group[g, :, at] = value
        else:
            group[g, :, :, :, :, :, at] = value.reshape(depth, across, rows, cores, height, PAIR)

    def span(g):
        return pl.ds(0, PAIR) if isinstance(g, int) and g == small_at else pl.ds(0, per)

    def hop_core(g):
        return remote(
            group.at[g, :, :, :, 1 - c, :, span(g)], n1.at[g, :, :, :, :, span(g)], s1.at[g], q1.at[g],
            device_at(dims, z, x, y, 1 - c),
        )

    def hop_x(g, dx):
        at = g * (across - 1) + dx - 1
        return remote(
            n1.at[g, :, (x + dx) % across, :, :, span(g)], n2.at[at, :, :, :, span(g)],
            s2.at[at], q2.at[at], device_at(dims, z, (x + dx) % across, y, c),
        )

    def hop_y(g, dy):
        at = g * (rows - 1) + dy - 1
        return remote(
            n2.at[g * (across - 1), :, (y + dy) % rows, :, span(g)], n3.at[at, :, :, span(g)],
            s3.at[at], q3.at[at], device_at(dims, z, x, (y + dy) % rows, c),
        )

    def hop_z(g, dz):
        at = g * (depth - 1) + dz - 1
        return remote(
            n3.at[g * (rows - 1), (z + dz) % depth, :, span(g)], n4.at[at, :, span(g)],
            s4.at[at], q4.at[at], device_at(dims, (z + dz) % depth, x, y, c),
        )

    def start(g):
        if not gathered:
            hop_core(g).start()

    def begin(g):
        if gathered:
            return
        hop_core(g).wait_recv()
        w = span(g)
        n1[g, :, :, :, :, w] = (
            group[g, :, :, :, c, :, w].astype(F32) + n1[g, :, :, :, :, w].astype(F32)
        ).astype(LOW)
        for dx in range(1, across):
            hop_x(g, dx).start()

    def middle_of(g):
        if gathered:
            return
        w = span(g)
        at = g * (across - 1)
        acc = n1[g, :, x, :, :, w].astype(F32)
        for dx in range(1, across):
            hop_x(g, dx).wait_recv()
            acc = acc + n2[at + dx - 1, :, :, :, w].astype(F32)
        n2[at, :, :, :, w] = acc.astype(LOW)
        for dy in range(1, rows):
            hop_y(g, dy).start()

    def end(g):
        if gathered:
            return
        w = span(g)
        at = g * (rows - 1)
        for dy in range(1, rows):
            hop_y(g, dy).wait_recv()
        acc = n2[g * (across - 1), :, y, :, w].astype(F32)
        for dy in range(1, rows):
            acc = acc + n3[at + dy - 1, :, :, w].astype(F32)
        n3[at, :, :, w] = acc.astype(LOW)
        for dz in range(1, depth):
            hop_z(g, dz).start()

    def last(g):
        w = span(g)
        acc = n3[g * (rows - 1), z, :, w].astype(F32)
        for dz in range(1, depth):
            hop_z(g, dz).wait_recv()
            acc = acc + n4[g * (depth - 1) + dz - 1, :, w].astype(F32)
        return acc

    total[...] = jnp.zeros_like(total)
    sums[...] = jnp.zeros_like(sums)
    slot_a, slot_b = slots[:, 0:1], slots[:, 1:2]
    slot_at = lax.broadcasted_iota(jnp.int32, (count, wide * stride), 1)
    third = PAIR // 4
    lane_at = lax.broadcasted_iota(jnp.int32, (stride, PAIR), 1)

    def split(w, carry):
        value = column_of(gate_slots[w])[0:stride]
        high = value.astype(LOW).astype(F32)
        mid = (value - high).astype(LOW).astype(F32)
        low = value - high - mid
        row = jnp.where(lane_at == w, high, 0.0) + jnp.where(lane_at == third + w, mid, 0.0)
        parts[w] = (row + jnp.where(lane_at == 2 * third + w, low, 0.0)).astype(LOW)
        return carry

    lax.fori_loop(0, wide, split, 0)
    picks = jnp.where((slot_at == slot_a) | (slot_at == slot_b), 1.0, 0.0).astype(LOW)
    picked = dot(picks, parts[...].reshape(wide * stride, PAIR))
    prob_grad = picked + pltpu.roll(picked, PAIR - third, 1) + pltpu.roll(picked, PAIR - 2 * third, 1)
    own = probs[...]
    prob_grad = jnp.where(lanes < experts, prob_grad, 0.0)
    logit_grad = (own * (prob_grad - jnp.sum(prob_grad * own, axis=1, keepdims=True))).astype(LOW)
    router[...] = dot(moe_low_t[...], logit_grad)
    moe_grad = dot(picks, token_rows[...].reshape(wide * stride, model)) + dot_nt(
        logit_grad, weights[:, 4 * model : 4 * model + PAIR]
    )
    xhat, scale = norm_parts(middle[...])
    sums[5:6] = jnp.sum(moe_grad * xhat, axis=0, keepdims=True)
    sums[6:7] = jnp.sum(moe_grad, axis=0, keepdims=True)
    mid = cotangent[...].astype(F32) + norm_back(moe_grad, vecs[5:6], xhat, scale)
    middle_grad[...] = mid
    branch[...] = mid.astype(LOW)
    sums[4:5] = jnp.sum(branch[...].astype(F32), axis=0, keepdims=True)
    for g in range(n_proj):
        for third_at in range(3):
            at = (g * 3 + third_at) * PAIR
            put(g, third_at, dot(attended_t[...], branch[:, at : at + PAIR]))
        start(g)
    begin(0)

    sides = lax.broadcasted_iota(jnp.int32, (PAIR, count), 0)

    def attend(pair, carry):
        at = lambda which: pl.ds(pl.multiple_of(which * model + pair * PAIR, PAIR), PAIR)
        here = at(0)
        grad_mixed = dot_nt(branch[...], weights[here, 3 * model : 4 * model]).astype(LOW)
        q_pair, k_pair, v_pair = queries[:, here], keys[:, here], values[:, here]
        k_turned = jnp.transpose(k_pair)
        q_grad_t, k_grad, v_grad = None, None, None
        for part in range(2):
            side = (lanes < HEAD) if part == 0 else (lanes >= HEAD)
            side_t = (sides < HEAD) if part == 0 else (sides >= HEAD)
            own_keys = jnp.where(side, k_pair, LOW(0))
            own_values = jnp.where(side, v_pair, LOW(0))
            own_queries = jnp.where(side, q_pair, LOW(0))
            own_grads = jnp.where(side, grad_mixed, LOW(0))
            own_turned = jnp.where(side_t, k_turned, LOW(0))
            scores = dot_nt(own_keys, q_pair) + bias[...]
            attn = jnp.exp(scores - lse_rows[pl.ds(2 * pair + part, 1), :])
            attn_grad = dot_nt(own_values, grad_mixed)
            mean = jnp.sum(attn * attn_grad, axis=0, keepdims=True)
            score_grad = (attn * (attn_grad - mean)).astype(LOW)
            v_part = dot(attn.astype(LOW), own_grads)
            k_part = dot(score_grad, own_queries)
            q_part = dot(own_turned, score_grad)
            if part == 0:
                q_grad_t, k_grad, v_grad = q_part, k_part, v_part
            else:
                q_grad_t, k_grad, v_grad = q_grad_t + q_part, k_grad + k_part, v_grad + v_part
        q_grad = (jnp.transpose(q_grad_t) * HEAD**-0.5).astype(LOW)
        k_grad = k_grad.astype(LOW)
        v_grad = v_grad.astype(LOW)
        sums[2:3, here] = jnp.sum(q_grad.astype(F32), axis=0, keepdims=True)
        sums[3:4, here] = jnp.sum(v_grad.astype(F32), axis=0, keepdims=True)
        source = normed_t[...]
        g = pair + n_proj
        for which, piece in enumerate((q_grad, k_grad, v_grad)):
            put(g, which, dot(source, piece))
        start(g)
        lax.fori_loop(wide - 1 - pairs + pair, wide - pairs + pair, give, 0)
        give_grad(PIECES - pairs + pair)
        total[...] += (
            dot_nt(q_grad, weights[:, at(0)]) + dot_nt(k_grad, weights[:, at(1)]) + dot_nt(v_grad, weights[:, at(2)])
        )
        if not gathered:
            begin(g - 1)

            @pl.when(g >= 3)
            def _():
                middle_of(g - 3)

            @pl.when(g >= 4)
            def _():
                end(g - 4)

        return carry

    lax.fori_loop(0, pairs, attend, 0)
    grad = total[...]
    xhat, scale = norm_parts(tokens[...].astype(F32))
    sums[0:1] = jnp.sum(grad * xhat, axis=0, keepdims=True)
    sums[1:2] = jnp.sum(grad, axis=0, keepdims=True)
    stacked = jnp.concatenate([sums[...], jnp.zeros((PAIR - 8, model), F32)], axis=0)
    turned = pltpu.roll(jnp.transpose(stacked), experts, 1)
    wide_lanes = lax.broadcasted_iota(jnp.int32, (model, PAIR), 1)
    put(small_at, 0, jnp.where(wide_lanes < experts, router[...], turned))
    start(small_at)
    begin(small_at - 1)
    middle_of(small_at - 3)
    end(small_at - 4)
    tokens_grad[...] = (middle_grad[...] + norm_back(grad, vecs[0:1], xhat, scale)).astype(LOW)
    begin(small_at)
    middle_of(small_at - 2)
    end(small_at - 3)
    middle_of(small_at - 1)
    middle_of(small_at)
    end(small_at - 2)
    end(small_at - 1)
    end(small_at)

    def taken(k, carry):
        d = k + 1
        y_copy(d, (me + d) % wide).wait_send()
        y_copy(d, (me - d + wide) % wide).wait_recv()
        return carry

    lax.fori_loop(0, wide - 1, taken, 0)
    keep_y.wait()
    returned = y_here[...].reshape(wide * stride, model)
    mixed = gates[:, 0:1] * dot(jnp.where(slot_at == slot_a, 1.0, 0.0).astype(LOW), returned)
    mixed += gates[:, 1:2] * dot(jnp.where(slot_at == slot_b, 1.0, 0.0).astype(LOW), returned)
    block_out[...] = (middle[...] + mixed).astype(LOW)
    if not gathered:
        for g in range(n_proj):
            out_proj[:, g * per : (g + 1) * per] = last(g)
        for pair in range(pairs):
            summed = last(n_proj + pair)
            for which in range(3):
                at = which * model + pair * PAIR
                out_qkv[:, at : at + PAIR] = summed[:, which * PAIR : (which + 1) * PAIR]
        summed = last(small_at)
        out_router[...] = summed[:, 0:experts]
        square = jnp.concatenate([summed, jnp.zeros((PAIR - height, PAIR), F32)], axis=0)
        turned = jnp.transpose(square)
        for i, ref in enumerate(out_vecs):
            ref[...] = turned[experts + i : experts + i + 1, 0:height]
        for g in range(small_at + 1):
            hop_core(g).wait_send()
            for dx in range(1, across):
                hop_x(g, dx).wait_send()
            for dy in range(1, rows):
                hop_y(g, dy).wait_send()
            for dz in range(1, depth):
                hop_z(g, dz).wait_send()
    for i in range(PIECES):
        for copy in g_copies(i):
            copy.wait()


def back_stage(
    dims, used, experts, gathered, tokens, saved, params, slots, token_rows, gate_slots, cotangent, y_rows, side_grads,
):
    depth, across, rows, cores = dims
    wide, narrow = depth * across, rows * cores
    count, model = tokens.shape
    stride = y_rows.shape[1]
    per = 3 * PAIR
    groups = model // per + model // PAIR + 1
    height = model // (wide * narrow)
    any_, vmem = pl.BlockSpec(memory_space=pl.ANY), pl.BlockSpec(memory_space=pltpu.VMEM)
    low = lambda *shape: jax.ShapeDtypeStruct(shape, LOW)
    f32 = lambda *shape: jax.ShapeDtypeStruct(shape, F32)
    sem = lambda size: [pltpu.SemaphoreType.DMA((size,))] * 2
    outs = [low(count, model), low(count, model), low(rows - 1, *side_grads[0].shape)]
    buffers, sems = [], []
    if gathered:
        outs.append(low(groups, model, per))
    else:
        outs += [f32(height, 3 * model), f32(height, model), f32(height, experts), *[f32(1, height)] * 7]
        buffers = [
            pltpu.VMEM((groups, depth, across, rows, cores, height, per), LOW),
            pltpu.VMEM((groups, depth, across, rows, height, per), LOW),
            pltpu.VMEM((groups * (across - 1), depth, rows, height, per), LOW),
            pltpu.VMEM((groups * (rows - 1), depth, height, per), LOW),
            pltpu.VMEM((groups * (depth - 1), height, per), LOW),
        ]
        sems = [
            *sem(groups), *sem(groups * (across - 1)), *sem(groups * (rows - 1)), *sem(groups * (depth - 1)),
        ]
    return pl.pallas_call(
        functools.partial(back_kernel, dims, used, experts, gathered),
        out_shape=tuple(outs),
        in_specs=[vmem] * 8 + [any_] + [vmem] * 10 + [any_] * rows,
        out_specs=[vmem] * 2 + [any_] + [vmem] * (len(outs) - 3),
        scratch_shapes=[
            *buffers,
            pltpu.VMEM((count, model), LOW),
            pltpu.VMEM((count, model), F32),
            pltpu.VMEM((count, model), F32),
            pltpu.VMEM((8, model), F32),
            pltpu.VMEM((model, PAIR), F32),
            pltpu.VMEM((wide, stride, PAIR), LOW),
            pltpu.VMEM((wide, stride, model), LOW),
            *sem(wide), *sem((rows - 1) * PIECES),
            pltpu.SemaphoreType.DMA((1,)),
            *sems,
        ],
        compiler_params=pltpu.CompilerParams(
            collective_id=1, has_side_effects=True, vmem_limit_bytes=60 * 1024 * 1024
        ),
        cost_estimate=pl.CostEstimate(flops=16 * 10**9, bytes_accessed=40 * 10**6, transcendentals=4 * 10**6),
        name="back_stage",
    )(
        tokens, *saved, params, slots, token_rows, gate_slots, cotangent, y_rows, *side_grads
    )


def tail_kernel(count, *refs):
    inputs, own, others = refs[:count], refs[count], refs[count + 1]
    outputs, grad_in, grad_out = refs[count + 2 : 2 * count + 2], refs[2 * count + 2], refs[2 * count + 3]
    terms, first, second, sems, loads, brings = refs[2 * count + 4 : 2 * count + 10]
    held = refs[2 * count + 10 :]
    rows = terms.shape[0]
    arrivals = [
        pltpu.make_async_copy(own if i == 0 else others.at[i - 1], terms.at[i], loads.at[i]) for i in range(rows)
    ]
    bring = [pltpu.make_async_copy(src, dst, brings.at[i]) for i, (src, dst) in enumerate(zip(inputs, held))]
    copies = [pltpu.make_async_copy(src, dst, sems.at[i]) for i, (src, dst) in enumerate(zip(held, outputs))]
    for copy in bring + arrivals:
        copy.start()
    for into, out in zip(bring, copies):
        into.wait()
        out.start()
    for copy in arrivals:
        copy.wait()

    def total(which):
        acc = terms[0, which].astype(F32)
        for i in range(1, rows):
            acc = acc + terms[i, which].astype(F32)
        return acc

    first[0] = total(0)
    copies.append(pltpu.make_async_copy(first, grad_in, sems.at[count]))
    copies[-1].start()
    second[0] = jnp.transpose(total(1))
    copies.append(pltpu.make_async_copy(second, grad_out, sems.at[count + 1]))
    copies[-1].start()
    for copy in copies:
        copy.wait()


def tail_stage(arrays, own, others):
    any_ = pl.BlockSpec(memory_space=pl.ANY)
    _, model, ff = own.shape
    count = len(arrays)
    shapes = [jax.ShapeDtypeStruct(a.shape, a.dtype) for a in arrays]
    shapes += [jax.ShapeDtypeStruct((1, model, ff), F32), jax.ShapeDtypeStruct((1, ff, model), F32)]
    rows = others.shape[0] + 1
    return pl.pallas_call(
        functools.partial(tail_kernel, count),
        out_shape=tuple(shapes),
        in_specs=[any_] * (count + 2),
        out_specs=[any_] * (count + 2),
        scratch_shapes=[
            pltpu.VMEM((rows, 2, model, ff), LOW),
            pltpu.VMEM((1, model, ff), F32),
            pltpu.VMEM((1, ff, model), F32),
            pltpu.SemaphoreType.DMA((count + 2,)),
            pltpu.SemaphoreType.DMA((rows,)),
            pltpu.SemaphoreType.DMA((count,)),
            *[pltpu.VMEM(a.shape, a.dtype) for a in arrays],
        ],
        compiler_params=pltpu.CompilerParams(vmem_limit_bytes=58 * 1024 * 1024),
        name="results",
    )(*arrays, own, others)


def gelu_and_slope(v):
    root = 0.7978845608028654
    cubic = 0.044715
    square = v * v
    half = 0.5 * jnp.tanh(v * (root + (root * cubic) * square)) + 0.5
    value = v * half
    slope = half + value * ((1.0 - half) * (2.0 * root + (6.0 * root * cubic) * square))
    return value, slope


def moe_kernel(
    dims, used, moe_low, slot_rows, slot_cols, gates, ups, b_in, b_out, w_in, w_out, *rest
):
    depth, across, rows, cores = dims
    wide = depth * across
    narrow = rows * cores
    side_out = rest[: rows - 1]
    rest = rest[rows - 1 :]
    token_rows, gate_slots, y_out, in_bias_grad, out_bias_grad = rest[:5]
    own_grad = rest[5]
    side_grad = rest[6 : 5 + rows]
    (
        full_in, full_out, x_send, x_here, g_send, g_here, dx_send, h_send, hidden, pre_grad, weighted,
        x_turned, w_turned, grad_send, grad_here, extra, extra_here, extra_y, blank,
        local, blanks, s_wy, r_wy, s_ey, r_ey, s_in, r_in, s_out, r_out, s_x, r_x, s_g, r_g, s_dx, r_dx, s_h, r_h, s_w, r_w, s_e, r_e,
    ) = rest[5 + rows :]
    z, x, y, c = place_of(dims)
    me, n = z * across + x, y * cores + c
    count, model = moe_low.shape
    capacity = x_send.shape[1]
    gate_width = g_send.shape[2]
    ff = full_in.shape[2]
    other = device_at(dims, z, x, y, 1 - c)

    def remote(src, dst, ssem, rsem, to):
        return pltpu.make_async_remote_copy(
            src_ref=src, dst_ref=dst, send_sem=ssem, recv_sem=rsem, device_id=to, device_id_type=MESH
        )

    along_y = [device_at(dims, z, x, (y + i) % rows, c) for i in range(1, rows)]
    body = pl.ds(0, used)
    if used < capacity:
        x_here[:, used:capacity] = jnp.zeros((wide, capacity - used, model), LOW)
        blank[...] = jnp.zeros_like(blank)
    greet([((me + d) % wide, n) for d in range(1, wide)] + [other] + along_y)
    fills = []
    if used < capacity:
        for w in range(wide):
            fills.append(pltpu.make_async_copy(blank, token_rows.at[w, pl.ds(used, capacity - used)], blanks.at[w]))

    held = [((y - i) % rows) * cores + c for i in range(rows)]
    from_y, in_passes, out_loads, out_passes = [], [], [], []
    for i, h in enumerate(held):
        src_out = w_out.at[0] if i == 0 else side_out[i - 1].at[0]
        out_loads.append(pltpu.make_async_copy(src_out, full_out.at[h], local.at[i]))
        out_passes.append(remote(src_out, full_out.at[h], s_out.at[i], r_out.at[i], other))
        if i:
            from_y.append(remote(w_in.at[0], full_in.at[n], s_wy.at[i - 1], r_wy.at[i - 1], along_y[i - 1]))
        src_in = w_in.at[0] if i == 0 else full_in.at[h]
        in_passes.append(remote(src_in, full_in.at[h], s_in.at[i], r_in.at[i], other))
    in_load = pltpu.make_async_copy(w_in.at[0], full_in.at[n], local.at[rows])
    for copy in from_y + out_loads + out_passes:
        copy.start()

    slot_a, slot_b = slot_cols[:, 0:1], slot_cols[:, 1:2]
    gate_a, gate_b = gates[:, 0:1], gates[:, 1:2]
    row_at = lax.broadcasted_iota(jnp.int32, (capacity, count), 0)
    lane_at = lax.broadcasted_iota(jnp.int32, (count, gate_width), 1)
    source = moe_low[...]

    def rows_for(expert):
        first = expert * capacity
        hit = (slot_rows[0:1] - first == row_at) | (slot_rows[1:2] - first == row_at)
        picked = dot(jnp.where(hit, 1.0, 0.0).astype(LOW), source).astype(LOW)
        inside = lane_at < capacity
        hit_a = (slot_a - first == lane_at) & inside
        hit_b = (slot_b - first == lane_at) & inside
        gate = jnp.where(hit_a, gate_a, 0.0) + jnp.where(hit_b, gate_b, 0.0)
        return picked, jnp.sum(gate, axis=0, keepdims=True)

    def x_copy(d, to):
        return remote(x_send.at[to, body], x_here.at[me, body], s_x.at[d], r_x.at[d], (to, n))

    def g_copy(d, to):
        return remote(g_send.at[to], g_here.at[me], s_g.at[d], r_g.at[d], (to, n))

    def dx_copy(d, to):
        return remote(dx_send.at[to, body], token_rows.at[me, body], s_dx.at[d], r_dx.at[d], (to, n))

    def h_copy(d, to):
        return remote(h_send.at[to], gate_slots.at[me], s_h.at[d], r_h.at[d], (to, n))

    def dispatch(k, carry):
        d = (k + wide // 2 - 1) % (wide - 1) + 1
        to = (me + d) % wide
        picked, gate = rows_for(to)
        x_send[to] = picked
        g_send[to] = gate
        x_copy(d, to).start()
        g_copy(d, to).start()
        return carry

    lax.fori_loop(0, wide - 1, dispatch, 0)
    in_load.start()
    in_passes[0].start()
    for copy in fills:
        copy.start()
    picked, gate = rows_for(me)
    x_here[me] = picked
    g_here[me] = gate
    extra[...] = jnp.zeros_like(extra)
    out_bias = b_out[...].astype(F32)
    for copy in out_loads:
        copy.wait()

    def backs_of(places):
        def backs(k, carry):
            two = pl.ds(2 * k, 2)
            up = ups[two].reshape(2 * capacity, model)
            for h in places:
                lanes = pl.ds(pl.multiple_of(h * ff, PAIR), ff)
                pre_grad[two, :, lanes] = dot_nt(up, full_out[h]).astype(LOW).reshape(2, capacity, ff)
            return carry

        return backs

    lax.fori_loop(0, wide // 2, backs_of([i * cores + c for i in range(rows)]), 0)
    for copy in out_passes:
        copy.wait_recv()
    lax.fori_loop(0, wide // 2, backs_of([i * cores + 1 - c for i in range(rows)]), 0)
    for i in range(1, rows):
        from_y[i - 1].wait_recv()
        in_passes[i].start()
    in_load.wait()
    for copy in in_passes:
        copy.wait_recv()

    def expert(src):
        own = x_here[src]
        up = ups[src]
        gate = jnp.transpose(jnp.broadcast_to(g_here[src], (PAIR, gate_width)))[:capacity, 0:1]
        weigh = (gate * up.astype(F32)).astype(LOW)
        weighted[src] = weigh
        back_total = jnp.sum(up.astype(F32) * out_bias, axis=1, keepdims=True)
        dx = None
        for h in range(narrow):
            pre = dot(own, full_in[h]) + b_in[h]
            back = pre_grad[src, :, h * ff : (h + 1) * ff].astype(F32)
            value, slope = gelu_and_slope(pre)
            low = value.astype(LOW)
            hidden[src, :, h * ff : (h + 1) * ff] = low
            back_total += jnp.sum(value * back, axis=1, keepdims=True)
            wide_grad = slope * (gate * back)
            grad = wide_grad.astype(LOW)
            pre_grad[src, :, h * ff : (h + 1) * ff] = grad
            extra[h, 0:1, :ff] += jnp.sum(wide_grad, axis=0, keepdims=True)
            part = dot_nt(grad, full_in[h])
            dx = part if dx is None else dx + part
        dx_send[src] = dx.astype(LOW)
        spread = jnp.broadcast_to(back_total, (capacity, PAIR))
        spread = jnp.concatenate([spread, jnp.zeros((gate_width - capacity, PAIR), F32)], axis=0)
        h_send[src] = jnp.transpose(spread)[0:1]

    expert(me)
    keep_rows = pltpu.make_async_copy(dx_send.at[me, body], token_rows.at[me, body], local.at[2 * rows])
    keep_gate = pltpu.make_async_copy(h_send.at[me], gate_slots.at[me], local.at[2 * rows + 1])
    keep_rows.start()
    keep_gate.start()

    def serve(k, carry):
        d = jnp.where(k % 2 == 0, k // 2 + 1, wide - (k + 1) // 2)
        src = (me - d + wide) % wide
        x_copy(d, src).wait_recv()
        g_copy(d, src).wait_recv()
        expert(src)
        dx_copy(d, src).start()
        h_copy(d, src).start()
        return carry

    lax.fori_loop(0, wide - 1, serve, 0)

    all_rows = wide * capacity
    x_turned[...] = jnp.transpose(x_here[...].reshape(all_rows, model))
    w_turned[...] = jnp.transpose(weighted[...].reshape(all_rows, model))
    bias_grad = jnp.sum(weighted[...].reshape(all_rows, model).astype(F32), axis=0, keepdims=True)
    for h in range(narrow):
        extra[h, 1:2] = bias_grad

    def grad_of(h):
        lanes = pl.ds(pl.multiple_of(h * ff, PAIR), ff)
        grad_in = dot(x_turned[...], pre_grad[:, :, lanes].reshape(all_rows, ff))
        grad_out = dot(w_turned[...], hidden[:, :, lanes].reshape(all_rows, ff))
        return grad_in, grad_out

    order = [*range(1, rows), 0]
    swaps, by_y, keep_grads = {}, {}, []
    for i in order:
        at = (y + i) % rows
        h = at * cores + 1 - c
        grad_in, grad_out = grad_of(h)
        grad_send[i, 0] = grad_in.astype(LOW)
        grad_send[i, 1] = grad_out.astype(LOW)
        swaps[i] = (
            remote(grad_send.at[i], grad_here.at[i], s_w.at[i], r_w.at[i], other),
            remote(extra.at[h], extra_here.at[i], s_e.at[i], r_e.at[i], other),
        )
        for copy in swaps[i]:
            copy.start()
        h = at * cores + c
        grad_in, grad_out = grad_of(h)
        for copy in swaps[i]:
            copy.wait_recv()
        grad_here[i, 0] = (grad_in + grad_here[i, 0].astype(F32)).astype(LOW)
        grad_here[i, 1] = (grad_out + grad_here[i, 1].astype(F32)).astype(LOW)
        extra_here[i] = extra_here[i] + extra[h]
        if i:
            by_y[i] = remote(
                extra_here.at[i], extra_y.at[i - 1], s_ey.at[i - 1], r_ey.at[i - 1], along_y[i - 1]
            )
            by_y[i].start()
        target = own_grad if i == 0 else side_grad[i - 1]
        keep_grads.append(pltpu.make_async_copy(grad_here.at[i], target, local.at[2 * rows + 3 + i]))
        keep_grads[-1].start()

    def outputs(src, carry):
        total = None
        for h in range(narrow):
            part = dot(hidden[src, :, h * ff : (h + 1) * ff], full_out[h])
            total = part if total is None else total + part
        x_send[src] = (total + out_bias).astype(LOW)
        return carry

    def sent(k, carry):
        to = (me + k + 1) % wide
        x_copy(k + 1, to).wait_send()
        g_copy(k + 1, to).wait_send()
        return carry

    lax.fori_loop(0, wide - 1, sent, 0)
    lax.fori_loop(0, wide, outputs, 0)
    keep_y = pltpu.make_async_copy(x_send, y_out, local.at[2 * rows + 2])
    keep_y.start()
    bias_rows = extra_here[0]
    for i in range(1, rows):
        by_y[i].wait_recv()
        bias_rows = bias_rows + extra_y[i - 1]
    in_bias_grad[...] = bias_rows[0:1, :ff]
    out_bias_grad[...] = bias_rows[1:2]

    def finish(k, carry):
        d = k + 1
        back = (me - d + wide) % wide
        dx_copy(d, back).wait_recv()
        h_copy(d, back).wait_recv()
        dx_copy(d, back).wait_send()
        h_copy(d, back).wait_send()
        return carry

    lax.fori_loop(0, wide - 1, finish, 0)
    pairs = [copy for i in range(rows) for copy in swaps[i]] + [by_y[i] for i in range(1, rows)]
    for copy in from_y + in_passes + out_passes + pairs:
        copy.wait_send()
    for copy in fills:
        copy.wait()
    for copy in [keep_rows, keep_gate, keep_y] + keep_grads:
        copy.wait()


def moe_stage(dims, used, capacity, moe_low, slot_rows, slots, gates, ups, b_in, b_out, w_in, w_out, side_out):
    depth, across, rows, cores = dims
    wide, narrow = depth * across, rows * cores
    count, model = moe_low.shape
    ff = w_in.shape[2]
    gate_width = -(-capacity // PAIR) * PAIR
    any_, vmem = pl.BlockSpec(memory_space=pl.ANY), pl.BlockSpec(memory_space=pltpu.VMEM)
    low = lambda *shape: jax.ShapeDtypeStruct(shape, LOW)
    f32 = lambda *shape: jax.ShapeDtypeStruct(shape, F32)
    sem = lambda size: [pltpu.SemaphoreType.DMA((size,))] * 2
    outs = pl.pallas_call(
        functools.partial(moe_kernel, dims, used),
        out_shape=(
            low(wide, capacity, model), f32(wide, 1, gate_width), low(wide, capacity, model),
            f32(1, ff), f32(1, model), *[low(2, model, ff)] * rows,
        ),
        in_specs=[vmem] * 7 + [any_] * (1 + rows),
        out_specs=[any_] * 3 + [vmem] * 2 + [any_] * rows,
        scratch_shapes=[
            pltpu.VMEM((narrow, model, ff), LOW),
            pltpu.VMEM((narrow, ff, model), LOW),
            pltpu.VMEM((wide, capacity, model), LOW),
            pltpu.VMEM((wide, capacity, model), LOW),
            pltpu.VMEM((wide, 1, gate_width), F32),
            pltpu.VMEM((wide, 1, gate_width), F32),
            pltpu.VMEM((wide, capacity, model), LOW),
            pltpu.VMEM((wide, 1, gate_width), F32),
            pltpu.VMEM((wide, capacity, narrow * ff), LOW),
            pltpu.VMEM((wide, capacity, narrow * ff), LOW),
            pltpu.VMEM((wide, capacity, model), LOW),
            pltpu.VMEM((model, wide * capacity), LOW),
            pltpu.VMEM((model, wide * capacity), LOW),
            pltpu.VMEM((rows, 2, model, ff), LOW),
            pltpu.VMEM((rows, 2, model, ff), LOW),
            pltpu.VMEM((narrow, 8, model), F32),
            pltpu.VMEM((rows, 8, model), F32),
            pltpu.VMEM((rows - 1, 8, model), F32),
            pltpu.VMEM((max(capacity - used, 8), model), LOW),
            pltpu.SemaphoreType.DMA((3 * rows + 3,)),
            pltpu.SemaphoreType.DMA((wide,)),
            *sem(rows), *sem(rows), *sem(rows), *sem(rows), *sem(wide), *sem(wide), *sem(wide), *sem(wide), *sem(rows), *sem(rows),
        ],
        compiler_params=pltpu.CompilerParams(
            collective_id=2, has_side_effects=True, vmem_limit_bytes=60 * 1024 * 1024
        ),
        cost_estimate=pl.CostEstimate(flops=36 * 10**9, bytes_accessed=25 * 10**6, transcendentals=4 * 10**6),
        name="moe_stage",
    )(moe_low, slot_rows, slots, gates, ups, b_in, b_out, w_in, w_out, *side_out)
    return outs[:3], outs[3:5], outs[5:]


def per_device(
    dims,
    tokens, segment_ids, patch_valid, routes, priority, gain_attn, shift_attn, w_qkv, query_bias, value_bias,
    w_proj, proj_bias, gain_moe, shift_moe, w_router, w_in, in_bias, w_out, out_bias, cotangent,
):
    count, model = tokens.shape
    experts = w_router.shape[1]
    capacity = (210 * count + 100 * experts - 1) // (100 * experts)
    shard_rows = gain_attn.shape[0]
    vectors = jnp.stack([gain_attn, shift_attn, query_bias, value_bias, proj_bias, gain_moe, shift_moe])
    stride = -(-capacity // 16) * 16
    gathered = shard_rows % 8 != 0
    every = ("wide", "narrow")
    if gathered:
        empty = jnp.zeros((shard_rows, PAIR - 7 - experts), LOW)
        pack = jnp.concatenate([w_qkv, w_proj, w_router, jnp.transpose(vectors), empty], axis=1)
        pack = [lax.all_gather(pack, every, axis=0, tiled=True)]
    else:
        pack = [w_qkv, w_proj, jnp.transpose(w_router), vectors]
    params, saved, (slots, slot_rows, full_b_in, ups), side_out = front_stage(
        dims, experts, capacity, stride, gathered, pack, tokens, segment_ids, patch_valid, routes, priority,
        cotangent, w_out, in_bias,
    )
    moe_low, gates = saved[7], saved[10]
    used = -(-capacity // 8) * 8
    (token_rows, gate_slots, y_rows), bias_grads, (own_grad, *side_grads) = moe_stage(
        dims, used, stride, moe_low, slot_rows, slots, gates, ups, full_b_in, out_bias, w_in, w_out, side_out
    )
    outs = back_stage(
        dims, used, experts, gathered, tokens, saved, params, slots, token_rows, gate_slots, cotangent, y_rows, side_grads,
    )
    settled = tail_stage([*outs[:2], *outs[3:], *bias_grads], own_grad, outs[2])
    outs, (grad_in_bias, grad_out_bias, grad_w_in, grad_w_out) = settled[:-4], settled[-4:]
    block_out, tokens_grad = outs[:2]
    if gathered:
        groups = lax.psum_scatter(outs[2].astype(F32), every, scatter_dimension=1, tiled=True)
        n_proj = model // (3 * PAIR)
        grad_proj = jnp.concatenate(list(groups[:n_proj]), axis=1)
        by_head = groups[n_proj:-1].reshape(-1, shard_rows, 3, PAIR)
        grad_qkv = by_head.transpose(1, 2, 0, 3).reshape(shard_rows, -1)
        grad_router = groups[-1, :, :experts]
        vector = [groups[-1, :, experts + i] for i in range(7)]
    else:
        grad_qkv, grad_proj, grad_router = outs[2:5]
        vector = [row.reshape(-1) for row in outs[5:]]
    return (
        block_out,
        tokens_grad,
        vector[0],
        vector[1],
        grad_qkv,
        vector[2],
        vector[3],
        grad_proj,
        vector[4],
        vector[5],
        vector[6],
        grad_router,
        grad_w_in,
        grad_in_bias,
        grad_w_out,
        grad_out_bias,
    )


def solution(mesh):
    dims = grid_of(mesh.shape["wide"], mesh.shape["narrow"])
    every = ("wide", "narrow")
    rows, vector = P(every, None), P(every)
    return jax.shard_map(
        functools.partial(per_device, dims),
        mesh=mesh,
        in_specs=(
            rows, rows, rows, rows, rows, vector, vector, rows, vector, vector, rows, vector, vector, vector,
            rows, P("wide", None, "narrow"), P("wide", "narrow"), P("wide", "narrow", None), P("wide", None), rows,
        ),
        out_specs=(
            rows, rows, vector, vector, rows, vector, vector, rows, vector, vector, vector, rows,
            P("wide", None, "narrow"), P("wide", "narrow"), P("wide", "narrow", None), P("wide", None),
        ),
        check_vma=False,
    )
```

time: 295 us -> 277 us (0.939)
  Pallas kernels: 246 us -> 270 us
  local copies, waits for them, and re-layouts: 23.1 us -> 2.72 us
  starting transfers between devices: 10.9 us -> 0 us
  matrix products: 7.13 us -> 0 us
  other arithmetic: 3.39 us -> 0 us
    pallas_call x3, Pallas kernels: 169 us -> 197 us  [the longest x1 95.6 us: back_stage(): pl.pallas_call(functools.partial(back_kernel, dims, used, experts, gather...]
    all_to_all x1 -> x0, starting transfers between devices: 8.82 us -> none  [per_device(): returned = swap(y).reshape(-1, model)]
    slice x8 -> x0, local copies, waits for them, and re-layouts: 7.15 us -> none  [the longest x1 1.99 us: per_device(): vector = lambda i: shares[:, at + i]]
    dot_general x2 -> x0, matrix products: 7.13 us -> none  [dot(): return jnp.dot(a, b, preferred_element_type=F32)]
    pallas_call x1, Pallas kernels: 77.4 us -> 72.4 us  [front_stage(): pl.pallas_call(functools.partial(front_kernel, dims, experts, capacity, g...]
    another operation x7 -> x1, local copies, waits for them, and re-layouts: 5.23 us -> 1.35 us  [per_device(): jnp.stack([gain_attn, shift_attn, query_bias, value_bias, proj_bias, gain...]
    unnamed x22 -> x1, local copies, waits for them, and re-layouts: 4.97 us -> 1.37 us
  transfers between devices with their start and end apart: 3 -> 0, of which waited for: 0 -> 0; matrix products, arithmetic and copies ran while one was open for 5% -> 0% of each run, Pallas kernels for 25% -> 0%
where the time goes in v3:
time: 277 us; the launch traced here: 273 us
  Pallas kernels  270 us (97%)
    pallas_call x1, Pallas kernels, back_stage(): pl.pallas_call(functools.partial(back_kernel, dims, used, experts, gather...  95.6 us
    pallas_call x1, Pallas kernels, moe_stage(): pl.pallas_call(functools.partial(moe_kernel, dims, used), out_shape=(low(...  94.1 us
    pallas_call x1, Pallas kernels, front_stage(): pl.pallas_call(functools.partial(front_kernel, dims, experts, capacity, g...  72.4 us
    pallas_call x1, Pallas kernels, tail_stage(): pl.pallas_call(functools.partial(tail_kernel, count), out_shape=tuple(sha...  7.46 us

profile of v3, /device:TPU:0, one launch (start us, length us, event | category | flops | bytes accessed | tf_op | source)
XLA Modules:
  0.0 273.2 jit_solution(11857976891652121685)
XLA Ops:
  0.6 1.3 stack.31.rest_3_
  2.0 72.4 %front_stage.1 = (bf16[32,24,3200]{2,1,0:T(8,128)(2,1)}, bf16[768,576]{1,0:T(8,128)(2,1)}, bf16[576,768]{1,0:T(8,128)(2,1)}, bf16[576,768]{1,0:T(8,128)(2,1)}, b...) custom-call(bf16[24,2304]{1,0:T(8,128)(2,1)} %rest_0_.2, ...), custom_call_target="tpu_custom_call" | custom-call | flops 7000000000 | bytes 20000000 | tf_op jit(solution)/shard_map/front_stage/pallas_call | solution.py:406
  74.4 94.1 %moe_stage.1 = (bf16[8,160,768]{2,1,0:T(8,128)(2,1)}, f32[8,1,256]{2,1,0:T(1,128)}, bf16[8,160,768]{2,1,0:T(8,128)(2,1)}, f32[1,768]{1,0:T(1,128)}, f32[1,768]{1...) custom-call(bf16[576,768]{1,0:T(8,128)(2,1)} %get-tuple-element.78.moe_low.rest_8_, ...), custom_call_target="tpu_custom_call" | custom-call | flops 35999997952 | bytes 25000000 | tf_op jit(solution)/shard_map/moe_stage/pallas_call | solution.py:1167
  168.5 95.6 %back_stage.1 = (bf16[576,768]{1,0:T(8,128)(2,1)}, bf16[576,768]{1,0:T(8,128)(2,1)}, bf16[1,2,768,768]{3,2,1,0:T(8,128)(2,1)}, f32[24,2304]{1,0:T(8,128)}, f32[2...) custom-call(bf16[576,768]{1,0:T(8,128)(2,1)} %rest_0_.3, ...), custom_call_target="tpu_custom_call" | custom-call | flops 16000000000 | bytes 40000000 | tf_op jit(solution)/shard_map/back_stage/pallas_call | solution.py:800
  264.1 7.5 %results.1 = (bf16[576,768]{1,0:T(8,128)(2,1)}, bf16[576,768]{1,0:T(8,128)(2,1)}, f32[24,2304]{1,0:T(8,128)}, f32[24,768]{1,0:T(8,128)}, f32[24,8]{1,0:T(8,128)}...) custom-call(bf16[576,768]{1,0:T(8,128)(2,1)} %get-tuple-element.94.r, ...), custom_call_target="tpu_custom_call" | custom-call | tf_op jit(solution)/shard_map/results/pallas_call | solution.py:870
  271.6 1.4 copy.36
